TPU v7x, 32 devices: a whole 2x2x4 slice. The times are simulated.
32 devices in a mesh: wide: 16 (over z, y, x), narrow: 2 (over core).
Axes of the slice: x: 2, y: 2, z: 4, core: 2. Of those that a mesh axis runs over, the one named last changes fastest.
Arguments:
- positions: float32 [3, 8192], P(None, ('wide', 'narrow')), may hold values from 0 to 1
- forces: float32 [3, 16, 8192], P(None, None, ('wide', 'narrow')), may hold values from -6 to 6
- waves: int32 [3, 8192], replicated, may hold values from -16 to 16, as said below
Outputs:
- velocity: float32 [3, 16, 8192], P(None, None, ('wide', 'narrow'))
Inputs may be any that keep to these rules, and one draw needn't show every extreme that they name: `waves`: no wavevector is (0, 0, 0).
All inputs are finite; a program needn't handle non-finite values.
Results may differ from a plain program's by a relative error of at most 0.0053.
Values may be sent and summed in bfloat16 or wider, within the bound.
No kernel may reach another device: no remote copies, remote signals or barrier semaphores. Data moves between devices by JAX's collectives and lax.ppermute only.
A program may use at most 64 MiB of HBM per device.

v0:
```python
import jax
import jax.numpy as jnp
from jax import lax
from jax.sharding import PartitionSpec as P

two_pi = 6.283185307179586
radius = 0.005
xi_split = 40.0


def make_tables(wblock, positions):
    mf = wblock.astype(jnp.float32)
    theta = two_pi * (
        mf[0][:, None] * positions[0][None, :]
        + mf[1][:, None] * positions[1][None, :]
        + mf[2][:, None] * positions[2][None, :]
    )
    return (jnp.cos(theta).astype(jnp.bfloat16), jnp.sin(theta).astype(jnp.bfloat16))


def scale_sums(sums, wblock, amp):
    cols = sums.shape[1]
    split = sums.reshape(2, 3, -1, cols)
    kvec = two_pi * wblock.astype(jnp.float32)
    ksq = jnp.sum(kvec * kvec, axis=0)
    inner = jnp.sum(kvec[None, :, None, :] * split, axis=1)
    proj = split - kvec[None, :, None, :] * (inner / ksq)[:, None, :, :]
    qarg = ksq / (4.0 * xi_split * xi_split)
    factor = (
        amp
        * (1.0 - radius * radius * ksq / 3.0)
        * (1.0 + qarg + 2.0 * qarg * qarg)
        * jnp.exp(-qarg)
        / ksq
    )
    return (proj * factor).reshape(sums.shape[0], cols).astype(jnp.bfloat16)


def shards(positions, forces, waves):
    rows = positions.shape[1]
    kwaves = waves.shape[1]
    devices = lax.axis_size("wide") * lax.axis_size("narrow")
    force_bf = forces.reshape(-1, rows).astype(jnp.bfloat16)
    half = force_bf.shape[0]
    width = 256
    dims = (((1,), (1,)), ((), ()))
    cos_table, sin_table = make_tables(waves, positions)
    sum_cos = lax.dot_general(force_bf, cos_table, dims, preferred_element_type=jnp.float32)
    sum_sin = lax.dot_general(force_bf, sin_table, dims, preferred_element_type=jnp.float32)
    terms = jnp.concatenate([sum_cos, sum_sin], axis=0)
    amp = 20000.0 / jnp.sqrt(jnp.float32(rows * devices) * jnp.float32(kwaves))

    def apply_block(total, piece, begin, cols):
        cosine = lax.dynamic_slice_in_dim(cos_table, begin, cols, 0)
        sine = lax.dynamic_slice_in_dim(sin_table, begin, cols, 0)
        total = total + jnp.dot(piece[:half], cosine, preferred_element_type=jnp.float32)
        return total + jnp.dot(piece[half:], sine, preferred_element_type=jnp.float32)

    empty = jnp.zeros((half, rows), jnp.float32)
    owned = lax.psum_scatter(terms, ("wide", "narrow"), scatter_dimension=1, tiled=True)
    cols = owned.shape[1]
    wblock = lax.dynamic_slice_in_dim(waves, lax.axis_index(("wide", "narrow")) * cols, cols, 1)
    scaled = scale_sums(owned, wblock, amp)
    piece = lax.all_gather(scaled, ("wide", "narrow"), axis=1, tiled=True)
    cols = piece.shape[1]

    def inner(step, acc):
        sub = lax.dynamic_slice_in_dim(piece, step * width, width, 1)
        return apply_block(acc, sub, step * width, width)

    total = lax.fori_loop(0, cols // width, inner, empty)
    return total.reshape(forces.shape)


def solution(mesh):
    placed = (P(None, ("wide", "narrow")), P(None, None, ("wide", "narrow")), P())
    return jax.shard_map(
        shards,
        mesh=mesh,
        in_specs=placed,
        out_specs=P(None, None, ("wide", "narrow")),
        check_vma=False,
    )
```

profile of v0, /device:TPU:0, one launch (start us, length us, event | category | flops | bytes accessed | tf_op | source)
XLA Modules:
  0.0 309.1 jit_solution(3159215597644270184)
XLA Ops:
  9.2 29.7 %convolution_bitcast_fusion.1 = f32[48,8192]{1,0:T(8,128)S(1)} fusion(bf16[48,256]{1,0:T(8,128)(2,1)S(1)} %bitcast.35, f32[256]{0:T(256)S(1)} %bitcast.40, f32[8192]{0:T(1024)S(1)} %bitcast.29, f32[256]{0:T(256)S(1)} %bitcast.43, f32[8192]{0:T(1024)S(1)} %bitcast.32, f32[256]{0:T(256)S(1)} %bitcast.37, f32[8192]{0:T(1024)S(1)} %bitcast.26), kind=kOutput, calls=%fused_computation.9 | convolution fusion | flops 216006656 | bytes 1698816 | tf_op jit(solution)/shard_map/dot_general | solution.py:48
  38.9 30.4 %convolution_bitcast_fusion = f32[48,8192]{1,0:T(8,128)S(1)} fusion(bf16[48,256]{1,0:T(8,128)(2,1)S(1)} %bitcast.36, f32[256]{0:T(256)S(1)} %bitcast.41, f32[8192]{0:T(1024)S(1)} %bitcast.30, f32[256]{0:T(256)S(1)} %bitcast.44, f32[8192]{0:T(1024)S(1)} %bitcast.33, f32[256]{0:T(256)S(1)} %bitcast.38, f32[8192]{0:T(1024)S(1)} %bitcast.27), kind=kOutput, calls=%fused_computation.8 | convolution fusion | flops 216006656 | bytes 1698816 | tf_op jit(solution)/shard_map/dot_general | solution.py:49
  69.3 1.9 pad_maximum_fusion
  72.0 104.2 %reduce-scatter.2.cloned.1.call-done = f32[96,256]{1,0:T(8,128)} async-done(((f32[96,8192]{1,0:T(8,128)}), f32[96,256]{1,0:T(8,128)}) %reduce-scatter.2.cloned.1.call-update) | async-done | bytes 98320 | tf_op jit(solution)/shard_map/reduce_scatter | solution.py:60
  177.1 1.5 fusion.7
  178.7 34.2 %sine_convert_fusion = (bf16[8192,256]{1,0:T(8,128)(2,1)}, bf16[8192,256]{1,0:T(8,128)(2,1)}) fusion(f32[256]{0:T(256)S(1)} %bitcast.42, f32[8192]{0:T(1024)S(1)} %bitcast.31, f32[256]{0:T(256)S(1)} %bitcast.45, f32[8192]{0:T(1024)S(1)} %bitcast.34, f32[256]{0:T(256)S(1)} %bitcast.39, f32[8192]{0:T(1024)S(1)} %bitcast.28), kind=kLoop, calls=%fused_computation.10 | loop fusion | flops 16777216 | bytes 8489984 | tf_op jit(solution)/shard_map/convert_element_type | solution.py:18
  212.9 19.7 %all-gather.2.cloned.1.call-done = bf16[96,8192]{1,0:T(8,128)(2,1)} async-done(((bf16[96,256]{1,0:T(8,128)(2,1)}), bf16[96,8192]{1,0:T(8,128)(2,1)}) %all-gather.2.cloned.1.call-update) | async-done | bytes 1572880 | tf_op jit(solution)/shard_map/all_gather | solution.py:64
  232.6 69.0 %while.14 = (s32[]{:T(128)}, f32[48,256]{1,0:T(8,128)S(1)}, bf16[96,8192]{1,0:T(8,128)(2,1)}, bf16[8192,256]{1,0:T(8,128)(2,1)}, bf16[8192,256]{1,0:T(8,128)(2,1...) while((s32[]{:T(128)}, f32[48,256]{1,0:T(8,128)S(1)}, bf16[96,8192]{1,0:T(8,128)(2,1)}, ...), condition=%wide.region_4.0_spmd.clone, body=%wide.region_3.0_spmd.clone.sunk | while | flops 12619784 | bytes 511144 | solution.py:71
  234.8 1.1 convolution_add_fusion.4
  236.9 1.1 convolution_add_fusion.4
  239.1 1.1 convolution_add_fusion.4
  241.2 1.1 convolution_add_fusion.4
  243.4 1.1 convolution_add_fusion.4
  245.5 1.1 convolution_add_fusion.4
  247.7 1.1 convolution_add_fusion.4
  249.9 1.1 convolution_add_fusion.4
  254.2 1.1 convolution_add_fusion.4
  258.5 1.1 convolution_add_fusion.4
  262.8 1.1 convolution_add_fusion.4
  267.1 1.1 convolution_add_fusion.4
  271.4 1.1 convolution_add_fusion.4
  273.6 1.1 convolution_add_fusion.4
  275.7 1.1 convolution_add_fusion.4
  277.9 1.1 convolution_add_fusion.4
  (64 shorter events, 56.6 us)
Async XLA Ops:
  6.5 169.6 %reduce-scatter.2.cloned.1.call-start = ((), (), s32[]{:S(2)}) async-start(), calls=%async_computation.1 | async-start | bytes 3244032 | tf_op jit(solution)/shard_map/reduce_scatter | solution.py:60
  71.2 161.4 %all-gather.2.cloned.1.call-start = ((), (), s32[]{:S(2)}) async-start(), calls=%async_computation.2 | async-start | bytes 1622016 | tf_op jit(solution)/shard_map/all_gather | solution.py:64
  301.6 0.6 copy-start
Sparse Core Ops, SparseCore 0:
  71.3 104.8 reduce-scatter.1
  179.0 53.5 all-gather.1
where the time goes:
time: 311 us; the launch traced here: 309 us
  matrix products  129 us (41%)
  waiting for transfers between devices  124 us (40%)
  other arithmetic  41 us (13%)
  between operations  13.5 us (4%)
    reduce_scatter x1, waiting for transfers between devices, shards(): lax.psum_scatter(terms, ('wide', 'narrow'), scatter_dimension=1, tiled=True)  104 us
    dot_general x32, matrix products, apply_block(): jnp.dot(piece[:half], cosine, preferred_element_type=jnp.float32)  34.5 us
    dot_general x32, matrix products, apply_block(): jnp.dot(piece[half:], sine, preferred_element_type=jnp.float32)  34.5 us
    convert_element_type x1, other arithmetic, make_tables(): jnp.sin(theta).astype(jnp.bfloat16)  34.2 us
    dot_general x1, matrix products, shards(): lax.dot_general(force_bf, sin_table, dims, preferred_element_type=jnp.flo...  30.4 us
    dot_general x1, matrix products, shards(): lax.dot_general(force_bf, cos_table, dims, preferred_element_type=jnp.flo...  29.7 us
    all_gather x1, waiting for transfers between devices, shards(): piece = lax.all_gather(scaled, ('wide', 'narrow'), axis=1, tiled=True)  19.7 us
  transfers between devices with their start and end apart: 2, of which 2 were waited for; matrix products, arithmetic and copies ran while one was open for 11% of the time, Pallas kernels for 0%

commit v1 on v0

v1 whole, which is shorter than its diff:
```python
import functools

import jax
import jax.numpy as jnp
from jax import lax
from jax.experimental import pallas as pl
from jax.experimental.pallas import tpu as pltpu
from jax.sharding import PartitionSpec as P

two_pi = 6.283185307179586
radius = 0.005
xi_split = 40.0
AXES = ("wide", "narrow")
VMEM = pltpu.VMEM
SMEM = pltpu.SMEM
f32, bf16 = jnp.float32, jnp.bfloat16

SIN = (4.442867901617319, -7.307443368323551, 3.594787581869042, -0.7843727161608242)
COS = (1.414213496635887, -6.9788509910181, 5.739461197516664, -1.8835630614207908, 0.31069820075132315)
ROUND = 12582912.0
HEAD = 16


def horner(coeffs, q):
    total = coeffs[-1] * q + coeffs[-2]
    for c in reversed(coeffs[:-2]):
        total = total * q + c
    return total


def full(shape_dtype):
    return pl.BlockSpec(memory_space=VMEM)


def call(kernel, out_shape, n_in, name, smem=0, scratch=(), flops=0):
    many = isinstance(out_shape, (list, tuple))
    return pl.pallas_call(
        kernel,
        out_shape=out_shape,
        in_specs=[pl.BlockSpec(memory_space=SMEM)] * smem + [pl.BlockSpec(memory_space=VMEM)] * n_in,
        out_specs=[pl.BlockSpec(memory_space=VMEM)] * len(out_shape) if many else pl.BlockSpec(memory_space=VMEM),
        scratch_shapes=scratch,
        name=name,
        compiler_params=pltpu.CompilerParams(vmem_limit_bytes=40 << 20),
        cost_estimate=pl.CostEstimate(flops=flops, bytes_accessed=flops // 256, transcendentals=0),
    )


def split3(x):
    hi = x.astype(bf16)
    rest = x - hi.astype(f32)
    mid = rest.astype(bf16)
    low = (rest - mid.astype(f32)).astype(bf16)
    return hi, mid, low


def pack_kernel(pos_ref, force_ref, out_ref):
    hi, mid, low = split3(pos_ref[...])
    rows = out_ref.shape[1]
    parts = [hi.astype(f32), mid.astype(f32), low.astype(f32), jnp.zeros((HEAD - 9, rows), f32)]
    out_ref[:HEAD, :] = jnp.concatenate(parts, axis=0).astype(bf16)
    for a in range(force_ref.shape[0]):
        p = force_ref.shape[1]
        out_ref[HEAD + a * p : HEAD + (a + 1) * p, :] = force_ref[a].astype(bf16)


def table_kernel(chunk, amp, idx_ref, waves_ref, *refs):
    blocks = refs[:-5]
    tab_ref, acc_ref, send_ref, frame_ref, wt_ref = refs[-5:]
    kwaves = tab_ref.shape[1]
    rows = tab_ref.shape[2]
    probes = acc_ref.shape[0] // 4
    first = pl.multiple_of(idx_ref[0] * kwaves, 128)
    m = waves_ref[:, pl.ds(first, kwaves)].astype(f32)
    msq = jnp.sum(m * m, axis=0, keepdims=True)
    n = m * lax.rsqrt(msq)
    nx, ny, nz = n[0:1], n[1:2], n[2:3]
    sign = jnp.where(nz >= 0.0, 1.0, -1.0)
    a = -1.0 / (sign + nz)
    b = nx * ny * a
    ksq = (two_pi * two_pi) * msq
    qarg = ksq / (4.0 * xi_split * xi_split)
    factor = amp * (1.0 - radius * radius * ksq / 3.0) * (1.0 + qarg + 2.0 * qarg * qarg) * jnp.exp(-qarg) / ksq
    frame_ref[...] = jnp.concatenate(
        [1.0 + sign * nx * nx * a, sign * b, -sign * nx, b, sign + ny * ny * a, -ny, factor, jnp.zeros_like(b)], axis=0
    )
    head = jnp.concatenate([m, m, m, jnp.zeros((HEAD - 9, kwaves), f32)], axis=0)
    wt_ref[...] = jnp.transpose(head).astype(bf16)
    packed = []
    for ref in blocks:
        if len(ref.shape) == 2:
            packed.append(ref[...])
        else:
            packed.extend(ref[j] for j in range(ref.shape[0]))
    width = packed[0].shape[1]
    phases = [p[:HEAD] for p in packed]
    forces = jnp.concatenate([p[HEAD:] for p in packed], axis=1)
    strip = 32

    def step(c, carry):
        base = pl.multiple_of(c * chunk, chunk)

        def inner(t, carry):
            row = pl.multiple_of(base + t * strip, strip)
            w = wt_ref[pl.ds(row, strip), :]
            for j, ph in enumerate(phases):
                u = jnp.dot(w, ph, preferred_element_type=f32)
                r = u - ((u + ROUND) - ROUND)
                q = r * r
                s = r * horner(SIN, q)
                co = horner(COS, q)
                tab_ref[0, pl.ds(row, strip), j * width : (j + 1) * width] = (1.0 - s * s).astype(bf16)
                tab_ref[1, pl.ds(row, strip), j * width : (j + 1) * width] = (s * co).astype(bf16)
            return carry

        lax.fori_loop(0, chunk // strip, inner, 0, unroll=True)
        cols = pl.ds(base, chunk)
        fr = frame_ref[:, cols]
        for part in range(2):
            t = tab_ref[part, cols, :]
            sums = lax.dot_general(forces, t, (((1,), (1,)), ((), ())), preferred_element_type=f32)
            for j in range(2):
                value = sum(fr[3 * j + x : 3 * j + x + 1] * sums[x * probes : (x + 1) * probes] for x in range(3))
                low = (2 * part + j) * probes
                acc_ref[low : low + probes, cols] = value
                send_ref[low : low + probes, cols] = value.astype(bf16)
        return carry

    lax.fori_loop(0, kwaves // chunk, step, 0)


def back_kernel(chunk, acc_ref, recv_ref, frame_ref, tab_ref, out_ref):
    kwaves = tab_ref.shape[1]
    probes = acc_ref.shape[0] // 4
    out_ref[...] = jnp.zeros_like(out_ref)

    def step(c, carry):
        cols = pl.ds(pl.multiple_of(c * chunk, chunk), chunk)
        fr = frame_ref[:, cols]
        sums = acc_ref[:, cols] + recv_ref[:, cols].astype(f32)
        total = out_ref[...]
        for part in range(2):
            t0 = fr[6:7] * sums[2 * part * probes : (2 * part + 1) * probes]
            t1 = fr[6:7] * sums[(2 * part + 1) * probes : (2 * part + 2) * probes]
            scaled = jnp.concatenate([fr[x : x + 1] * t0 + fr[3 + x : 4 + x] * t1 for x in range(3)], axis=0).astype(bf16)
            total = total + jnp.dot(scaled, tab_ref[part, cols, :], preferred_element_type=f32)
        out_ref[...] = total
        return carry

    lax.fori_loop(0, kwaves // chunk, step, 0)


def shards(positions, forces, waves):
    wide, narrow = lax.axis_size("wide"), lax.axis_size("narrow")
    devices = wide * narrow
    bits = devices.bit_length() - 1
    assert devices == 1 << bits and bits >= 2
    rows = positions.shape[1]
    kwaves = waves.shape[1]
    half = forces.shape[0] * forces.shape[1]
    probes = forces.shape[1]
    top = devices >> 1
    amp = 20000.0 / float(rows * devices * kwaves) ** 0.5

    def swap(x, bit):
        return lax.ppermute(x, AXES, [(d, d ^ bit) for d in range(devices)])

    me = lax.axis_index(AXES)
    block = 2 * (me // top) + me % 2
    mine = kwaves // 4
    own = call(pack_kernel, jax.ShapeDtypeStruct((HEAD + half, rows), bf16), 2, "pack")(positions, forces)
    far = swap(own, top)
    near = swap(jnp.stack([own, far]), 1)
    pairs = mine * 4 * rows
    chunk = 256
    tab, acc, send, frame = call(
        functools.partial(table_kernel, chunk, amp),
        (
            jax.ShapeDtypeStruct((2, mine, 4 * rows), bf16),
            jax.ShapeDtypeStruct((4 * probes, mine), f32),
            jax.ShapeDtypeStruct((4 * probes, mine), bf16),
            jax.ShapeDtypeStruct((8, mine), f32),
        ),
        4,
        "table",
        smem=1,
        scratch=[VMEM((mine, HEAD), bf16)],
        flops=pairs * 4 * half,
    )(block.reshape(1), waves, own, far, near)
    bit = 2
    while bit < top:
        got = swap(send, bit)
        bit *= 2
        if bit < top:
            acc = acc + got.astype(f32)
            send = acc.astype(bf16)
    part = call(functools.partial(back_kernel, chunk), jax.ShapeDtypeStruct((half, 4 * rows), f32), 4, "back", flops=pairs * 4 * half)(
        acc, got, frame, tab
    )
    there = swap(part[:, 2 * rows :].astype(bf16), 1)
    part = part[:, : 2 * rows] + there.astype(f32)
    there = swap(part[:, rows:].astype(bf16), top)
    total = part[:, :rows] + there.astype(f32)
    return total.reshape(forces.shape)


def solution(mesh):
    placed = (P(None, AXES), P(None, None, AXES), P())
    return jax.shard_map(
        shards,
        mesh=mesh,
        in_specs=placed,
        out_specs=P(None, None, AXES),
        check_vma=False,
    )
```

time: 311 us -> 53.5 us (0.17)
  matrix products: 129 us -> 0 us
  waiting for transfers between devices: 124 us -> 24.2 us
  other arithmetic: 41 us -> 0.8 us
  Pallas kernels: 0 us -> 13.5 us
  between operations: 13.5 us -> 0.1 us
  starting transfers between devices: 0.04 us -> 12.2 us
    dot_general x66 -> x0, matrix products: 129 us -> none  [the longest x32 34.5 us: apply_block(): jnp.dot(piece[:half], cosine, preferred_element_type=jnp.float32)]
    reduce_scatter x1 -> x0, waiting for transfers between devices: 104 us -> none  [shards(): lax.psum_scatter(terms, ('wide', 'narrow'), scatter_dimension=1, tiled=True)]
    convert_element_type x4 -> x2, other arithmetic: 37.5 us -> 0.16 us  [shards(): send = acc.astype(bf16)]
    ppermute x0 -> x7, waiting for transfers between devices: none -> 24.2 us  [swap(): return lax.ppermute(x, AXES, [(d, d ^ bit) for d in range(devices)])]
    all_gather x1 -> x0, waiting for transfers between devices: 19.7 us -> none  [shards(): piece = lax.all_gather(scaled, ('wide', 'narrow'), axis=1, tiled=True)]
    pallas_call x0 -> x3, Pallas kernels: none -> 13.5 us  [the longest x1 11.1 us: shards(): call(functools.partial(table_kernel, chunk, amp), (jax.ShapeDtypeStruct((...]
    ppermute x0 -> x7, starting transfers between devices: none -> 12.2 us  [swap(): return lax.ppermute(x, AXES, [(d, d ^ bit) for d in range(devices)])]
  transfers between devices with their start and end apart: 2 -> 7, of which waited for: 2 -> 7; matrix products, arithmetic and copies ran while one was open for 11% -> 0% of each run, Pallas kernels for 0% -> 0%
where the time goes in v1:
time: 53.5 us; the launch traced here: 53.3 us
  waiting for transfers between devices  24.2 us (45%)
  Pallas kernels  13.5 us (25%)
  starting transfers between devices  12.2 us (23%)
  local copies, waits for them, and re-layouts  2.4 us (4%)
  other arithmetic  0.8 us (1%)
    ppermute x7, waiting for transfers between devices, swap(): return lax.ppermute(x, AXES, [(d, d ^ bit) for d in range(devices)])  24.2 us
    ppermute x7, starting transfers between devices, swap(): return lax.ppermute(x, AXES, [(d, d ^ bit) for d in range(devices)])  12.2 us
    pallas_call x1, Pallas kernels, shards(): call(functools.partial(table_kernel, chunk, amp), (jax.ShapeDtypeStruct((...  11.1 us
    pallas_call x1, Pallas kernels, shards(): call(functools.partial(back_kernel, chunk), jax.ShapeDtypeStruct((half, 4...  2.4 us
    unnamed x6, local copies, waits for them, and re-layouts  2.39 us
  transfers between devices with their start and end apart: 7, of which 7 were waited for; matrix products, arithmetic and copies ran while one was open for 0% of the time, Pallas kernels for 0%

profile of v1, /device:TPU:0, one launch (start us, length us, event | category | flops | bytes accessed | tf_op | source)
XLA Modules:
  0.0 53.3 jit_solution(9760966156940213420)
XLA Ops:
  0.0 0.0 copy-start
  0.0 0.8 %copy-done = f32[3,16,256]{2,1,0:T(8,128)S(1)} copy-done((f32[3,16,256]{2,1,0:T(8,128)S(1)}, f32[3,16,256]{2,1,0:T(8,128)}, u32[]{:S(2)}) %copy-start) | copy-done | bytes 49176
  0.8 0.0 copy-start.1
  0.8 0.7 %copy-done.1 = f32[3,256]{1,0:T(4,128)S(1)} copy-done((f32[3,256]{1,0:T(4,128)S(1)}, f32[3,256]{1,0:T(4,128)}, u32[]{:S(2)}) %copy-start.1) | copy-done | bytes 3096
  1.5 4.1 %collective-permute-start = (bf16[64,256]{1,0:T(8,128)(2,1)S(1)}, bf16[64,256]{1,0:T(8,128)(2,1)S(1)}, u32[]{:S(2)}, u32[]{:S(2)}) collective-permute-start(bf16[64,256]{1,0:T(8,128)(2,1)S(1)} %pack.1.refs_0_), channel_id=1, source_target_pairs={{0,16},{1,17},{2,18},{3,19},{4,20},{5,21},{6,22},{7,23},{8,24},{9,... | collective-permute-start | bytes 98312 | tf_op jit(solution)/shard_map/ppermute | solution.py:166
  5.6 2.2 %collective-permute-done.refs_1_ = bf16[64,256]{1,0:T(8,128)(2,1)S(1)} collective-permute-done((bf16[64,256]{1,0:T(8,128)(2,1)S(1)}, bf16[64,256]{1,0:T(8,128)(2,1)S(1)}, u32[]{:S(2)}, u32[]{:S(2)}) %collective-permute-start) | collective-permute-done | bytes 32800 | tf_op jit(solution)/shard_map/ppermute | solution.py:166
  7.9 0.1 collective-permute-start.1
  8.0 1.2 %collective-permute-done.1.refs_2_ = bf16[2,64,256]{2,1,0:T(8,128)(2,1)S(1)} collective-permute-done((bf16[2,64,256]{2,1,0:T(8,128)(2,1)S(1)}, bf16[2,64,256]{2,1,0:T(8,128)(2,1)S(1)}, u32[]{:S(2)}, u32[]{:S(2)}) %collective-permute-start.1) | collective-permute-done | bytes 65568 | tf_op jit(solution)/shard_map/ppermute | solution.py:166
  9.2 0.9 %copy-done.2 = s32[3,8192]{1,0:T(4,128)S(1)} copy-done((s32[3,8192]{1,0:T(4,128)S(1)}, s32[3,8192]{1,0:T(4,128)}, u32[]{:S(2)}) %copy-start.2) | copy-done | bytes 98328
  10.1 11.1 %table.1 = (bf16[2,2048,1024]{2,1,0:T(8,128)(2,1)S(1)}, f32[64,2048]{1,0:T(8,128)S(1)}, bf16[64,2048]{1,0:T(8,128)(2,1)S(1)}, f32[8,2048]{1,0:T(8,128)S(1)}) custom-call(s32[1]{0:T(128)} %bitcast.idx_ref, s32[3,8192]{1,0:T(4,128)S(1)} %copy-done.2, bf16[64,256]{1,0:T(8,128)(2,1)S(1)} %pack.1.refs_0_, bf16[64,256]{1,0:T(8,128)(2,1)S(1)} %collective-permute-done.refs_1_, ...), custom_call_target="tpu_custom_call" | custom-call | flops 402653184 | bytes 1572864 | tf_op jit(solution)/shard_map/table/pallas_call | solution.py:176
  21.2 1.8 %collective-permute-start.2 = (bf16[64,2048]{1,0:T(8,128)(2,1)S(1)}, bf16[64,2048]{1,0:T(8,128)(2,1)S(1)}, u32[]{:S(2)}, u32[]{:S(2)}) collective-permute-start(bf16[64,2048]{1,0:T(8,128)(2,1)S(1)} %get-tuple-element.10), channel_id=1, source_target_pairs={{0,2},{1,3},{2,0},{3,1},{4,6},{5,7},{6,4},{7,5},{8,10},{9,11},{10,... | collective-permute-start | bytes 786440 | tf_op jit(solution)/shard_map/ppermute | solution.py:166
  23.0 6.7 %collective-permute-done.2 = bf16[64,2048]{1,0:T(8,128)(2,1)S(1)} collective-permute-done((bf16[64,2048]{1,0:T(8,128)(2,1)S(1)}, bf16[64,2048]{1,0:T(8,128)(2,1)S(1)}, u32[]{:S(2)}, u32[]{:S(2)}) %collective-permute-start.2) | collective-permute-done | bytes 262176 | tf_op jit(solution)/shard_map/ppermute | solution.py:166
  29.7 0.1 fusion
  29.7 1.8 %collective-permute-start.3 = (bf16[64,2048]{1,0:T(8,128)(2,1)S(1)}, bf16[64,2048]{1,0:T(8,128)(2,1)S(1)}, u32[]{:S(2)}, u32[]{:S(2)}) collective-permute-start(bf16[64,2048]{1,0:T(8,128)(2,1)S(1)} %fusion), channel_id=1, source_target_pairs={{0,4},{1,5},{2,6},{3,7},{4,0},{5,1},{6,2},{7,3},{8,12},{9,13},{10,... | collective-permute-start | bytes 786440 | tf_op jit(solution)/shard_map/ppermute | solution.py:166
  31.5 5.8 %collective-permute-done.3 = bf16[64,2048]{1,0:T(8,128)(2,1)S(1)} collective-permute-done((bf16[64,2048]{1,0:T(8,128)(2,1)S(1)}, bf16[64,2048]{1,0:T(8,128)(2,1)S(1)}, u32[]{:S(2)}, u32[]{:S(2)}) %collective-permute-start.3) | collective-permute-done | bytes 262176 | tf_op jit(solution)/shard_map/ppermute | solution.py:166
  37.3 0.1 fusion.1
  37.4 1.6 %collective-permute-start.4 = (bf16[64,2048]{1,0:T(8,128)(2,1)S(1)}, bf16[64,2048]{1,0:T(8,128)(2,1)S(1)}, u32[]{:S(2)}, u32[]{:S(2)}) collective-permute-start(bf16[64,2048]{1,0:T(8,128)(2,1)S(1)} %get-tuple-element.13), channel_id=1, source_target_pairs={{0,8},{1,9},{2,10},{3,11},{4,12},{5,13},{6,14},{7,15},{8,0},{9,1},... | collective-permute-start | bytes 786440 | tf_op jit(solution)/shard_map/ppermute | solution.py:166
  39.0 5.1 %collective-permute-done.4.recv_ref = bf16[64,2048]{1,0:T(8,128)(2,1)S(1)} collective-permute-done((bf16[64,2048]{1,0:T(8,128)(2,1)S(1)}, bf16[64,2048]{1,0:T(8,128)(2,1)S(1)}, u32[]{:S(2)}, u32[]{:S(2)}) %collective-permute-start.4) | collective-permute-done | bytes 262176 | tf_op jit(solution)/shard_map/ppermute | solution.py:166
  44.1 2.4 %back.1 = f32[48,1024]{1,0:T(8,128)S(1)} custom-call(f32[64,2048]{1,0:T(8,128)S(1)} %get-tuple-element.14.acc_ref, bf16[64,2048]{1,0:T(8,128)(2,1)S(1)} %collective-permute-done.4.recv_ref, f32[8,2048]{1,0:T(8,128)S(1)} %get-tuple-element.11.frame_ref, bf16[2,2048,1024]{2,1,0:T(8,128)(2,1)S(1)} %get-tuple-element.12.tab_ref), custom_call_target="tpu_custom_call" | custom-call | flops 402653184 | bytes 1572864 | tf_op jit(solution)/shard_map/back/pallas_call | solution.py:197
  46.5 0.1 collective-permute-start.5
  46.6 1.2 %collective-permute-done.5 = bf16[48,512]{1,0:T(8,128)(2,1)S(1)} collective-permute-done((bf16[48,512]{1,0:T(8,128)(2,1)S(1)}, bf16[48,512]{1,0:T(8,128)(2,1)S(1)}, u32[]{:S(2)}, u32[]{:S(2)}) %collective-permute-start.5) | collective-permute-done | bytes 49184 | tf_op jit(solution)/shard_map/ppermute | solution.py:166
  47.9 2.7 %collective-permute-start.6 = (bf16[48,256]{1,0:T(8,128)(2,1)S(1)}, bf16[48,256]{1,0:T(8,128)(2,1)S(1)}, u32[]{:S(2)}, u32[]{:S(2)}) collective-permute-start(bf16[48,256]{1,0:T(8,128)(2,1)S(1)} %slice.27), channel_id=1, source_target_pairs={{0,16},{1,17},{2,18},{3,19},{4,20},{5,21},{6,22},{7,23},{8,24},{9,... | collective-permute-start | bytes 73736 | tf_op jit(solution)/shard_map/ppermute | solution.py:166
  50.6 2.1 %collective-permute-done.6 = bf16[48,256]{1,0:T(8,128)(2,1)S(1)} collective-permute-done((bf16[48,256]{1,0:T(8,128)(2,1)S(1)}, bf16[48,256]{1,0:T(8,128)(2,1)S(1)}, u32[]{:S(2)}, u32[]{:S(2)}) %collective-permute-start.6) | collective-permute-done | bytes 24608 | tf_op jit(solution)/shard_map/ppermute | solution.py:166
  52.7 0.6 %slice_add_fusion.1 = f32[48,256]{1,0:T(8,128)} fusion(f32[48,512]{1,0:T(8,128)S(1)} %slice_add_fusion, bf16[48,256]{1,0:T(8,128)(2,1)S(1)} %collective-permute-done.6), kind=kLoop, calls=%fused_computation.7 | loop fusion | flops 24576 | bytes 122880 | tf_op jit(solution)/shard_map/add | solution.py:203
  (6 shorter events, 0.1 us)
Async XLA Ops:
  0.0 0.8 %copy-start = (f32[3,16,256]{2,1,0:T(8,128)S(1)}, f32[3,16,256]{2,1,0:T(8,128)}, u32[]{:S(2)}) copy-start(f32[3,16,256]{2,1,0:T(8,128)} %force_ref.1) | copy-start | bytes 147460
  0.8 0.7 %copy-start.1 = (f32[3,256]{1,0:T(4,128)S(1)}, f32[3,256]{1,0:T(4,128)}, u32[]{:S(2)}) copy-start(f32[3,256]{1,0:T(4,128)} %pos_ref.1) | copy-start | bytes 9220
  1.5 6.4 %collective-permute-start = (bf16[64,256]{1,0:T(8,128)(2,1)S(1)}, bf16[64,256]{1,0:T(8,128)(2,1)S(1)}, u32[]{:S(2)}, u32[]{:S(2)}) collective-permute-start(bf16[64,256]{1,0:T(8,128)(2,1)S(1)} %pack.1.refs_0_), channel_id=1, source_target_pairs={{0,16},{1,17},{2,18},{3,19},{4,20},{5,21},{6,22},{7,23},{8,24},{9,... | collective-permute-start | bytes 98312 | tf_op jit(solution)/shard_map/ppermute | solution.py:166
  7.9 1.3 %collective-permute-start.1 = (bf16[2,64,256]{2,1,0:T(8,128)(2,1)S(1)}, bf16[2,64,256]{2,1,0:T(8,128)(2,1)S(1)}, u32[]{:S(2)}, u32[]{:S(2)}) collective-permute-start(bf16[2,64,256]{2,1,0:T(8,128)(2,1)S(1)} %pad_maximum_fusion), channel_id=1, source_target_pairs={{0,1},{1,0},{2,3},{3,2},{4,5},{5,4},{6,7},{7,6},{8,9},{9,8},{10,11... | collective-permute-start | bytes 196616 | tf_op jit(solution)/shard_map/ppermute | solution.py:166
  9.2 0.9 %copy-start.2 = (s32[3,8192]{1,0:T(4,128)S(1)}, s32[3,8192]{1,0:T(4,128)}, u32[]{:S(2)}) copy-start(s32[3,8192]{1,0:T(4,128)} %waves_ref.1) | copy-start | bytes 294916
  21.2 8.4 %collective-permute-start.2 = (bf16[64,2048]{1,0:T(8,128)(2,1)S(1)}, bf16[64,2048]{1,0:T(8,128)(2,1)S(1)}, u32[]{:S(2)}, u32[]{:S(2)}) collective-permute-start(bf16[64,2048]{1,0:T(8,128)(2,1)S(1)} %get-tuple-element.10), channel_id=1, source_target_pairs={{0,2},{1,3},{2,0},{3,1},{4,6},{5,7},{6,4},{7,5},{8,10},{9,11},{10,... | collective-permute-start | bytes 786440 | tf_op jit(solution)/shard_map/ppermute | solution.py:166
  29.7 7.6 %collective-permute-start.3 = (bf16[64,2048]{1,0:T(8,128)(2,1)S(1)}, bf16[64,2048]{1,0:T(8,128)(2,1)S(1)}, u32[]{:S(2)}, u32[]{:S(2)}) collective-permute-start(bf16[64,2048]{1,0:T(8,128)(2,1)S(1)} %fusion), channel_id=1, source_target_pairs={{0,4},{1,5},{2,6},{3,7},{4,0},{5,1},{6,2},{7,3},{8,12},{9,13},{10,... | collective-permute-start | bytes 786440 | tf_op jit(solution)/shard_map/ppermute | solution.py:166
  37.4 6.7 %collective-permute-start.4 = (bf16[64,2048]{1,0:T(8,128)(2,1)S(1)}, bf16[64,2048]{1,0:T(8,128)(2,1)S(1)}, u32[]{:S(2)}, u32[]{:S(2)}) collective-permute-start(bf16[64,2048]{1,0:T(8,128)(2,1)S(1)} %get-tuple-element.13), channel_id=1, source_target_pairs={{0,8},{1,9},{2,10},{3,11},{4,12},{5,13},{6,14},{7,15},{8,0},{9,1},... | collective-permute-start | bytes 786440 | tf_op jit(solution)/shard_map/ppermute | solution.py:166
  46.5 1.3 %collective-permute-start.5 = (bf16[48,512]{1,0:T(8,128)(2,1)S(1)}, bf16[48,512]{1,0:T(8,128)(2,1)S(1)}, u32[]{:S(2)}, u32[]{:S(2)}) collective-permute-start(bf16[48,512]{1,0:T(8,128)(2,1)S(1)} %slice.26), channel_id=1, source_target_pairs={{0,1},{1,0},{2,3},{3,2},{4,5},{5,4},{6,7},{7,6},{8,9},{9,8},{10,11... | collective-permute-start | bytes 147464 | tf_op jit(solution)/shard_map/ppermute | solution.py:166
  47.9 4.8 %collective-permute-start.6 = (bf16[48,256]{1,0:T(8,128)(2,1)S(1)}, bf16[48,256]{1,0:T(8,128)(2,1)S(1)}, u32[]{:S(2)}, u32[]{:S(2)}) collective-permute-start(bf16[48,256]{1,0:T(8,128)(2,1)S(1)} %slice.27), channel_id=1, source_target_pairs={{0,16},{1,17},{2,18},{3,19},{4,20},{5,21},{6,22},{7,23},{8,24},{9,... | collective-permute-start | bytes 73736 | tf_op jit(solution)/shard_map/ppermute | solution.py:166

commit v2 on v1

--- a/solution.py
+++ b/solution.py
@@ -64,14 +64,13 @@
         out_ref[HEAD + a * p : HEAD + (a + 1) * p, :] = force_ref[a].astype(bf16)
 
 
-def table_kernel(chunk, amp, idx_ref, waves_ref, *refs):
-    blocks = refs[:-5]
-    tab_ref, acc_ref, send_ref, frame_ref, wt_ref = refs[-5:]
-    kwaves = tab_ref.shape[1]
-    rows = tab_ref.shape[2]
-    probes = acc_ref.shape[0] // 4
+def frame_kernel(amp, idx_ref, waves_ref, frame_ref, wt_ref, own_ref, sem):
+    kwaves = own_ref.shape[1]
     first = pl.multiple_of(idx_ref[0] * kwaves, 128)
-    m = waves_ref[:, pl.ds(first, kwaves)].astype(f32)
+    copy = pltpu.make_async_copy(waves_ref.at[:, pl.ds(first, kwaves)], own_ref, sem)
+    copy.start()
+    copy.wait()
+    m = own_ref[...].astype(f32)
     msq = jnp.sum(m * m, axis=0, keepdims=True)
     n = m * lax.rsqrt(msq)
     nx, ny, nz = n[0:1], n[1:2], n[2:3]
@@ -86,6 +85,13 @@
     )
     head = jnp.concatenate([m, m, m, jnp.zeros((HEAD - 9, kwaves), f32)], axis=0)
     wt_ref[...] = jnp.transpose(head).astype(bf16)
+
+
+def table_kernel(chunk, frame_ref, wt_ref, *refs):
+    blocks = refs[:-3]
+    tab_ref, acc_ref, send_ref = refs[-3:]
+    kwaves = tab_ref.shape[1]
+    probes = acc_ref.shape[0] // 4
     packed = []
     for ref in blocks:
         if len(ref.shape) == 2:
@@ -173,25 +179,31 @@
     near = swap(jnp.stack([own, far]), 1)
     pairs = mine * 4 * rows
     chunk = 256
-    tab, acc, send, frame = call(
-        functools.partial(table_kernel, chunk, amp),
+    frame, wt = pl.pallas_call(
+        functools.partial(frame_kernel, amp),
+        out_shape=(jax.ShapeDtypeStruct((8, mine), f32), jax.ShapeDtypeStruct((mine, HEAD), bf16)),
+        in_specs=[pl.BlockSpec(memory_space=SMEM), pl.BlockSpec(memory_space=pl.ANY)],
+        out_specs=[pl.BlockSpec(memory_space=VMEM)] * 2,
+        scratch_shapes=[VMEM((3, mine), jnp.int32), pltpu.SemaphoreType.DMA],
+        name="frame",
+        cost_estimate=pl.CostEstimate(flops=mine * 1000, bytes_accessed=mine * 1000, transcendentals=0),
+    )(block.reshape(1), waves)
+    tab, acc, send = call(
+        functools.partial(table_kernel, chunk),
         (
             jax.ShapeDtypeStruct((2, mine, 4 * rows), bf16),
             jax.ShapeDtypeStruct((4 * probes, mine), f32),
             jax.ShapeDtypeStruct((4 * probes, mine), bf16),
-            jax.ShapeDtypeStruct((8, mine), f32),
         ),
-        4,
+        5,
         "table",
-        smem=1,
-        scratch=[VMEM((mine, HEAD), bf16)],
         flops=pairs * 4 * half,
-    )(block.reshape(1), waves, own, far, near)
-    bit = 2
-    while bit < top:
-        got = swap(send, bit)
-        bit *= 2
-        if bit < top:
+    )(frame, wt, own, far, near)
+    middle = [1 << j for j in range(1, bits - 1)]
+    for j in range(len(middle)):
+        turn = [middle[(j + core) % len(middle)] for core in range(2)]
+        got = lax.ppermute(send, AXES, [(d, d ^ turn[d % 2]) for d in range(devices)])
+        if j + 1 < len(middle):
             acc = acc + got.astype(f32)
             send = acc.astype(bf16)
     part = call(functools.partial(back_kernel, chunk), jax.ShapeDtypeStruct((half, 4 * rows), f32), 4, "back", flops=pairs * 4 * half)(

time: 53.5 us -> 51.6 us (0.964)
  waiting for transfers between devices: 24.2 us -> 19.7 us
  Pallas kernels: 13.5 us -> 15.1 us
  local copies, waits for them, and re-layouts: 2.4 us -> 3.37 us
    ppermute x7 -> x4, waiting for transfers between devices: 24.2 us -> 5.59 us  [swap(): return lax.ppermute(x, AXES, [(d, d ^ bit) for d in range(devices)])]
    ppermute x0 -> x3, waiting for transfers between devices: none -> 14.1 us  [shards(): lax.ppermute(send, AXES, [(d, d ^ turn[d % 2]) for d in range(devices)])]
    ppermute x7 -> x4, starting transfers between devices: 12.2 us -> 6.93 us  [swap(): return lax.ppermute(x, AXES, [(d, d ^ bit) for d in range(devices)])]
    ppermute x0 -> x3, starting transfers between devices: none -> 5.18 us  [shards(): lax.ppermute(send, AXES, [(d, d ^ turn[d % 2]) for d in range(devices)])]
    pallas_call x1 -> x2, Pallas kernels: 11.1 us -> 12.7 us  [the longest x1 10.9 us: shards(): call(functools.partial(table_kernel, chunk), (jax.ShapeDtypeStruct((2, mi...]
    unnamed x6 -> x8, local copies, waits for them, and re-layouts: 2.39 us -> 3.36 us
  transfers between devices with their start and end apart: 7 -> 7, of which waited for: 7 -> 6; matrix products, arithmetic and copies ran while one was open for 0% -> 0% of each run, Pallas kernels for 0% -> 4%
where the time goes in v2:
time: 51.6 us; the launch traced here: 51.2 us
  waiting for transfers between devices  19.7 us (38%)
  Pallas kernels  15.1 us (29%)
  starting transfers between devices  12.1 us (23%)
  local copies, waits for them, and re-layouts  3.37 us (7%)
  other arithmetic  0.78 us (2%)
    ppermute x3, waiting for transfers between devices, shards(): lax.ppermute(send, AXES, [(d, d ^ turn[d % 2]) for d in range(devices)])  14.1 us
    pallas_call x1, Pallas kernels, shards(): call(functools.partial(table_kernel, chunk), (jax.ShapeDtypeStruct((2, mi...  10.9 us
    ppermute x4, starting transfers between devices, swap(): return lax.ppermute(x, AXES, [(d, d ^ bit) for d in range(devices)])  6.93 us
    ppermute x4, waiting for transfers between devices, swap(): return lax.ppermute(x, AXES, [(d, d ^ bit) for d in range(devices)])  5.59 us
    ppermute x3, starting transfers between devices, shards(): lax.ppermute(send, AXES, [(d, d ^ turn[d % 2]) for d in range(devices)])  5.18 us
    unnamed x8, local copies, waits for them, and re-layouts  3.36 us
    pallas_call x1, Pallas kernels, shards(): call(functools.partial(back_kernel, chunk), jax.ShapeDtypeStruct((half, 4...  2.39 us
    pallas_call x1, Pallas kernels, shards(): pl.pallas_call(functools.partial(frame_kernel, amp), out_shape=(jax.Shape...  1.81 us
  transfers between devices with their start and end apart: 7, of which 6 were waited for; matrix products, arithmetic and copies ran while one was open for 0% of the time, Pallas kernels for 4%

profile of v2, /device:TPU:0, one launch (start us, length us, event | category | flops | bytes accessed | tf_op | source)
XLA Modules:
  0.0 51.2 jit_solution(13978085751326486894)
XLA Ops:
  0.0 0.8 %copy-done.1 = f32[3,16,256]{2,1,0:T(8,128)S(1)} copy-done((f32[3,16,256]{2,1,0:T(8,128)S(1)}, f32[3,16,256]{2,1,0:T(8,128)}, u32[]{:S(2)}) %copy-start.1) | copy-done | bytes 49176
  0.8 0.7 %copy-done.2 = f32[3,256]{1,0:T(4,128)S(1)} copy-done((f32[3,256]{1,0:T(4,128)S(1)}, f32[3,256]{1,0:T(4,128)}, u32[]{:S(2)}) %copy-start.2) | copy-done | bytes 3096
  1.5 4.1 %collective-permute-start = (bf16[64,256]{1,0:T(8,128)(2,1)S(1)}, bf16[64,256]{1,0:T(8,128)(2,1)S(1)}, u32[]{:S(2)}, u32[]{:S(2)}) collective-permute-start(bf16[64,256]{1,0:T(8,128)(2,1)S(1)} %pack.1.refs_0_), channel_id=1, source_target_pairs={{0,16},{1,17},{2,18},{3,19},{4,20},{5,21},{6,22},{7,23},{8,24},{9,... | collective-permute-start | bytes 98312 | tf_op jit(solution)/shard_map/ppermute | solution.py:172
  5.6 2.2 %collective-permute-done.refs_1_ = bf16[64,256]{1,0:T(8,128)(2,1)S(1)} collective-permute-done((bf16[64,256]{1,0:T(8,128)(2,1)S(1)}, bf16[64,256]{1,0:T(8,128)(2,1)S(1)}, u32[]{:S(2)}, u32[]{:S(2)}) %collective-permute-start) | collective-permute-done | bytes 32800 | tf_op jit(solution)/shard_map/ppermute | solution.py:172
  7.9 0.1 collective-permute-start.1
  8.0 1.8 %frame.1 = (f32[8,2048]{1,0:T(8,128)}, bf16[2048,16]{1,0:T(8,128)(2,1)}) custom-call(s32[1]{0:T(128)} %bitcast.idx_ref, s32[3,8192]{1,0:T(4,128)} %waves_ref.1), custom_call_target="tpu_custom_call" | custom-call | flops 2048000 | bytes 2048000 | tf_op jit(solution)/shard_map/frame/pallas_call | solution.py:182
  9.8 0.0 collective-permute-done.1.refs_2_
  9.8 0.0 copy-start
  9.8 0.8 %copy-done = f32[8,2048]{1,0:T(8,128)S(1)} copy-done((f32[8,2048]{1,0:T(8,128)S(1)}, f32[8,2048]{1,0:T(8,128)}, u32[]{:S(2)}) %copy-start) | copy-done | bytes 65560
  10.7 1.0 %copy-done.3 = bf16[2048,16]{1,0:T(8,128)(2,1)S(1)} copy-done((bf16[2048,16]{1,0:T(8,128)(2,1)S(1)}, bf16[2048,16]{1,0:T(8,128)(2,1)}, u32[]{:S(2)}) %copy-start.3) | copy-done | bytes 65560
  11.7 10.9 %table.1 = (bf16[2,2048,1024]{2,1,0:T(8,128)(2,1)S(1)}, f32[64,2048]{1,0:T(8,128)S(1)}, bf16[64,2048]{1,0:T(8,128)(2,1)S(1)}) custom-call(f32[8,2048]{1,0:T(8,128)S(1)} %copy-done, bf16[2048,16]{1,0:T(8,128)(2,1)S(1)} %copy-done.3, bf16[64,256]{1,0:T(8,128)(2,1)S(1)} %pack.1.refs_0_, bf16[64,256]{1,0:T(8,128)(2,1)S(1)} %collective-permute-done.refs_1_, ...), custom_call_target="tpu_custom_call" | custom-call | flops 402653184 | bytes 1572864 | tf_op jit(solution)/shard_map/table/pallas_call | solution.py:191
  22.6 1.8 %collective-permute-start.2 = (bf16[64,2048]{1,0:T(8,128)(2,1)S(1)}, bf16[64,2048]{1,0:T(8,128)(2,1)S(1)}, u32[]{:S(2)}, u32[]{:S(2)}) collective-permute-start(bf16[64,2048]{1,0:T(8,128)(2,1)S(1)} %get-tuple-element.13), channel_id=1, source_target_pairs={{0,2},{1,5},{2,0},{3,7},{4,6},{5,1},{6,4},{7,3},{8,10},{9,13},{10,... | collective-permute-start | bytes 786440 | tf_op jit(solution)/shard_map/ppermute | solution.py:205
  24.4 4.7 %collective-permute-done.2 = bf16[64,2048]{1,0:T(8,128)(2,1)S(1)} collective-permute-done((bf16[64,2048]{1,0:T(8,128)(2,1)S(1)}, bf16[64,2048]{1,0:T(8,128)(2,1)S(1)}, u32[]{:S(2)}, u32[]{:S(2)}) %collective-permute-start.2) | collective-permute-done | bytes 262176 | tf_op jit(solution)/shard_map/ppermute | solution.py:205
  29.1 1.8 %collective-permute-start.3 = (bf16[64,2048]{1,0:T(8,128)(2,1)S(1)}, bf16[64,2048]{1,0:T(8,128)(2,1)S(1)}, u32[]{:S(2)}, u32[]{:S(2)}) collective-permute-start(bf16[64,2048]{1,0:T(8,128)(2,1)S(1)} %fusion), channel_id=1, source_target_pairs={{0,4},{1,9},{2,6},{3,11},{4,0},{5,13},{6,2},{7,15},{8,12},{9,1},{1... | collective-permute-start | bytes 786440 | tf_op jit(solution)/shard_map/ppermute | solution.py:205
  30.9 4.6 %collective-permute-done.3 = bf16[64,2048]{1,0:T(8,128)(2,1)S(1)} collective-permute-done((bf16[64,2048]{1,0:T(8,128)(2,1)S(1)}, bf16[64,2048]{1,0:T(8,128)(2,1)S(1)}, u32[]{:S(2)}, u32[]{:S(2)}) %collective-permute-start.3) | collective-permute-done | bytes 262176 | tf_op jit(solution)/shard_map/ppermute | solution.py:205
  35.5 0.1 fusion.1
  35.6 1.6 %collective-permute-start.4 = (bf16[64,2048]{1,0:T(8,128)(2,1)S(1)}, bf16[64,2048]{1,0:T(8,128)(2,1)S(1)}, u32[]{:S(2)}, u32[]{:S(2)}) collective-permute-start(bf16[64,2048]{1,0:T(8,128)(2,1)S(1)} %get-tuple-element.15), channel_id=1, source_target_pairs={{0,8},{1,3},{2,10},{3,1},{4,12},{5,7},{6,14},{7,5},{8,0},{9,11},{1... | collective-permute-start | bytes 786440 | tf_op jit(solution)/shard_map/ppermute | solution.py:205
  37.2 4.8 %collective-permute-done.4.recv_ref = bf16[64,2048]{1,0:T(8,128)(2,1)S(1)} collective-permute-done((bf16[64,2048]{1,0:T(8,128)(2,1)S(1)}, bf16[64,2048]{1,0:T(8,128)(2,1)S(1)}, u32[]{:S(2)}, u32[]{:S(2)}) %collective-permute-start.4) | collective-permute-done | bytes 262176 | tf_op jit(solution)/shard_map/ppermute | solution.py:205
  42.0 2.4 %back.1 = f32[48,1024]{1,0:T(8,128)S(1)} custom-call(f32[64,2048]{1,0:T(8,128)S(1)} %get-tuple-element.16.acc_ref, bf16[64,2048]{1,0:T(8,128)(2,1)S(1)} %collective-permute-done.4.recv_ref, f32[8,2048]{1,0:T(8,128)S(1)} %copy-done, bf16[2,2048,1024]{2,1,0:T(8,128)(2,1)S(1)} %get-tuple-element.14.tab_ref), custom_call_target="tpu_custom_call" | custom-call | flops 402653184 | bytes 1572864 | tf_op jit(solution)/shard_map/back/pallas_call | solution.py:209
  44.5 0.1 collective-permute-start.5
  44.5 1.2 %collective-permute-done.5 = bf16[48,512]{1,0:T(8,128)(2,1)S(1)} collective-permute-done((bf16[48,512]{1,0:T(8,128)(2,1)S(1)}, bf16[48,512]{1,0:T(8,128)(2,1)S(1)}, u32[]{:S(2)}, u32[]{:S(2)}) %collective-permute-start.5) | collective-permute-done | bytes 49184 | tf_op jit(solution)/shard_map/ppermute | solution.py:172
  45.8 2.7 %collective-permute-start.6 = (bf16[48,256]{1,0:T(8,128)(2,1)S(1)}, bf16[48,256]{1,0:T(8,128)(2,1)S(1)}, u32[]{:S(2)}, u32[]{:S(2)}) collective-permute-start(bf16[48,256]{1,0:T(8,128)(2,1)S(1)} %slice.27), channel_id=1, source_target_pairs={{0,16},{1,17},{2,18},{3,19},{4,20},{5,21},{6,22},{7,23},{8,24},{9,... | collective-permute-start | bytes 73736 | tf_op jit(solution)/shard_map/ppermute | solution.py:172
  48.5 2.1 %collective-permute-done.6 = bf16[48,256]{1,0:T(8,128)(2,1)S(1)} collective-permute-done((bf16[48,256]{1,0:T(8,128)(2,1)S(1)}, bf16[48,256]{1,0:T(8,128)(2,1)S(1)}, u32[]{:S(2)}, u32[]{:S(2)}) %collective-permute-start.6) | collective-permute-done | bytes 24608 | tf_op jit(solution)/shard_map/ppermute | solution.py:172
  50.6 0.6 %slice_add_fusion.1 = f32[48,256]{1,0:T(8,128)} fusion(f32[48,512]{1,0:T(8,128)S(1)} %slice_add_fusion, bf16[48,256]{1,0:T(8,128)(2,1)S(1)} %collective-permute-done.6), kind=kLoop, calls=%fused_computation.7 | loop fusion | flops 24576 | bytes 122880 | tf_op jit(solution)/shard_map/add | solution.py:215
  (9 shorter events, 0.1 us)
Async XLA Ops:
  0.0 0.8 %copy-start.1 = (f32[3,16,256]{2,1,0:T(8,128)S(1)}, f32[3,16,256]{2,1,0:T(8,128)}, u32[]{:S(2)}) copy-start(f32[3,16,256]{2,1,0:T(8,128)} %force_ref.1) | copy-start | bytes 147460
  0.8 0.7 %copy-start.2 = (f32[3,256]{1,0:T(4,128)S(1)}, f32[3,256]{1,0:T(4,128)}, u32[]{:S(2)}) copy-start(f32[3,256]{1,0:T(4,128)} %pos_ref.1) | copy-start | bytes 9220
  1.5 6.4 %collective-permute-start = (bf16[64,256]{1,0:T(8,128)(2,1)S(1)}, bf16[64,256]{1,0:T(8,128)(2,1)S(1)}, u32[]{:S(2)}, u32[]{:S(2)}) collective-permute-start(bf16[64,256]{1,0:T(8,128)(2,1)S(1)} %pack.1.refs_0_), channel_id=1, source_target_pairs={{0,16},{1,17},{2,18},{3,19},{4,20},{5,21},{6,22},{7,23},{8,24},{9,... | collective-permute-start | bytes 98312 | tf_op jit(solution)/shard_map/ppermute | solution.py:172
  7.9 1.9 %collective-permute-start.1 = (bf16[2,64,256]{2,1,0:T(8,128)(2,1)S(1)}, bf16[2,64,256]{2,1,0:T(8,128)(2,1)S(1)}, u32[]{:S(2)}, u32[]{:S(2)}) collective-permute-start(bf16[2,64,256]{2,1,0:T(8,128)(2,1)S(1)} %pad_maximum_fusion), channel_id=1, source_target_pairs={{0,1},{1,0},{2,3},{3,2},{4,5},{5,4},{6,7},{7,6},{8,9},{9,8},{10,11... | collective-permute-start | bytes 196616 | tf_op jit(solution)/shard_map/ppermute | solution.py:172
  9.8 0.8 %copy-start = (f32[8,2048]{1,0:T(8,128)S(1)}, f32[8,2048]{1,0:T(8,128)}, u32[]{:S(2)}) copy-start(f32[8,2048]{1,0:T(8,128)} %get-tuple-element.10.frame_ref) | copy-start | bytes 196612
  10.7 1.0 %copy-start.3 = (bf16[2048,16]{1,0:T(8,128)(2,1)S(1)}, bf16[2048,16]{1,0:T(8,128)(2,1)}, u32[]{:S(2)}) copy-start(bf16[2048,16]{1,0:T(8,128)(2,1)} %get-tuple-element.11.wt_ref) | copy-start | bytes 196612
  22.6 6.4 %collective-permute-start.2 = (bf16[64,2048]{1,0:T(8,128)(2,1)S(1)}, bf16[64,2048]{1,0:T(8,128)(2,1)S(1)}, u32[]{:S(2)}, u32[]{:S(2)}) collective-permute-start(bf16[64,2048]{1,0:T(8,128)(2,1)S(1)} %get-tuple-element.13), channel_id=1, source_target_pairs={{0,2},{1,5},{2,0},{3,7},{4,6},{5,1},{6,4},{7,3},{8,10},{9,13},{10,... | collective-permute-start | bytes 786440 | tf_op jit(solution)/shard_map/ppermute | solution.py:205
  29.1 6.4 %collective-permute-start.3 = (bf16[64,2048]{1,0:T(8,128)(2,1)S(1)}, bf16[64,2048]{1,0:T(8,128)(2,1)S(1)}, u32[]{:S(2)}, u32[]{:S(2)}) collective-permute-start(bf16[64,2048]{1,0:T(8,128)(2,1)S(1)} %fusion), channel_id=1, source_target_pairs={{0,4},{1,9},{2,6},{3,11},{4,0},{5,13},{6,2},{7,15},{8,12},{9,1},{1... | collective-permute-start | bytes 786440 | tf_op jit(solution)/shard_map/ppermute | solution.py:205
  35.6 6.4 %collective-permute-start.4 = (bf16[64,2048]{1,0:T(8,128)(2,1)S(1)}, bf16[64,2048]{1,0:T(8,128)(2,1)S(1)}, u32[]{:S(2)}, u32[]{:S(2)}) collective-permute-start(bf16[64,2048]{1,0:T(8,128)(2,1)S(1)} %get-tuple-element.15), channel_id=1, source_target_pairs={{0,8},{1,3},{2,10},{3,1},{4,12},{5,7},{6,14},{7,5},{8,0},{9,11},{1... | collective-permute-start | bytes 786440 | tf_op jit(solution)/shard_map/ppermute | solution.py:205
  44.5 1.3 %collective-permute-start.5 = (bf16[48,512]{1,0:T(8,128)(2,1)S(1)}, bf16[48,512]{1,0:T(8,128)(2,1)S(1)}, u32[]{:S(2)}, u32[]{:S(2)}) collective-permute-start(bf16[48,512]{1,0:T(8,128)(2,1)S(1)} %slice.26), channel_id=1, source_target_pairs={{0,1},{1,0},{2,3},{3,2},{4,5},{5,4},{6,7},{7,6},{8,9},{9,8},{10,11... | collective-permute-start | bytes 147464 | tf_op jit(solution)/shard_map/ppermute | solution.py:172
  45.8 4.8 %collective-permute-start.6 = (bf16[48,256]{1,0:T(8,128)(2,1)S(1)}, bf16[48,256]{1,0:T(8,128)(2,1)S(1)}, u32[]{:S(2)}, u32[]{:S(2)}) collective-permute-start(bf16[48,256]{1,0:T(8,128)(2,1)S(1)} %slice.27), channel_id=1, source_target_pairs={{0,16},{1,17},{2,18},{3,19},{4,20},{5,21},{6,22},{7,23},{8,24},{9,... | collective-permute-start | bytes 73736 | tf_op jit(solution)/shard_map/ppermute | solution.py:172

commit v3 on v2

v3 whole, which is shorter than its diff:
```python
import functools

import jax
import jax.numpy as jnp
from jax import lax
from jax.experimental import pallas as pl
from jax.experimental.pallas import tpu as pltpu
from jax.sharding import PartitionSpec as P

two_pi = 6.283185307179586
radius = 0.005
xi_split = 40.0
AXES = ("wide", "narrow")
VMEM = pltpu.VMEM
SMEM = pltpu.SMEM
f32, bf16 = jnp.float32, jnp.bfloat16

SIN = (4.442867901617319, -7.307443368323551, 3.594787581869042, -0.7843727161608242)
COS = (1.414213496635887, -6.9788509910181, 5.739461197516664, -1.8835630614207908, 0.31069820075132315)
ROUND = 12582912.0
HEAD = 16


def horner(coeffs, q):
    total = coeffs[-1] * q + coeffs[-2]
    for c in reversed(coeffs[:-2]):
        total = total * q + c
    return total


def call(kernel, out_shape, name, specs, scratch=(), flops=0):
    many = isinstance(out_shape, (list, tuple))
    spaces = {"v": VMEM, "s": SMEM, "h": pl.ANY}
    return pl.pallas_call(
        kernel,
        out_shape=out_shape,
        in_specs=[pl.BlockSpec(memory_space=spaces[x]) for x in specs],
        out_specs=[pl.BlockSpec(memory_space=VMEM)] * len(out_shape) if many else pl.BlockSpec(memory_space=VMEM),
        scratch_shapes=scratch,
        name=name,
        compiler_params=pltpu.CompilerParams(vmem_limit_bytes=24 << 20),
        cost_estimate=pl.CostEstimate(flops=flops, bytes_accessed=flops // 256, transcendentals=0),
    )


def split3(x):
    hi = x.astype(bf16)
    rest = x - hi.astype(f32)
    mid = rest.astype(bf16)
    low = (rest - mid.astype(f32)).astype(bf16)
    return hi, mid, low


def pack_kernel(pos_ref, force_ref, out_ref):
    hi, mid, low = split3(pos_ref[...])
    rows = out_ref.shape[1]
    parts = [hi.astype(f32), mid.astype(f32), low.astype(f32), jnp.zeros((HEAD - 9, rows), f32)]
    out_ref[:HEAD, :] = jnp.concatenate(parts, axis=0).astype(bf16)
    for a in range(force_ref.shape[0]):
        p = force_ref.shape[1]
        out_ref[HEAD + a * p : HEAD + (a + 1) * p, :] = force_ref[a].astype(bf16)


def frame_kernel(amp, idx_ref, waves_ref, frame_ref, wt_ref, own_ref, sem):
    kwaves = own_ref.shape[1]
    first = pl.multiple_of(idx_ref[0] * kwaves, 128)
    copy = pltpu.make_async_copy(waves_ref.at[:, pl.ds(first, kwaves)], own_ref, sem)
    copy.start()
    copy.wait()
    m = own_ref[...].astype(f32)
    msq = jnp.sum(m * m, axis=0, keepdims=True)
    n = m * lax.rsqrt(msq)
    nx, ny, nz = n[0:1], n[1:2], n[2:3]
    sign = jnp.where(nz >= 0.0, 1.0, -1.0)
    a = -1.0 / (sign + nz)
    b = nx * ny * a
    ksq = (two_pi * two_pi) * msq
    qarg = ksq / (4.0 * xi_split * xi_split)
    factor = amp * (1.0 - radius * radius * ksq / 3.0) * (1.0 + qarg + 2.0 * qarg * qarg) * jnp.exp(-qarg) / ksq
    frame_ref[...] = jnp.concatenate(
        [1.0 + sign * nx * nx * a, sign * b, -sign * nx, b, sign + ny * ny * a, -ny, factor, jnp.zeros_like(b)], axis=0
    )
    head = jnp.concatenate([m, m, m, jnp.zeros((HEAD - 9, kwaves), f32)], axis=0)
    wt_ref[...] = jnp.transpose(head).astype(bf16)


def trig(w, phase, tab_ref, rows, cols):
    u = jnp.dot(w, phase, preferred_element_type=f32)
    r = u - ((u + ROUND) - ROUND)
    q = r * r
    s = r * horner(SIN, q)
    tab_ref[0, rows, cols] = (1.0 - s * s).astype(bf16)
    tab_ref[1, rows, cols] = (s * horner(COS, q)).astype(bf16)


def trig_kernel(first, wt_ref, pack_ref, tab_ref):
    strip = 64
    phase = pack_ref[:HEAD]

    def step(t, carry):
        row = pl.multiple_of(t * strip, strip)
        trig(wt_ref[pl.ds(first + row, strip), :], phase, tab_ref, pl.ds(row, strip), slice(None))
        return carry

    lax.fori_loop(0, tab_ref.shape[1] // strip, step, 0, unroll=4)


def unpacked(refs):
    blocks = []
    for ref in refs:
        blocks.extend([ref[...]] if len(ref.shape) == 2 else [ref[j] for j in range(ref.shape[0])])
    return blocks


def sums_kernel(first, offsets, chunk, frame_ref, wt_ref, *refs):
    count = len(offsets)
    ready, packs, todo = refs[:count], refs[count : 2 * count], refs[2 * count : -3]
    tab_ref, acc_ref, send_ref = refs[-3:]
    kwaves = tab_ref.shape[1]
    probes = acc_ref.shape[0] // 4
    blocks = unpacked(todo)
    width = blocks[0].shape[1]
    forces = jnp.concatenate([b[HEAD:] for b in blocks], axis=1)
    strip = 32

    def step(c, carry):
        base = pl.multiple_of(c * chunk, chunk)
        for t in range(chunk // strip):
            row = pl.multiple_of(base + t * strip, strip)
            w = wt_ref[pl.ds(first + row, strip), :]
            for j, block in enumerate(blocks):
                trig(w, block[:HEAD], tab_ref, pl.ds(row, strip), slice(j * width, (j + 1) * width))
        fr = frame_ref[:, pl.ds(first + base, chunk)]
        for part in range(2):
            sums = jnp.zeros((3 * probes, chunk), f32)
            for offset, table, pack in zip(offsets, ready, packs):
                t = table[part, pl.ds(offset + base, chunk), :]
                sums += lax.dot_general(pack[HEAD:], t, (((1,), (1,)), ((), ())), preferred_element_type=f32)
            t = tab_ref[part, pl.ds(base, chunk), :]
            sums += lax.dot_general(forces, t, (((1,), (1,)), ((), ())), preferred_element_type=f32)
            for j in range(2):
                value = sum(fr[3 * j + x : 3 * j + x + 1] * sums[x * probes : (x + 1) * probes] for x in range(3))
                low = (2 * part + j) * probes
                acc_ref[low : low + probes, pl.ds(base, chunk)] = value
                send_ref[low : low + probes, pl.ds(base, chunk)] = value.astype(bf16)
        return carry

    lax.fori_loop(0, kwaves // chunk, step, 0)


def back_kernel(first, offsets, chunk, last, acc_ref, recv_ref, frame_ref, *refs):
    tables = refs[: len(offsets)]
    rest = refs[len(offsets) :]
    kwaves = acc_ref.shape[1]
    probes = acc_ref.shape[0] // 4
    halves = []
    for part in range(2):
        cols = slice(first, first + kwaves)
        t0, t1 = (
            frame_ref[6:7, cols] * (acc_ref[low : low + probes] + recv_ref[low : low + probes].astype(f32))
            for low in (2 * part * probes, (2 * part + 1) * probes)
        )
        halves.append(
            jnp.concatenate([frame_ref[x : x + 1, cols] * t0 + frame_ref[3 + x : 4 + x, cols] * t1 for x in range(3)], axis=0).astype(bf16)
        )
    begin = 0
    for offset, table in zip(offsets, tables):
        width = table.shape[2]
        total = sum(
            jnp.dot(halves[part], table[part, offset : offset + kwaves, :], preferred_element_type=f32) for part in range(2)
        )
        if not last:
            rest[0][:, begin : begin + width] = total
            begin += width
            continue
        earlier, keep, send = rest
        total += earlier[:, begin : begin + width]
        split = keep.shape[1]
        if begin < split:
            keep[:, begin : min(begin + width, split)] = total[:, : split - begin]
        if begin + width > split:
            low = max(begin, split)
            send[:, low - split : begin + width - split] = total[:, low - begin :].astype(bf16)
        begin += width


def shards(positions, forces, waves):
    wide, narrow = lax.axis_size("wide"), lax.axis_size("narrow")
    devices = wide * narrow
    bits = devices.bit_length() - 1
    assert devices == 1 << bits and bits >= 2
    rows = positions.shape[1]
    kwaves = waves.shape[1]
    half = forces.shape[0] * forces.shape[1]
    probes = forces.shape[1]
    top = devices >> 1
    amp = 20000.0 / float(rows * devices * kwaves) ** 0.5

    def swap(x, bit):
        return lax.ppermute(x, AXES, [(d, d ^ bit) for d in range(devices)])

    me = lax.axis_index(AXES)
    block = 2 * (me // top) + me % 2
    mine = kwaves // 4
    part = mine // 2
    fl = 4 * half * rows
    shape = jax.ShapeDtypeStruct
    own = call(pack_kernel, shape((HEAD + half, rows), bf16), "pack", "vv")(positions, forces)
    far = swap(own, top)
    frame, wt = call(
        functools.partial(frame_kernel, amp),
        (shape((8, mine), f32), shape((mine, HEAD), bf16)),
        "frame",
        "sh",
        scratch=[VMEM((3, mine), jnp.int32), pltpu.SemaphoreType.DMA],
        flops=mine * 1000,
    )(block.reshape(1), waves)
    tab_own = call(functools.partial(trig_kernel, 0), shape((2, mine, rows), bf16), "trig_own", "vv", flops=mine * fl)(wt, own)
    both, tab_own, frame, wt = lax.optimization_barrier((jnp.stack([own, far]), tab_own, frame, wt))
    near = swap(both, 1)
    tab_far = call(functools.partial(trig_kernel, 0), shape((2, part, rows), bf16), "trig_far", "vv", flops=part * fl)(wt, far)

    def sums(first, offsets, ready, packs, todo, width):
        return call(
            functools.partial(sums_kernel, first, offsets, 256),
            (shape((2, part, width), bf16), shape((4 * probes, part), f32), shape((4 * probes, part), bf16)),
            "sums",
            "v" * (2 + 2 * len(ready) + len(todo)),
            flops=part * fl * (width // rows),
        )(frame, wt, *ready, *packs, *todo)

    middle = [1 << j for j in range(1, bits - 1)]
    steps = len(middle)

    def exchange(x, j, chunk):
        turn = [middle[(j + core + 2 * chunk) % steps] for core in range(2)]
        return lax.ppermute(x, AXES, [(d, d ^ turn[d % 2]) for d in range(devices)])

    tab_a, acc_a, send_a = sums(0, (0, 0), (tab_own, tab_far), (own, far), (near,), 2 * rows)
    tab_b, acc_b, send_b = sums(part, (part,), (tab_own,), (own,), (far, near), 3 * rows)
    state = [[acc_a, send_a, None], [acc_b, send_b, None]]
    for j in range(steps):
        for chunk in range(2):
            acc, send, _ = state[chunk]
            got = exchange(send, j, chunk)
            if j + 1 < steps:
                acc = acc + got.astype(f32)
                send = acc.astype(bf16)
            state[chunk] = [acc, send, got]
    first = call(
        functools.partial(back_kernel, 0, (0, 0, 0), 256, False), shape((half, 4 * rows), f32), "back", "vvvvvv", flops=part * fl * 4
    )(state[0][0], state[0][2], frame, tab_own, tab_far, tab_a)
    keep, send = call(
        functools.partial(back_kernel, part, (part, 0), 256, True),
        (shape((half, 2 * rows), f32), shape((half, 2 * rows), bf16)),
        "back",
        "vvvvvv",
        flops=part * fl * 4,
    )(state[1][0], state[1][2], frame, tab_own, tab_b, first)
    there = swap(send, 1)
    keep = keep + there.astype(f32)
    there = swap(keep[:, rows:].astype(bf16), top)
    total = keep[:, :rows] + there.astype(f32)
    return total.reshape(forces.shape)


def solution(mesh):
    placed = (P(None, AXES), P(None, None, AXES), P())
    return jax.shard_map(
        shards,
        mesh=mesh,
        in_specs=placed,
        out_specs=P(None, None, AXES),
        check_vma=False,
    )
```

time: 51.6 us -> 45.5 us (0.88)
  waiting for transfers between devices: 19.7 us -> 15.3 us
  Pallas kernels: 15.1 us -> 13.8 us
  local copies, waits for them, and re-layouts: 3.37 us -> 2.39 us
  starting transfers between devices: 12.1 us -> 12.9 us
    ppermute x3 -> x6, waiting for transfers between devices: 14.1 us -> 10.2 us  [exchange(): return lax.ppermute(x, AXES, [(d, d ^ turn[d % 2]) for d in range(devices)])]
    ppermute x3 -> x6, starting transfers between devices: 5.18 us -> 7.53 us  [exchange(): return lax.ppermute(x, AXES, [(d, d ^ turn[d % 2]) for d in range(devices)])]
    ppermute x4, starting transfers between devices: 6.93 us -> 5.34 us  [swap(): return lax.ppermute(x, AXES, [(d, d ^ bit) for d in range(devices)])]
    pallas_call x4 -> x8, Pallas kernels: 15.1 us -> 13.8 us  [the longest x2 7.94 us: sums(): call(functools.partial(sums_kernel, first, offsets, 256), (shape((2, part...]
    unnamed x8 -> x6, local copies, waits for them, and re-layouts: 3.36 us -> 2.39 us
  transfers between devices with their start and end apart: 7 -> 10, of which waited for: 6 -> 6; matrix products, arithmetic and copies ran while one was open for 0% -> 0% of each run, Pallas kernels for 4% -> 21%
where the time goes in v3:
time: 45.5 us; the launch traced here: 45.3 us
  waiting for transfers between devices  15.3 us (34%)
  Pallas kernels  13.8 us (30%)
  starting transfers between devices  12.9 us (28%)
  local copies, waits for them, and re-layouts  2.39 us (5%)
  other arithmetic  0.8 us (2%)
    ppermute x6, waiting for transfers between devices, exchange(): return lax.ppermute(x, AXES, [(d, d ^ turn[d % 2]) for d in range(devices)])  10.2 us
    pallas_call x2, Pallas kernels, sums(): call(functools.partial(sums_kernel, first, offsets, 256), (shape((2, part...  7.94 us
    ppermute x6, starting transfers between devices, exchange(): return lax.ppermute(x, AXES, [(d, d ^ turn[d % 2]) for d in range(devices)])  7.53 us
    ppermute x4, starting transfers between devices, swap(): return lax.ppermute(x, AXES, [(d, d ^ bit) for d in range(devices)])  5.34 us
    ppermute x4, waiting for transfers between devices, swap(): return lax.ppermute(x, AXES, [(d, d ^ bit) for d in range(devices)])  5.11 us
    pallas_call x1, Pallas kernels, shards(): call(functools.partial(trig_kernel, 0), shape((2, mine, rows), bf16), 'tr...  2.63 us
    unnamed x6, local copies, waits for them, and re-layouts  2.39 us
    pallas_call x1, Pallas kernels, shards(): call(functools.partial(trig_kernel, 0), shape((2, part, rows), bf16), 'tr...  1.32 us
  transfers between devices with their start and end apart: 10, of which 6 were waited for; matrix products, arithmetic and copies ran while one was open for 0% of the time, Pallas kernels for 21%

profile of v3, /device:TPU:0, one launch (start us, length us, event | category | flops | bytes accessed | tf_op | source)
XLA Modules:
  0.0 45.3 jit_solution(18063461504987336839)
XLA Ops:
  0.0 0.8 %copy-done.1 = f32[3,16,256]{2,1,0:T(8,128)S(1)} copy-done((f32[3,16,256]{2,1,0:T(8,128)S(1)}, f32[3,16,256]{2,1,0:T(8,128)}, u32[]{:S(2)}) %copy-start.1) | copy-done | bytes 49176
  0.8 0.7 %copy-done.2 = f32[3,256]{1,0:T(4,128)S(1)} copy-done((f32[3,256]{1,0:T(4,128)S(1)}, f32[3,256]{1,0:T(4,128)}, u32[]{:S(2)}) %copy-start.2) | copy-done | bytes 3096
  1.5 4.1 %collective-permute-start = (bf16[64,256]{1,0:T(8,128)(2,1)S(1)}, bf16[64,256]{1,0:T(8,128)(2,1)S(1)}, u32[]{:S(2)}, u32[]{:S(2)}) collective-permute-start(bf16[64,256]{1,0:T(8,128)(2,1)S(1)} %pack.1.pack_ref.refs_1_.refs_2_), channel_id=1, source_target_pairs={{0,16},{1,17},{2,18},{3,19},{4,20},{5,21},{6,22},{7,23},{8,24},{9,... | collective-permute-start | bytes 98312 | tf_op jit(solution)/shard_map/ppermute | solution.py:200
  5.6 0.9 %copy-done = s32[3,8192]{1,0:T(4,128)S(1)} copy-done((s32[3,8192]{1,0:T(4,128)S(1)}, s32[3,8192]{1,0:T(4,128)}, u32[]{:S(2)}) %copy-start) | copy-done | bytes 98328
  6.5 0.3 frame.1
  6.8 2.6 %trig_own.1.refs_0_ = bf16[2,2048,256]{2,1,0:T(8,128)(2,1)S(1)} custom-call(bf16[2048,16]{1,0:T(8,128)(2,1)S(1)} %get-tuple-element.22.wt_ref, bf16[64,256]{1,0:T(8,128)(2,1)S(1)} %pack.1.pack_ref.refs_1_.refs_2_), custom_call_target="tpu_custom_call" | custom-call | flops 100663296 | bytes 393216 | tf_op jit(solution)/shard_map/trig_own/pallas_call | solution.py:218
  9.6 1.3 %trig_far.1.refs_1_ = bf16[2,1024,256]{2,1,0:T(8,128)(2,1)S(1)} custom-call(bf16[2048,16]{1,0:T(8,128)(2,1)S(1)} %get-tuple-element.22.wt_ref, bf16[64,256]{1,0:T(8,128)(2,1)S(1)} %collective-permute-done.refs_2_.pack_ref.refs_3_), custom_call_target="tpu_custom_call" | custom-call | flops 50331648 | bytes 196608 | tf_op jit(solution)/shard_map/trig_far/pallas_call | solution.py:221
  10.9 3.3 %sums.3 = (bf16[2,1024,512]{2,1,0:T(8,128)(2,1)S(1)}, f32[64,1024]{1,0:T(8,128)S(1)}, bf16[64,1024]{1,0:T(8,128)(2,1)S(1)}) custom-call(f32[8,2048]{1,0:T(8,128)S(1)} %get-tuple-element.21.frame_ref, bf16[2048,16]{1,0:T(8,128)(2,1)S(1)} %get-tuple-element.22.wt_ref, bf16[2,2048,256]{2,1,0:T(8,128)(2,1)S(1)} %trig_own.1.refs_0_, ...), custom_call_target="tpu_custom_call" | custom-call | flops 100663296 | bytes 393216 | tf_op jit(solution)/shard_map/sums/pallas_call | solution.py:224
  14.2 1.6 %collective-permute-start.5 = (bf16[64,1024]{1,0:T(8,128)(2,1)S(1)}, bf16[64,1024]{1,0:T(8,128)(2,1)S(1)}, u32[]{:S(2)}, u32[]{:S(2)}) collective-permute-start(bf16[64,1024]{1,0:T(8,128)(2,1)S(1)} %get-tuple-element.29), channel_id=1, source_target_pairs={{0,2},{1,5},{2,0},{3,7},{4,6},{5,1},{6,4},{7,3},{8,10},{9,13},{10,... | collective-permute-start | bytes 393224 | tf_op jit(solution)/shard_map/ppermute | solution.py:237
  15.8 4.6 %sums.2 = (bf16[2,1024,768]{2,1,0:T(8,128)(2,1)S(1)}, f32[64,1024]{1,0:T(8,128)S(1)}, bf16[64,1024]{1,0:T(8,128)(2,1)S(1)}) custom-call(f32[8,2048]{1,0:T(8,128)S(1)} %get-tuple-element.21.frame_ref, bf16[2048,16]{1,0:T(8,128)(2,1)S(1)} %get-tuple-element.22.wt_ref, bf16[2,2048,256]{2,1,0:T(8,128)(2,1)S(1)} %trig_own.1.refs_0_, ...), custom_call_target="tpu_custom_call" | custom-call | flops 150994944 | bytes 589824 | tf_op jit(solution)/shard_map/sums/pallas_call | solution.py:224
  20.4 1.6 %collective-permute-start.2 = (bf16[64,1024]{1,0:T(8,128)(2,1)S(1)}, bf16[64,1024]{1,0:T(8,128)(2,1)S(1)}, u32[]{:S(2)}, u32[]{:S(2)}) collective-permute-start(bf16[64,1024]{1,0:T(8,128)(2,1)S(1)} %get-tuple-element.26), channel_id=1, source_target_pairs={{0,8},{1,3},{2,10},{3,1},{4,12},{5,7},{6,14},{7,5},{8,0},{9,11},{1... | collective-permute-start | bytes 393224 | tf_op jit(solution)/shard_map/ppermute | solution.py:237
  22.1 1.6 %collective-permute-start.6 = (bf16[64,1024]{1,0:T(8,128)(2,1)S(1)}, bf16[64,1024]{1,0:T(8,128)(2,1)S(1)}, u32[]{:S(2)}, u32[]{:S(2)}) collective-permute-start(bf16[64,1024]{1,0:T(8,128)(2,1)S(1)} %fusion.1), channel_id=1, source_target_pairs={{0,4},{1,9},{2,6},{3,11},{4,0},{5,13},{6,2},{7,15},{8,12},{9,1},{1... | collective-permute-start | bytes 393224 | tf_op jit(solution)/shard_map/ppermute | solution.py:237
  23.7 2.6 %collective-permute-done.2 = bf16[64,1024]{1,0:T(8,128)(2,1)S(1)} collective-permute-done((bf16[64,1024]{1,0:T(8,128)(2,1)S(1)}, bf16[64,1024]{1,0:T(8,128)(2,1)S(1)}, u32[]{:S(2)}, u32[]{:S(2)}) %collective-permute-start.2) | collective-permute-done | bytes 131104 | tf_op jit(solution)/shard_map/ppermute | solution.py:237
  26.3 0.6 %collective-permute-start.3 = (bf16[64,1024]{1,0:T(8,128)(2,1)S(1)}, bf16[64,1024]{1,0:T(8,128)(2,1)S(1)}, u32[]{:S(2)}, u32[]{:S(2)}) collective-permute-start(bf16[64,1024]{1,0:T(8,128)(2,1)S(1)} %fusion), channel_id=1, source_target_pairs={{0,2},{1,5},{2,0},{3,7},{4,6},{5,1},{6,4},{7,3},{8,10},{9,13},{10,... | collective-permute-start | bytes 393224 | tf_op jit(solution)/shard_map/ppermute | solution.py:237
  27.2 1.4 %collective-permute-start.7 = (bf16[64,1024]{1,0:T(8,128)(2,1)S(1)}, bf16[64,1024]{1,0:T(8,128)(2,1)S(1)}, u32[]{:S(2)}, u32[]{:S(2)}) collective-permute-start(bf16[64,1024]{1,0:T(8,128)(2,1)S(1)} %get-tuple-element.33), channel_id=1, source_target_pairs={{0,8},{1,3},{2,10},{3,1},{4,12},{5,7},{6,14},{7,5},{8,0},{9,11},{1... | collective-permute-start | bytes 393224 | tf_op jit(solution)/shard_map/ppermute | solution.py:237
  28.6 3.9 %collective-permute-done.3 = bf16[64,1024]{1,0:T(8,128)(2,1)S(1)} collective-permute-done((bf16[64,1024]{1,0:T(8,128)(2,1)S(1)}, bf16[64,1024]{1,0:T(8,128)(2,1)S(1)}, u32[]{:S(2)}, u32[]{:S(2)}) %collective-permute-start.3) | collective-permute-done | bytes 131104 | tf_op jit(solution)/shard_map/ppermute | solution.py:237
  32.5 0.7 %collective-permute-start.4 = (bf16[64,1024]{1,0:T(8,128)(2,1)S(1)}, bf16[64,1024]{1,0:T(8,128)(2,1)S(1)}, u32[]{:S(2)}, u32[]{:S(2)}) collective-permute-start(bf16[64,1024]{1,0:T(8,128)(2,1)S(1)} %get-tuple-element.35), channel_id=1, source_target_pairs={{0,4},{1,9},{2,6},{3,11},{4,0},{5,13},{6,2},{7,15},{8,12},{9,1},{1... | collective-permute-start | bytes 393224 | tf_op jit(solution)/shard_map/ppermute | solution.py:237
  33.2 0.8 %back.2.refs_2_ = f32[48,1024]{1,0:T(8,128)S(1)} custom-call(f32[64,1024]{1,0:T(8,128)S(1)} %get-tuple-element.34.acc_ref, bf16[64,1024]{1,0:T(8,128)(2,1)S(1)} %collective-permute-done.7.recv_ref, f32[8,2048]{1,0:T(8,128)S(1)} %get-tuple-element.21.frame_ref, bf16[2,2048,256]{2,1,0:T(8,128)(2,1)S(1)} %trig_own.1.refs_0_, ...), custom_call_target="tpu_custom_call" | custom-call | flops 201326592 | bytes 786432 | tf_op jit(solution)/shard_map/back/pallas_call | solution.py:250
  34.1 3.5 %collective-permute-done.4.recv_ref = bf16[64,1024]{1,0:T(8,128)(2,1)S(1)} collective-permute-done((bf16[64,1024]{1,0:T(8,128)(2,1)S(1)}, bf16[64,1024]{1,0:T(8,128)(2,1)S(1)}, u32[]{:S(2)}, u32[]{:S(2)}) %collective-permute-start.4) | collective-permute-done | bytes 131104 | tf_op jit(solution)/shard_map/ppermute | solution.py:237
  37.6 0.8 %back.3 = (f32[48,512]{1,0:T(8,128)S(1)}, bf16[48,512]{1,0:T(8,128)(2,1)S(1)}) custom-call(f32[64,1024]{1,0:T(8,128)S(1)} %get-tuple-element.36.acc_ref, bf16[64,1024]{1,0:T(8,128)(2,1)S(1)} %collective-permute-done.4.recv_ref, f32[8,2048]{1,0:T(8,128)S(1)} %get-tuple-element.21.frame_ref, bf16[2,2048,256]{2,1,0:T(8,128)(2,1)S(1)} %trig_own.1.refs_0_, ...), custom_call_target="tpu_custom_call" | custom-call | flops 201326592 | bytes 786432 | tf_op jit(solution)/shard_map/back/pallas_call | solution.py:253
  38.5 1.2 %collective-permute-done.8 = bf16[48,512]{1,0:T(8,128)(2,1)S(1)} collective-permute-done((bf16[48,512]{1,0:T(8,128)(2,1)S(1)}, bf16[48,512]{1,0:T(8,128)(2,1)S(1)}, u32[]{:S(2)}, u32[]{:S(2)}) %collective-permute-start.8) | collective-permute-done | bytes 49184 | tf_op jit(solution)/shard_map/ppermute | solution.py:200
  39.7 1.1 %collective-permute-start.9 = (bf16[48,256]{1,0:T(8,128)(2,1)S(1)}, bf16[48,256]{1,0:T(8,128)(2,1)S(1)}, u32[]{:S(2)}, u32[]{:S(2)}) collective-permute-start(bf16[48,256]{1,0:T(8,128)(2,1)S(1)} %slice.13), channel_id=1, source_target_pairs={{0,16},{1,17},{2,18},{3,19},{4,20},{5,21},{6,22},{7,23},{8,24},{9,... | collective-permute-start | bytes 73736 | tf_op jit(solution)/shard_map/ppermute | solution.py:200
  40.8 3.9 %collective-permute-done.9 = bf16[48,256]{1,0:T(8,128)(2,1)S(1)} collective-permute-done((bf16[48,256]{1,0:T(8,128)(2,1)S(1)}, bf16[48,256]{1,0:T(8,128)(2,1)S(1)}, u32[]{:S(2)}, u32[]{:S(2)}) %collective-permute-start.9) | collective-permute-done | bytes 24608 | tf_op jit(solution)/shard_map/ppermute | solution.py:200
  44.7 0.6 %slice_add_fusion = f32[48,256]{1,0:T(8,128)} fusion(f32[48,512]{1,0:T(8,128)S(1)} %convert_add_fusion.4, bf16[48,256]{1,0:T(8,128)(2,1)S(1)} %collective-permute-done.9), kind=kLoop, calls=%fused_computation.9 | loop fusion | flops 24576 | bytes 122880 | tf_op jit(solution)/shard_map/add | solution.py:263
  (18 shorter events, 0.6 us)
Async XLA Ops:
  0.0 0.8 %copy-start.1 = (f32[3,16,256]{2,1,0:T(8,128)S(1)}, f32[3,16,256]{2,1,0:T(8,128)}, u32[]{:S(2)}) copy-start(f32[3,16,256]{2,1,0:T(8,128)} %force_ref.1) | copy-start | bytes 147460
  0.8 0.7 %copy-start.2 = (f32[3,256]{1,0:T(4,128)S(1)}, f32[3,256]{1,0:T(4,128)}, u32[]{:S(2)}) copy-start(f32[3,256]{1,0:T(4,128)} %pos_ref.1) | copy-start | bytes 9220
  1.5 7.9 %collective-permute-start = (bf16[64,256]{1,0:T(8,128)(2,1)S(1)}, bf16[64,256]{1,0:T(8,128)(2,1)S(1)}, u32[]{:S(2)}, u32[]{:S(2)}) collective-permute-start(bf16[64,256]{1,0:T(8,128)(2,1)S(1)} %pack.1.pack_ref.refs_1_.refs_2_), channel_id=1, source_target_pairs={{0,16},{1,17},{2,18},{3,19},{4,20},{5,21},{6,22},{7,23},{8,24},{9,... | collective-permute-start | bytes 98312 | tf_op jit(solution)/shard_map/ppermute | solution.py:200
  5.6 0.9 %copy-start = (s32[3,8192]{1,0:T(4,128)S(1)}, s32[3,8192]{1,0:T(4,128)}, u32[]{:S(2)}) copy-start(s32[3,8192]{1,0:T(4,128)} %waves_ref.1) | copy-start | bytes 294916
  9.5 1.4 %collective-permute-start.1 = (bf16[2,64,256]{2,1,0:T(8,128)(2,1)S(1)}, bf16[2,64,256]{2,1,0:T(8,128)(2,1)S(1)}, u32[]{:S(2)}, u32[]{:S(2)}) collective-permute-start(bf16[2,64,256]{2,1,0:T(8,128)(2,1)S(1)} %pad_maximum_fusion), channel_id=1, source_target_pairs={{0,1},{1,0},{2,3},{3,2},{4,5},{5,4},{6,7},{7,6},{8,9},{9,8},{10,11... | collective-permute-start | bytes 196616 | tf_op jit(solution)/shard_map/ppermute | solution.py:200
  14.2 7.8 %collective-permute-start.5 = (bf16[64,1024]{1,0:T(8,128)(2,1)S(1)}, bf16[64,1024]{1,0:T(8,128)(2,1)S(1)}, u32[]{:S(2)}, u32[]{:S(2)}) collective-permute-start(bf16[64,1024]{1,0:T(8,128)(2,1)S(1)} %get-tuple-element.29), channel_id=1, source_target_pairs={{0,2},{1,5},{2,0},{3,7},{4,6},{5,1},{6,4},{7,3},{8,10},{9,13},{10,... | collective-permute-start | bytes 393224 | tf_op jit(solution)/shard_map/ppermute | solution.py:237
  20.4 5.9 %collective-permute-start.2 = (bf16[64,1024]{1,0:T(8,128)(2,1)S(1)}, bf16[64,1024]{1,0:T(8,128)(2,1)S(1)}, u32[]{:S(2)}, u32[]{:S(2)}) collective-permute-start(bf16[64,1024]{1,0:T(8,128)(2,1)S(1)} %get-tuple-element.26), channel_id=1, source_target_pairs={{0,8},{1,3},{2,10},{3,1},{4,12},{5,7},{6,14},{7,5},{8,0},{9,11},{1... | collective-permute-start | bytes 393224 | tf_op jit(solution)/shard_map/ppermute | solution.py:237
  22.1 5.0 %collective-permute-start.6 = (bf16[64,1024]{1,0:T(8,128)(2,1)S(1)}, bf16[64,1024]{1,0:T(8,128)(2,1)S(1)}, u32[]{:S(2)}, u32[]{:S(2)}) collective-permute-start(bf16[64,1024]{1,0:T(8,128)(2,1)S(1)} %fusion.1), channel_id=1, source_target_pairs={{0,4},{1,9},{2,6},{3,11},{4,0},{5,13},{6,2},{7,15},{8,12},{9,1},{1... | collective-permute-start | bytes 393224 | tf_op jit(solution)/shard_map/ppermute | solution.py:237
  26.3 6.2 %collective-permute-start.3 = (bf16[64,1024]{1,0:T(8,128)(2,1)S(1)}, bf16[64,1024]{1,0:T(8,128)(2,1)S(1)}, u32[]{:S(2)}, u32[]{:S(2)}) collective-permute-start(bf16[64,1024]{1,0:T(8,128)(2,1)S(1)} %fusion), channel_id=1, source_target_pairs={{0,2},{1,5},{2,0},{3,7},{4,6},{5,1},{6,4},{7,3},{8,10},{9,13},{10,... | collective-permute-start | bytes 393224 | tf_op jit(solution)/shard_map/ppermute | solution.py:237
  27.2 6.1 %collective-permute-start.7 = (bf16[64,1024]{1,0:T(8,128)(2,1)S(1)}, bf16[64,1024]{1,0:T(8,128)(2,1)S(1)}, u32[]{:S(2)}, u32[]{:S(2)}) collective-permute-start(bf16[64,1024]{1,0:T(8,128)(2,1)S(1)} %get-tuple-element.33), channel_id=1, source_target_pairs={{0,8},{1,3},{2,10},{3,1},{4,12},{5,7},{6,14},{7,5},{8,0},{9,11},{1... | collective-permute-start | bytes 393224 | tf_op jit(solution)/shard_map/ppermute | solution.py:237
  32.5 5.0 %collective-permute-start.4 = (bf16[64,1024]{1,0:T(8,128)(2,1)S(1)}, bf16[64,1024]{1,0:T(8,128)(2,1)S(1)}, u32[]{:S(2)}, u32[]{:S(2)}) collective-permute-start(bf16[64,1024]{1,0:T(8,128)(2,1)S(1)} %get-tuple-element.35), channel_id=1, source_target_pairs={{0,4},{1,9},{2,6},{3,11},{4,0},{5,13},{6,2},{7,15},{8,12},{9,1},{1... | collective-permute-start | bytes 393224 | tf_op jit(solution)/shard_map/ppermute | solution.py:237
  38.4 1.3 %collective-permute-start.8 = (bf16[48,512]{1,0:T(8,128)(2,1)S(1)}, bf16[48,512]{1,0:T(8,128)(2,1)S(1)}, u32[]{:S(2)}, u32[]{:S(2)}) collective-permute-start(bf16[48,512]{1,0:T(8,128)(2,1)S(1)} %get-tuple-element.32), channel_id=1, source_target_pairs={{0,1},{1,0},{2,3},{3,2},{4,5},{5,4},{6,7},{7,6},{8,9},{9,8},{10,11... | collective-permute-start | bytes 147464 | tf_op jit(solution)/shard_map/ppermute | solution.py:200
  39.7 5.0 %collective-permute-start.9 = (bf16[48,256]{1,0:T(8,128)(2,1)S(1)}, bf16[48,256]{1,0:T(8,128)(2,1)S(1)}, u32[]{:S(2)}, u32[]{:S(2)}) collective-permute-start(bf16[48,256]{1,0:T(8,128)(2,1)S(1)} %slice.13), channel_id=1, source_target_pairs={{0,16},{1,17},{2,18},{3,19},{4,20},{5,21},{6,22},{7,23},{8,24},{9,... | collective-permute-start | bytes 73736 | tf_op jit(solution)/shard_map/ppermute | solution.py:200

commit v4 on v3

--- a/solution.py
+++ b/solution.py
@@ -16,8 +16,8 @@
 f32, bf16 = jnp.float32, jnp.bfloat16
 
 SIN = (4.442867901617319, -7.307443368323551, 3.594787581869042, -0.7843727161608242)
-COS = (1.414213496635887, -6.9788509910181, 5.739461197516664, -1.8835630614207908, 0.31069820075132315)
 ROUND = 12582912.0
+TINY = 1e-30
 HEAD = 16
 
 
@@ -30,7 +30,7 @@
 
 def call(kernel, out_shape, name, specs, scratch=(), flops=0):
     many = isinstance(out_shape, (list, tuple))
-    spaces = {"v": VMEM, "s": SMEM, "h": pl.ANY}
+    spaces = {"v": VMEM, "s": SMEM, "h": pltpu.HBM}
     return pl.pallas_call(
         kernel,
         out_shape=out_shape,
@@ -51,7 +51,17 @@
     return hi, mid, low
 
 
-def pack_kernel(pos_ref, force_ref, out_ref):
+def pack_kernel(idx_ref, pos_hbm, force_hbm, waves_hbm, out_ref, own_ref, pos_ref, force_ref, sems):
+    first = pl.multiple_of(idx_ref[0] * own_ref.shape[1], 128)
+    copies = [
+        pltpu.make_async_copy(pos_hbm, pos_ref, sems.at[0]),
+        pltpu.make_async_copy(force_hbm, force_ref, sems.at[1]),
+        pltpu.make_async_copy(waves_hbm.at[:, pl.ds(first, own_ref.shape[1])], own_ref, sems.at[2]),
+    ]
+    for copy in copies:
+        copy.start()
+    for copy in copies:
+        copy.wait()
     hi, mid, low = split3(pos_ref[...])
     rows = out_ref.shape[1]
     parts = [hi.astype(f32), mid.astype(f32), low.astype(f32), jnp.zeros((HEAD - 9, rows), f32)]
@@ -61,12 +71,8 @@
         out_ref[HEAD + a * p : HEAD + (a + 1) * p, :] = force_ref[a].astype(bf16)
 
 
-def frame_kernel(amp, idx_ref, waves_ref, frame_ref, wt_ref, own_ref, sem):
+def frame_kernel(amp, own_ref, frame_ref, wt_ref):
     kwaves = own_ref.shape[1]
-    first = pl.multiple_of(idx_ref[0] * kwaves, 128)
-    copy = pltpu.make_async_copy(waves_ref.at[:, pl.ds(first, kwaves)], own_ref, sem)
-    copy.start()
-    copy.wait()
     m = own_ref[...].astype(f32)
     msq = jnp.sum(m * m, axis=0, keepdims=True)
     n = m * lax.rsqrt(msq)
@@ -87,10 +93,11 @@
 def trig(w, phase, tab_ref, rows, cols):
     u = jnp.dot(w, phase, preferred_element_type=f32)
     r = u - ((u + ROUND) - ROUND)
-    q = r * r
-    s = r * horner(SIN, q)
-    tab_ref[0, rows, cols] = (1.0 - s * s).astype(bf16)
-    tab_ref[1, rows, cols] = (s * horner(COS, q)).astype(bf16)
+    s = r * horner(SIN, r * r)
+    square = s * s
+    tab_ref[0, rows, cols] = (1.0 - square).astype(bf16)
+    rest = jnp.maximum(2.0 - square, TINY)
+    tab_ref[1, rows, cols] = (s * (rest * lax.rsqrt(rest))).astype(bf16)
 
 
 def trig_kernel(first, wt_ref, pack_ref, tab_ref):
@@ -202,31 +209,35 @@
     me = lax.axis_index(AXES)
     block = 2 * (me // top) + me % 2
     mine = kwaves // 4
-    part = mine // 2
     fl = 4 * half * rows
     shape = jax.ShapeDtypeStruct
-    own = call(pack_kernel, shape((HEAD + half, rows), bf16), "pack", "vv")(positions, forces)
+    own, owned = call(
+        pack_kernel,
+        (shape((HEAD + half, rows), bf16), shape((3, mine), jnp.int32)),
+        "pack",
+        "shhh",
+        scratch=[VMEM(positions.shape, f32), VMEM(forces.shape, f32), pltpu.SemaphoreType.DMA((3,))],
+    )(block.reshape(1), *(pltpu.with_memory_space_constraint(x, pltpu.HBM) for x in (positions, forces, waves)))
     far = swap(own, top)
     frame, wt = call(
-        functools.partial(frame_kernel, amp),
-        (shape((8, mine), f32), shape((mine, HEAD), bf16)),
-        "frame",
-        "sh",
-        scratch=[VMEM((3, mine), jnp.int32), pltpu.SemaphoreType.DMA],
-        flops=mine * 1000,
-    )(block.reshape(1), waves)
+        functools.partial(frame_kernel, amp), (shape((8, mine), f32), shape((mine, HEAD), bf16)), "frame", "v", flops=mine * 1000
+    )(owned)
     tab_own = call(functools.partial(trig_kernel, 0), shape((2, mine, rows), bf16), "trig_own", "vv", flops=mine * fl)(wt, own)
     both, tab_own, frame, wt = lax.optimization_barrier((jnp.stack([own, far]), tab_own, frame, wt))
     near = swap(both, 1)
-    tab_far = call(functools.partial(trig_kernel, 0), shape((2, part, rows), bf16), "trig_far", "vv", flops=part * fl)(wt, far)
-
-    def sums(first, offsets, ready, packs, todo, width):
+    split = mine * 5 // 8 // 256 * 256
+    parts = (split, mine - split)
+
+    def trig_call(name, first, count, pack):
+        return call(functools.partial(trig_kernel, first), shape((2, count, rows), bf16), name, "vv", flops=count * fl)(wt, pack)
+
+    def sums(first, count, offsets, ready, packs, todo, width):
         return call(
             functools.partial(sums_kernel, first, offsets, 256),
-            (shape((2, part, width), bf16), shape((4 * probes, part), f32), shape((4 * probes, part), bf16)),
+            (shape((2, count, width), bf16), shape((4 * probes, count), f32), shape((4 * probes, count), bf16)),
             "sums",
             "v" * (2 + 2 * len(ready) + len(todo)),
-            flops=part * fl * (width // rows),
+            flops=count * fl * (width // rows),
         )(frame, wt, *ready, *packs, *todo)
 
     middle = [1 << j for j in range(1, bits - 1)]
@@ -236,8 +247,9 @@
         turn = [middle[(j + core + 2 * chunk) % steps] for core in range(2)]
         return lax.ppermute(x, AXES, [(d, d ^ turn[d % 2]) for d in range(devices)])
 
-    tab_a, acc_a, send_a = sums(0, (0, 0), (tab_own, tab_far), (own, far), (near,), 2 * rows)
-    tab_b, acc_b, send_b = sums(part, (part,), (tab_own,), (own,), (far, near), 3 * rows)
+    tab_far = trig_call("trig_far", 0, split, far)
+    tab_a, acc_a, send_a = sums(0, parts[0], (0, 0), (tab_own, tab_far), (own, far), (near,), 2 * rows)
+    tab_b, acc_b, send_b = sums(split, parts[1], (split,), (tab_own,), (own,), (far, near), 3 * rows)
     state = [[acc_a, send_a, None], [acc_b, send_b, None]]
     for j in range(steps):
         for chunk in range(2):
@@ -248,14 +260,14 @@
                 send = acc.astype(bf16)
             state[chunk] = [acc, send, got]
     first = call(
-        functools.partial(back_kernel, 0, (0, 0, 0), 256, False), shape((half, 4 * rows), f32), "back", "vvvvvv", flops=part * fl * 4
+        functools.partial(back_kernel, 0, (0, 0, 0), 256, False), shape((half, 4 * rows), f32), "back", "vvvvvv", flops=parts[0] * fl * 4
     )(state[0][0], state[0][2], frame, tab_own, tab_far, tab_a)
     keep, send = call(
-        functools.partial(back_kernel, part, (part, 0), 256, True),
+        functools.partial(back_kernel, split, (split, 0), 256, True),
         (shape((half, 2 * rows), f32), shape((half, 2 * rows), bf16)),
         "back",
         "vvvvvv",
-        flops=part * fl * 4,
+        flops=parts[1] * fl * 4,
     )(state[1][0], state[1][2], frame, tab_own, tab_b, first)
     there = swap(send, 1)
     keep = keep + there.astype(f32)

time: 45.5 us -> 41.2 us (0.905)
  waiting for transfers between devices: 15.3 us -> 11.5 us
  local copies, waits for them, and re-layouts: 2.39 us -> 0.01 us
  starting transfers between devices: 12.9 us -> 14.9 us
    ppermute x6, waiting for transfers between devices: 10.2 us -> 7.73 us  [exchange(): return lax.ppermute(x, AXES, [(d, d ^ turn[d % 2]) for d in range(devices)])]
    unnamed x6 -> x0, local copies, waits for them, and re-layouts: 2.39 us -> none
    ppermute x4, waiting for transfers between devices: 5.11 us -> 3.8 us  [swap(): return lax.ppermute(x, AXES, [(d, d ^ bit) for d in range(devices)])]
    ppermute x4, starting transfers between devices: 5.34 us -> 6.5 us  [swap(): return lax.ppermute(x, AXES, [(d, d ^ bit) for d in range(devices)])]
    ppermute x6, starting transfers between devices: 7.53 us -> 8.36 us  [exchange(): return lax.ppermute(x, AXES, [(d, d ^ turn[d % 2]) for d in range(devices)])]
  transfers between devices with their start and end apart: 10 -> 10, of which waited for: 6 -> 7; matrix products, arithmetic and copies ran while one was open for 0% -> 0% of each run, Pallas kernels for 21% -> 20%
where the time goes in v4:
time: 41.2 us; the launch traced here: 41 us
  starting transfers between devices  14.9 us (36%)
  Pallas kernels  13.7 us (33%)
  waiting for transfers between devices  11.5 us (28%)
  other arithmetic  0.78 us (2%)
    ppermute x6, starting transfers between devices, exchange(): return lax.ppermute(x, AXES, [(d, d ^ turn[d % 2]) for d in range(devices)])  8.36 us
    ppermute x6, waiting for transfers between devices, exchange(): return lax.ppermute(x, AXES, [(d, d ^ turn[d % 2]) for d in range(devices)])  7.73 us
    pallas_call x2, Pallas kernels, sums(): call(functools.partial(sums_kernel, first, offsets, 256), (shape((2, coun...  7 us
    ppermute x4, starting transfers between devices, swap(): return lax.ppermute(x, AXES, [(d, d ^ bit) for d in range(devices)])  6.5 us
    ppermute x4, waiting for transfers between devices, swap(): return lax.ppermute(x, AXES, [(d, d ^ bit) for d in range(devices)])  3.8 us
    pallas_call x1, Pallas kernels, shards(): call(functools.partial(trig_kernel, 0), shape((2, mine, rows), bf16), 'tr...  2.43 us
    pallas_call x1, Pallas kernels, trig_call(): call(functools.partial(trig_kernel, first), shape((2, count, rows), bf16)...  1.52 us
    pallas_call x1, Pallas kernels, shards(): call(functools.partial(back_kernel, 0, (0, 0, 0), 256, False), shape((hal...  0.99 us
  transfers between devices with their start and end apart: 10, of which 7 were waited for; matrix products, arithmetic and copies ran while one was open for 0% of the time, Pallas kernels for 20%

profile of v4, /device:TPU:0, one launch (start us, length us, event | category | flops | bytes accessed | tf_op | source)
XLA Modules:
  0.0 41.0 jit_solution(6395108069040084475)
XLA Ops:
  0.0 0.9 %pack.1 = (bf16[64,256]{1,0:T(8,128)(2,1)S(1)}, s32[3,2048]{1,0:T(4,128)S(1)}) custom-call(s32[1]{0:T(128)} %bitcast.idx_ref, f32[3,256]{1,0:T(4,128)} %pos_hbm.1, f32[3,16,256]{2,1,0:T(8,128)} %force_hbm.1, s32[3,8192]{1,0:T(4,128)} %waves_hbm.1), custom_call_target="tpu_custom_call" | custom-call | tf_op jit(solution)/shard_map/pack/pallas_call | solution.py:214
  0.9 4.1 %collective-permute-start = (bf16[64,256]{1,0:T(8,128)(2,1)S(1)}, bf16[64,256]{1,0:T(8,128)(2,1)S(1)}, u32[]{:S(2)}, u32[]{:S(2)}) collective-permute-start(bf16[64,256]{1,0:T(8,128)(2,1)S(1)} %get-tuple-element.21.pack_ref.refs_1_.refs_2_), channel_id=1, source_target_pairs={{0,16},{1,17},{2,18},{3,19},{4,20},{5,21},{6,22},{7,23},{8,24},{9,... | collective-permute-start | bytes 98312 | tf_op jit(solution)/shard_map/ppermute | solution.py:207
  5.0 0.2 frame.1
  5.2 2.4 %trig_own.1.refs_0_ = bf16[2,2048,256]{2,1,0:T(8,128)(2,1)S(1)} custom-call(bf16[2048,16]{1,0:T(8,128)(2,1)S(1)} %get-tuple-element.26.wt_ref, bf16[64,256]{1,0:T(8,128)(2,1)S(1)} %get-tuple-element.21.pack_ref.refs_1_.refs_2_), custom_call_target="tpu_custom_call" | custom-call | flops 100663296 | bytes 393216 | tf_op jit(solution)/shard_map/trig_own/pallas_call | solution.py:225
  7.8 1.5 %trig_far.1.refs_1_ = bf16[2,1280,256]{2,1,0:T(8,128)(2,1)S(1)} custom-call(bf16[2048,16]{1,0:T(8,128)(2,1)S(1)} %get-tuple-element.26.wt_ref, bf16[64,256]{1,0:T(8,128)(2,1)S(1)} %collective-permute-done.refs_2_.pack_ref.refs_3_), custom_call_target="tpu_custom_call" | custom-call | flops 62914560 | bytes 245760 | tf_op jit(solution)/shard_map/trig_far/pallas_call | solution.py:232
  9.3 3.8 %sums.3 = (bf16[2,1280,512]{2,1,0:T(8,128)(2,1)S(1)}, f32[64,1280]{1,0:T(8,128)S(1)}, bf16[64,1280]{1,0:T(8,128)(2,1)S(1)}) custom-call(f32[8,2048]{1,0:T(8,128)S(1)} %get-tuple-element.25.frame_ref, bf16[2048,16]{1,0:T(8,128)(2,1)S(1)} %get-tuple-element.26.wt_ref, bf16[2,2048,256]{2,1,0:T(8,128)(2,1)S(1)} %trig_own.1.refs_0_, ...), custom_call_target="tpu_custom_call" | custom-call | flops 125829120 | bytes 491520 | tf_op jit(solution)/shard_map/sums/pallas_call | solution.py:235
  13.2 1.5 %collective-permute-start.5 = (bf16[64,1280]{1,0:T(8,128)(2,1)S(1)}, bf16[64,1280]{1,0:T(8,128)(2,1)S(1)}, u32[]{:S(2)}, u32[]{:S(2)}) collective-permute-start(bf16[64,1280]{1,0:T(8,128)(2,1)S(1)} %get-tuple-element.33), channel_id=1, source_target_pairs={{0,2},{1,5},{2,0},{3,7},{4,6},{5,1},{6,4},{7,3},{8,10},{9,13},{10,... | collective-permute-start | bytes 491528 | tf_op jit(solution)/shard_map/ppermute | solution.py:248
  14.7 3.2 %sums.2 = (bf16[2,768,768]{2,1,0:T(8,128)(2,1)S(1)}, f32[64,768]{1,0:T(8,128)S(1)}, bf16[64,768]{1,0:T(8,128)(2,1)S(1)}) custom-call(f32[8,2048]{1,0:T(8,128)S(1)} %get-tuple-element.25.frame_ref, bf16[2048,16]{1,0:T(8,128)(2,1)S(1)} %get-tuple-element.26.wt_ref, bf16[2,2048,256]{2,1,0:T(8,128)(2,1)S(1)} %trig_own.1.refs_0_, ...), custom_call_target="tpu_custom_call" | custom-call | flops 113246208 | bytes 442368 | tf_op jit(solution)/shard_map/sums/pallas_call | solution.py:235
  17.9 1.7 %collective-permute-start.2 = (bf16[64,768]{1,0:T(8,128)(2,1)S(1)}, bf16[64,768]{1,0:T(8,128)(2,1)S(1)}, u32[]{:S(2)}, u32[]{:S(2)}) collective-permute-start(bf16[64,768]{1,0:T(8,128)(2,1)S(1)} %get-tuple-element.30), channel_id=1, source_target_pairs={{0,8},{1,3},{2,10},{3,1},{4,12},{5,7},{6,14},{7,5},{8,0},{9,11},{1... | collective-permute-start | bytes 294920 | tf_op jit(solution)/shard_map/ppermute | solution.py:248
  19.6 1.6 %collective-permute-start.6 = (bf16[64,1280]{1,0:T(8,128)(2,1)S(1)}, bf16[64,1280]{1,0:T(8,128)(2,1)S(1)}, u32[]{:S(2)}, u32[]{:S(2)}) collective-permute-start(bf16[64,1280]{1,0:T(8,128)(2,1)S(1)} %fusion), channel_id=1, source_target_pairs={{0,4},{1,9},{2,6},{3,11},{4,0},{5,13},{6,2},{7,15},{8,12},{9,1},{1... | collective-permute-start | bytes 491528 | tf_op jit(solution)/shard_map/ppermute | solution.py:248
  21.1 1.9 %collective-permute-done.2 = bf16[64,768]{1,0:T(8,128)(2,1)S(1)} collective-permute-done((bf16[64,768]{1,0:T(8,128)(2,1)S(1)}, bf16[64,768]{1,0:T(8,128)(2,1)S(1)}, u32[]{:S(2)}, u32[]{:S(2)}) %collective-permute-start.2) | collective-permute-done | bytes 98336 | tf_op jit(solution)/shard_map/ppermute | solution.py:248
  23.0 0.6 %collective-permute-start.3 = (bf16[64,768]{1,0:T(8,128)(2,1)S(1)}, bf16[64,768]{1,0:T(8,128)(2,1)S(1)}, u32[]{:S(2)}, u32[]{:S(2)}) collective-permute-start(bf16[64,768]{1,0:T(8,128)(2,1)S(1)} %fusion.1), channel_id=1, source_target_pairs={{0,2},{1,5},{2,0},{3,7},{4,6},{5,1},{6,4},{7,3},{8,10},{9,13},{10,... | collective-permute-start | bytes 294920 | tf_op jit(solution)/shard_map/ppermute | solution.py:248
  23.7 1.6 %collective-permute-done.6 = bf16[64,1280]{1,0:T(8,128)(2,1)S(1)} collective-permute-done((bf16[64,1280]{1,0:T(8,128)(2,1)S(1)}, bf16[64,1280]{1,0:T(8,128)(2,1)S(1)}, u32[]{:S(2)}, u32[]{:S(2)}) %collective-permute-start.6) | collective-permute-done | bytes 163872 | tf_op jit(solution)/shard_map/ppermute | solution.py:248
  25.3 0.3 collective-permute-start.7
  25.6 2.7 %collective-permute-done.3 = bf16[64,768]{1,0:T(8,128)(2,1)S(1)} collective-permute-done((bf16[64,768]{1,0:T(8,128)(2,1)S(1)}, bf16[64,768]{1,0:T(8,128)(2,1)S(1)}, u32[]{:S(2)}, u32[]{:S(2)}) %collective-permute-start.3) | collective-permute-done | bytes 98336 | tf_op jit(solution)/shard_map/ppermute | solution.py:248
  28.3 2.6 %collective-permute-start.4 = (bf16[64,768]{1,0:T(8,128)(2,1)S(1)}, bf16[64,768]{1,0:T(8,128)(2,1)S(1)}, u32[]{:S(2)}, u32[]{:S(2)}) collective-permute-start(bf16[64,768]{1,0:T(8,128)(2,1)S(1)} %get-tuple-element.39), channel_id=1, source_target_pairs={{0,4},{1,9},{2,6},{3,11},{4,0},{5,13},{6,2},{7,15},{8,12},{9,1},{1... | collective-permute-start | bytes 294920 | tf_op jit(solution)/shard_map/ppermute | solution.py:248
  31.0 0.3 collective-permute-done.7.recv_ref
  31.3 1.0 %back.2.refs_2_ = f32[48,1024]{1,0:T(8,128)S(1)} custom-call(f32[64,1280]{1,0:T(8,128)S(1)} %get-tuple-element.38.acc_ref, bf16[64,1280]{1,0:T(8,128)(2,1)S(1)} %collective-permute-done.7.recv_ref, f32[8,2048]{1,0:T(8,128)S(1)} %get-tuple-element.25.frame_ref, bf16[2,2048,256]{2,1,0:T(8,128)(2,1)S(1)} %trig_own.1.refs_0_, ...), custom_call_target="tpu_custom_call" | custom-call | flops 251658240 | bytes 983040 | tf_op jit(solution)/shard_map/back/pallas_call | solution.py:262
  32.3 1.2 %collective-permute-done.4.recv_ref = bf16[64,768]{1,0:T(8,128)(2,1)S(1)} collective-permute-done((bf16[64,768]{1,0:T(8,128)(2,1)S(1)}, bf16[64,768]{1,0:T(8,128)(2,1)S(1)}, u32[]{:S(2)}, u32[]{:S(2)}) %collective-permute-start.4) | collective-permute-done | bytes 98336 | tf_op jit(solution)/shard_map/ppermute | solution.py:248
  33.6 0.6 %back.3 = (f32[48,512]{1,0:T(8,128)S(1)}, bf16[48,512]{1,0:T(8,128)(2,1)S(1)}) custom-call(f32[64,768]{1,0:T(8,128)S(1)} %get-tuple-element.40.acc_ref, bf16[64,768]{1,0:T(8,128)(2,1)S(1)} %collective-permute-done.4.recv_ref, f32[8,2048]{1,0:T(8,128)S(1)} %get-tuple-element.25.frame_ref, bf16[2,2048,256]{2,1,0:T(8,128)(2,1)S(1)} %trig_own.1.refs_0_, ...), custom_call_target="tpu_custom_call" | custom-call | flops 150994944 | bytes 589824 | tf_op jit(solution)/shard_map/back/pallas_call | solution.py:265
  34.3 1.2 %collective-permute-done.8 = bf16[48,512]{1,0:T(8,128)(2,1)S(1)} collective-permute-done((bf16[48,512]{1,0:T(8,128)(2,1)S(1)}, bf16[48,512]{1,0:T(8,128)(2,1)S(1)}, u32[]{:S(2)}, u32[]{:S(2)}) %collective-permute-start.8) | collective-permute-done | bytes 49184 | tf_op jit(solution)/shard_map/ppermute | solution.py:207
  35.6 2.2 %collective-permute-start.9 = (bf16[48,256]{1,0:T(8,128)(2,1)S(1)}, bf16[48,256]{1,0:T(8,128)(2,1)S(1)}, u32[]{:S(2)}, u32[]{:S(2)}) collective-permute-start(bf16[48,256]{1,0:T(8,128)(2,1)S(1)} %slice.13), channel_id=1, source_target_pairs={{0,16},{1,17},{2,18},{3,19},{4,20},{5,21},{6,22},{7,23},{8,24},{9,... | collective-permute-start | bytes 73736 | tf_op jit(solution)/shard_map/ppermute | solution.py:207
  37.8 2.6 %collective-permute-done.9 = bf16[48,256]{1,0:T(8,128)(2,1)S(1)} collective-permute-done((bf16[48,256]{1,0:T(8,128)(2,1)S(1)}, bf16[48,256]{1,0:T(8,128)(2,1)S(1)}, u32[]{:S(2)}, u32[]{:S(2)}) %collective-permute-start.9) | collective-permute-done | bytes 24608 | tf_op jit(solution)/shard_map/ppermute | solution.py:207
  40.4 0.6 %slice_add_fusion = f32[48,256]{1,0:T(8,128)} fusion(f32[48,512]{1,0:T(8,128)S(1)} %convert_add_fusion.4, bf16[48,256]{1,0:T(8,128)(2,1)S(1)} %collective-permute-done.9), kind=kLoop, calls=%fused_computation.9 | loop fusion | flops 24576 | bytes 122880 | tf_op jit(solution)/shard_map/add | solution.py:275
  (12 shorter events, 0.3 us)
Async XLA Ops:
  0.9 6.8 %collective-permute-start = (bf16[64,256]{1,0:T(8,128)(2,1)S(1)}, bf16[64,256]{1,0:T(8,128)(2,1)S(1)}, u32[]{:S(2)}, u32[]{:S(2)}) collective-permute-start(bf16[64,256]{1,0:T(8,128)(2,1)S(1)} %get-tuple-element.21.pack_ref.refs_1_.refs_2_), channel_id=1, source_target_pairs={{0,16},{1,17},{2,18},{3,19},{4,20},{5,21},{6,22},{7,23},{8,24},{9,... | collective-permute-start | bytes 98312 | tf_op jit(solution)/shard_map/ppermute | solution.py:207
  7.7 1.6 %collective-permute-start.1 = (bf16[2,64,256]{2,1,0:T(8,128)(2,1)S(1)}, bf16[2,64,256]{2,1,0:T(8,128)(2,1)S(1)}, u32[]{:S(2)}, u32[]{:S(2)}) collective-permute-start(bf16[2,64,256]{2,1,0:T(8,128)(2,1)S(1)} %pad_maximum_fusion), channel_id=1, source_target_pairs={{0,1},{1,0},{2,3},{3,2},{4,5},{5,4},{6,7},{7,6},{8,9},{9,8},{10,11... | collective-permute-start | bytes 196616 | tf_op jit(solution)/shard_map/ppermute | solution.py:207
  13.2 6.4 %collective-permute-start.5 = (bf16[64,1280]{1,0:T(8,128)(2,1)S(1)}, bf16[64,1280]{1,0:T(8,128)(2,1)S(1)}, u32[]{:S(2)}, u32[]{:S(2)}) collective-permute-start(bf16[64,1280]{1,0:T(8,128)(2,1)S(1)} %get-tuple-element.33), channel_id=1, source_target_pairs={{0,2},{1,5},{2,0},{3,7},{4,6},{5,1},{6,4},{7,3},{8,10},{9,13},{10,... | collective-permute-start | bytes 491528 | tf_op jit(solution)/shard_map/ppermute | solution.py:248
  17.9 5.1 %collective-permute-start.2 = (bf16[64,768]{1,0:T(8,128)(2,1)S(1)}, bf16[64,768]{1,0:T(8,128)(2,1)S(1)}, u32[]{:S(2)}, u32[]{:S(2)}) collective-permute-start(bf16[64,768]{1,0:T(8,128)(2,1)S(1)} %get-tuple-element.30), channel_id=1, source_target_pairs={{0,8},{1,3},{2,10},{3,1},{4,12},{5,7},{6,14},{7,5},{8,0},{9,11},{1... | collective-permute-start | bytes 294920 | tf_op jit(solution)/shard_map/ppermute | solution.py:248
  19.6 5.7 %collective-permute-start.6 = (bf16[64,1280]{1,0:T(8,128)(2,1)S(1)}, bf16[64,1280]{1,0:T(8,128)(2,1)S(1)}, u32[]{:S(2)}, u32[]{:S(2)}) collective-permute-start(bf16[64,1280]{1,0:T(8,128)(2,1)S(1)} %fusion), channel_id=1, source_target_pairs={{0,4},{1,9},{2,6},{3,11},{4,0},{5,13},{6,2},{7,15},{8,12},{9,1},{1... | collective-permute-start | bytes 491528 | tf_op jit(solution)/shard_map/ppermute | solution.py:248
  23.0 5.3 %collective-permute-start.3 = (bf16[64,768]{1,0:T(8,128)(2,1)S(1)}, bf16[64,768]{1,0:T(8,128)(2,1)S(1)}, u32[]{:S(2)}, u32[]{:S(2)}) collective-permute-start(bf16[64,768]{1,0:T(8,128)(2,1)S(1)} %fusion.1), channel_id=1, source_target_pairs={{0,2},{1,5},{2,0},{3,7},{4,6},{5,1},{6,4},{7,3},{8,10},{9,13},{10,... | collective-permute-start | bytes 294920 | tf_op jit(solution)/shard_map/ppermute | solution.py:248
  25.3 6.0 %collective-permute-start.7 = (bf16[64,1280]{1,0:T(8,128)(2,1)S(1)}, bf16[64,1280]{1,0:T(8,128)(2,1)S(1)}, u32[]{:S(2)}, u32[]{:S(2)}) collective-permute-start(bf16[64,1280]{1,0:T(8,128)(2,1)S(1)} %get-tuple-element.37), channel_id=1, source_target_pairs={{0,8},{1,3},{2,10},{3,1},{4,12},{5,7},{6,14},{7,5},{8,0},{9,11},{1... | collective-permute-start | bytes 491528 | tf_op jit(solution)/shard_map/ppermute | solution.py:248
  28.3 5.2 %collective-permute-start.4 = (bf16[64,768]{1,0:T(8,128)(2,1)S(1)}, bf16[64,768]{1,0:T(8,128)(2,1)S(1)}, u32[]{:S(2)}, u32[]{:S(2)}) collective-permute-start(bf16[64,768]{1,0:T(8,128)(2,1)S(1)} %get-tuple-element.39), channel_id=1, source_target_pairs={{0,4},{1,9},{2,6},{3,11},{4,0},{5,13},{6,2},{7,15},{8,12},{9,1},{1... | collective-permute-start | bytes 294920 | tf_op jit(solution)/shard_map/ppermute | solution.py:248
  34.2 1.3 %collective-permute-start.8 = (bf16[48,512]{1,0:T(8,128)(2,1)S(1)}, bf16[48,512]{1,0:T(8,128)(2,1)S(1)}, u32[]{:S(2)}, u32[]{:S(2)}) collective-permute-start(bf16[48,512]{1,0:T(8,128)(2,1)S(1)} %get-tuple-element.36), channel_id=1, source_target_pairs={{0,1},{1,0},{2,3},{3,2},{4,5},{5,4},{6,7},{7,6},{8,9},{9,8},{10,11... | collective-permute-start | bytes 147464 | tf_op jit(solution)/shard_map/ppermute | solution.py:207
  35.6 4.8 %collective-permute-start.9 = (bf16[48,256]{1,0:T(8,128)(2,1)S(1)}, bf16[48,256]{1,0:T(8,128)(2,1)S(1)}, u32[]{:S(2)}, u32[]{:S(2)}) collective-permute-start(bf16[48,256]{1,0:T(8,128)(2,1)S(1)} %slice.13), channel_id=1, source_target_pairs={{0,16},{1,17},{2,18},{3,19},{4,20},{5,21},{6,22},{7,23},{8,24},{9,... | collective-permute-start | bytes 73736 | tf_op jit(solution)/shard_map/ppermute | solution.py:207

commit v5 on v4

--- a/solution.py
+++ b/solution.py
@@ -18,6 +18,7 @@
 SIN = (4.442867901617319, -7.307443368323551, 3.594787581869042, -0.7843727161608242)
 ROUND = 12582912.0
 TINY = 1e-30
+PACE = 2
 HEAD = 16
 
 
@@ -104,12 +105,8 @@
     strip = 64
     phase = pack_ref[:HEAD]
 
-    def step(t, carry):
-        row = pl.multiple_of(t * strip, strip)
-        trig(wt_ref[pl.ds(first + row, strip), :], phase, tab_ref, pl.ds(row, strip), slice(None))
-        return carry
-
-    lax.fori_loop(0, tab_ref.shape[1] // strip, step, 0, unroll=4)
+    for row in range(0, tab_ref.shape[1], strip):
+        trig(wt_ref[first + row : first + row + strip, :], phase, tab_ref, slice(row, row + strip), slice(None))
 
 
 def unpacked(refs):
@@ -130,29 +127,32 @@
     forces = jnp.concatenate([b[HEAD:] for b in blocks], axis=1)
     strip = 32
 
-    def step(c, carry):
-        base = pl.multiple_of(c * chunk, chunk)
-        for t in range(chunk // strip):
-            row = pl.multiple_of(base + t * strip, strip)
-            w = wt_ref[pl.ds(first + row, strip), :]
+    sources = list(zip(ready, offsets, [pack[HEAD:] for pack in packs])) + [(tab_ref, 0, forces)]
+
+    def sum_up(base, part):
+        sums = 0.0
+        for table, offset, force in sources:
+            t = table[part, offset + base : offset + base + chunk, :]
+            sums += lax.dot_general(force, t, (((1,), (1,)), ((), ())), preferred_element_type=f32)
+        cols = slice(base, base + chunk)
+        fr = frame_ref[:, first + base : first + base + chunk]
+        for j in range(2):
+            value = sum(fr[3 * j + x : 3 * j + x + 1] * sums[x * probes : (x + 1) * probes] for x in range(3))
+            low = (2 * part + j) * probes
+            acc_ref[low : low + probes, cols] = value
+            send_ref[low : low + probes, cols] = value.astype(bf16)
+
+    waiting = []
+    for base in range(0, kwaves, chunk):
+        for row in range(base, base + chunk, strip):
+            w = wt_ref[first + row : first + row + strip, :]
             for j, block in enumerate(blocks):
-                trig(w, block[:HEAD], tab_ref, pl.ds(row, strip), slice(j * width, (j + 1) * width))
-        fr = frame_ref[:, pl.ds(first + base, chunk)]
-        for part in range(2):
-            sums = jnp.zeros((3 * probes, chunk), f32)
-            for offset, table, pack in zip(offsets, ready, packs):
-                t = table[part, pl.ds(offset + base, chunk), :]
-                sums += lax.dot_general(pack[HEAD:], t, (((1,), (1,)), ((), ())), preferred_element_type=f32)
-            t = tab_ref[part, pl.ds(base, chunk), :]
-            sums += lax.dot_general(forces, t, (((1,), (1,)), ((), ())), preferred_element_type=f32)
-            for j in range(2):
-                value = sum(fr[3 * j + x : 3 * j + x + 1] * sums[x * probes : (x + 1) * probes] for x in range(3))
-                low = (2 * part + j) * probes
-                acc_ref[low : low + probes, pl.ds(base, chunk)] = value
-                send_ref[low : low + probes, pl.ds(base, chunk)] = value.astype(bf16)
-        return carry
-
-    lax.fori_loop(0, kwaves // chunk, step, 0)
+                trig(w, block[:HEAD], tab_ref, slice(row, row + strip), slice(j * width, (j + 1) * width))
+            if waiting and (row - base) // strip % PACE == 0:
+                sum_up(*waiting.pop(0))
+        waiting.extend((base, part) for part in range(2))
+    for late in waiting:
+        sum_up(*late)
 
 
 def back_kernel(first, offsets, chunk, last, acc_ref, recv_ref, frame_ref, *refs):

time: 41.2 us -> 38.5 us (0.934)
  Pallas kernels: 13.7 us -> 9.95 us
  starting transfers between devices: 14.9 us -> 15.6 us
    pallas_call x2, Pallas kernels: 7 us -> 4.85 us  [sums(): call(functools.partial(sums_kernel, first, offsets, 256), (shape((2, coun...]
    pallas_call x1, Pallas kernels: 2.43 us -> 1.42 us  [shards(): call(functools.partial(trig_kernel, 0), shape((2, mine, rows), bf16), 'tr...]
    ppermute x4, waiting for transfers between devices: 3.8 us -> 4.45 us  [swap(): return lax.ppermute(x, AXES, [(d, d ^ bit) for d in range(devices)])]
    pallas_call x1, Pallas kernels: 1.52 us -> 0.95 us  [trig_call(): call(functools.partial(trig_kernel, first), shape((2, count, rows), bf16)...]
    ppermute x6, starting transfers between devices: 8.36 us -> 8.9 us  [exchange(): return lax.ppermute(x, AXES, [(d, d ^ turn[d % 2]) for d in range(devices)])]
  transfers between devices with their start and end apart: 10 -> 10, of which waited for: 7 -> 9; matrix products, arithmetic and copies ran while one was open for 0% -> 0% of each run, Pallas kernels for 20% -> 15%
where the time goes in v5:
time: 38.5 us; the launch traced here: 38.3 us
  starting transfers between devices  15.6 us (41%)
  waiting for transfers between devices  11.9 us (31%)
  Pallas kernels  9.95 us (26%)
  other arithmetic  0.78 us (2%)
    ppermute x6, starting transfers between devices, exchange(): return lax.ppermute(x, AXES, [(d, d ^ turn[d % 2]) for d in range(devices)])  8.9 us
    ppermute x6, waiting for transfers between devices, exchange(): return lax.ppermute(x, AXES, [(d, d ^ turn[d % 2]) for d in range(devices)])  7.42 us
    ppermute x4, starting transfers between devices, swap(): return lax.ppermute(x, AXES, [(d, d ^ bit) for d in range(devices)])  6.7 us
    pallas_call x2, Pallas kernels, sums(): call(functools.partial(sums_kernel, first, offsets, 256), (shape((2, coun...  4.85 us
    ppermute x4, waiting for transfers between devices, swap(): return lax.ppermute(x, AXES, [(d, d ^ bit) for d in range(devices)])  4.45 us
    pallas_call x1, Pallas kernels, shards(): call(functools.partial(trig_kernel, 0), shape((2, mine, rows), bf16), 'tr...  1.42 us
    pallas_call x1, Pallas kernels, shards(): call(functools.partial(back_kernel, 0, (0, 0, 0), 256, False), shape((hal...  0.99 us
    pallas_call x1, Pallas kernels, trig_call(): call(functools.partial(trig_kernel, first), shape((2, count, rows), bf16)...  0.95 us
  transfers between devices with their start and end apart: 10, of which 9 were waited for; matrix products, arithmetic and copies ran while one was open for 0% of the time, Pallas kernels for 15%

profile of v5, /device:TPU:0, one launch (start us, length us, event | category | flops | bytes accessed | tf_op | source)
XLA Modules:
  0.0 38.3 jit_solution(13121898709608707868)
XLA Ops:
  0.0 0.9 %pack.1 = (bf16[64,256]{1,0:T(8,128)(2,1)S(1)}, s32[3,2048]{1,0:T(4,128)S(1)}) custom-call(s32[1]{0:T(128)} %bitcast.idx_ref, f32[3,256]{1,0:T(4,128)} %pos_hbm.1, f32[3,16,256]{2,1,0:T(8,128)} %force_hbm.1, s32[3,8192]{1,0:T(4,128)} %waves_hbm.1), custom_call_target="tpu_custom_call" | custom-call | tf_op jit(solution)/shard_map/pack/pallas_call | solution.py:214
  0.9 4.1 %collective-permute-start = (bf16[64,256]{1,0:T(8,128)(2,1)S(1)}, bf16[64,256]{1,0:T(8,128)(2,1)S(1)}, u32[]{:S(2)}, u32[]{:S(2)}) collective-permute-start(bf16[64,256]{1,0:T(8,128)(2,1)S(1)} %get-tuple-element.21.pack_ref.refs_1_.refs_2_), channel_id=1, source_target_pairs={{0,16},{1,17},{2,18},{3,19},{4,20},{5,21},{6,22},{7,23},{8,24},{9,... | collective-permute-start | bytes 98312 | tf_op jit(solution)/shard_map/ppermute | solution.py:207
  5.0 0.2 frame.1
  5.2 1.4 %trig_own.1.refs_0_ = bf16[2,2048,256]{2,1,0:T(8,128)(2,1)S(1)} custom-call(bf16[2048,16]{1,0:T(8,128)(2,1)S(1)} %get-tuple-element.26.wt_ref, bf16[64,256]{1,0:T(8,128)(2,1)S(1)} %get-tuple-element.21.pack_ref.refs_1_.refs_2_), custom_call_target="tpu_custom_call" | custom-call | flops 100663296 | bytes 393216 | tf_op jit(solution)/shard_map/trig_own/pallas_call | solution.py:225
  6.7 0.6 %collective-permute-done.refs_2_.pack_ref.refs_3_ = bf16[64,256]{1,0:T(8,128)(2,1)S(1)} collective-permute-done((bf16[64,256]{1,0:T(8,128)(2,1)S(1)}, bf16[64,256]{1,0:T(8,128)(2,1)S(1)}, u32[]{:S(2)}, u32[]{:S(2)}) %collective-permute-start) | collective-permute-done | bytes 32800 | tf_op jit(solution)/shard_map/ppermute | solution.py:207
  7.3 0.9 %trig_far.1.refs_1_ = bf16[2,1280,256]{2,1,0:T(8,128)(2,1)S(1)} custom-call(bf16[2048,16]{1,0:T(8,128)(2,1)S(1)} %get-tuple-element.26.wt_ref, bf16[64,256]{1,0:T(8,128)(2,1)S(1)} %collective-permute-done.refs_2_.pack_ref.refs_3_), custom_call_target="tpu_custom_call" | custom-call | flops 62914560 | bytes 245760 | tf_op jit(solution)/shard_map/trig_far/pallas_call | solution.py:232
  8.3 0.3 collective-permute-done.1.refs_3_.refs_4_
  8.6 2.6 %sums.3 = (bf16[2,1280,512]{2,1,0:T(8,128)(2,1)S(1)}, f32[64,1280]{1,0:T(8,128)S(1)}, bf16[64,1280]{1,0:T(8,128)(2,1)S(1)}) custom-call(f32[8,2048]{1,0:T(8,128)S(1)} %get-tuple-element.25.frame_ref, bf16[2048,16]{1,0:T(8,128)(2,1)S(1)} %get-tuple-element.26.wt_ref, bf16[2,2048,256]{2,1,0:T(8,128)(2,1)S(1)} %trig_own.1.refs_0_, ...), custom_call_target="tpu_custom_call" | custom-call | flops 125829120 | bytes 491520 | tf_op jit(solution)/shard_map/sums/pallas_call | solution.py:235
  11.2 1.8 %collective-permute-start.5 = (bf16[64,1280]{1,0:T(8,128)(2,1)S(1)}, bf16[64,1280]{1,0:T(8,128)(2,1)S(1)}, u32[]{:S(2)}, u32[]{:S(2)}) collective-permute-start(bf16[64,1280]{1,0:T(8,128)(2,1)S(1)} %get-tuple-element.33), channel_id=1, source_target_pairs={{0,2},{1,5},{2,0},{3,7},{4,6},{5,1},{6,4},{7,3},{8,10},{9,13},{10,... | collective-permute-start | bytes 491528 | tf_op jit(solution)/shard_map/ppermute | solution.py:248
  12.9 2.3 %sums.2 = (bf16[2,768,768]{2,1,0:T(8,128)(2,1)S(1)}, f32[64,768]{1,0:T(8,128)S(1)}, bf16[64,768]{1,0:T(8,128)(2,1)S(1)}) custom-call(f32[8,2048]{1,0:T(8,128)S(1)} %get-tuple-element.25.frame_ref, bf16[2048,16]{1,0:T(8,128)(2,1)S(1)} %get-tuple-element.26.wt_ref, bf16[2,2048,256]{2,1,0:T(8,128)(2,1)S(1)} %trig_own.1.refs_0_, ...), custom_call_target="tpu_custom_call" | custom-call | flops 113246208 | bytes 442368 | tf_op jit(solution)/shard_map/sums/pallas_call | solution.py:235
  15.2 1.4 %collective-permute-start.2 = (bf16[64,768]{1,0:T(8,128)(2,1)S(1)}, bf16[64,768]{1,0:T(8,128)(2,1)S(1)}, u32[]{:S(2)}, u32[]{:S(2)}) collective-permute-start(bf16[64,768]{1,0:T(8,128)(2,1)S(1)} %get-tuple-element.30), channel_id=1, source_target_pairs={{0,8},{1,3},{2,10},{3,1},{4,12},{5,7},{6,14},{7,5},{8,0},{9,11},{1... | collective-permute-start | bytes 294920 | tf_op jit(solution)/shard_map/ppermute | solution.py:248
  16.7 1.9 %collective-permute-start.6 = (bf16[64,1280]{1,0:T(8,128)(2,1)S(1)}, bf16[64,1280]{1,0:T(8,128)(2,1)S(1)}, u32[]{:S(2)}, u32[]{:S(2)}) collective-permute-start(bf16[64,1280]{1,0:T(8,128)(2,1)S(1)} %fusion), channel_id=1, source_target_pairs={{0,4},{1,9},{2,6},{3,11},{4,0},{5,13},{6,2},{7,15},{8,12},{9,1},{1... | collective-permute-start | bytes 491528 | tf_op jit(solution)/shard_map/ppermute | solution.py:248
  18.5 2.1 %collective-permute-done.2 = bf16[64,768]{1,0:T(8,128)(2,1)S(1)} collective-permute-done((bf16[64,768]{1,0:T(8,128)(2,1)S(1)}, bf16[64,768]{1,0:T(8,128)(2,1)S(1)}, u32[]{:S(2)}, u32[]{:S(2)}) %collective-permute-start.2) | collective-permute-done | bytes 98336 | tf_op jit(solution)/shard_map/ppermute | solution.py:248
  20.7 1.7 %collective-permute-done.6 = bf16[64,1280]{1,0:T(8,128)(2,1)S(1)} collective-permute-done((bf16[64,1280]{1,0:T(8,128)(2,1)S(1)}, bf16[64,1280]{1,0:T(8,128)(2,1)S(1)}, u32[]{:S(2)}, u32[]{:S(2)}) %collective-permute-start.6) | collective-permute-done | bytes 163872 | tf_op jit(solution)/shard_map/ppermute | solution.py:248
  22.4 1.7 %collective-permute-start.7 = (bf16[64,1280]{1,0:T(8,128)(2,1)S(1)}, bf16[64,1280]{1,0:T(8,128)(2,1)S(1)}, u32[]{:S(2)}, u32[]{:S(2)}) collective-permute-start(bf16[64,1280]{1,0:T(8,128)(2,1)S(1)} %get-tuple-element.37), channel_id=1, source_target_pairs={{0,8},{1,3},{2,10},{3,1},{4,12},{5,7},{6,14},{7,5},{8,0},{9,11},{1... | collective-permute-start | bytes 491528 | tf_op jit(solution)/shard_map/ppermute | solution.py:248
  24.1 2.0 %collective-permute-done.3 = bf16[64,768]{1,0:T(8,128)(2,1)S(1)} collective-permute-done((bf16[64,768]{1,0:T(8,128)(2,1)S(1)}, bf16[64,768]{1,0:T(8,128)(2,1)S(1)}, u32[]{:S(2)}, u32[]{:S(2)}) %collective-permute-start.3) | collective-permute-done | bytes 98336 | tf_op jit(solution)/shard_map/ppermute | solution.py:248
  26.2 2.1 %collective-permute-start.4 = (bf16[64,768]{1,0:T(8,128)(2,1)S(1)}, bf16[64,768]{1,0:T(8,128)(2,1)S(1)}, u32[]{:S(2)}, u32[]{:S(2)}) collective-permute-start(bf16[64,768]{1,0:T(8,128)(2,1)S(1)} %get-tuple-element.39), channel_id=1, source_target_pairs={{0,4},{1,9},{2,6},{3,11},{4,0},{5,13},{6,2},{7,15},{8,12},{9,1},{1... | collective-permute-start | bytes 294920 | tf_op jit(solution)/shard_map/ppermute | solution.py:248
  28.4 1.0 %back.2.refs_2_ = f32[48,1024]{1,0:T(8,128)S(1)} custom-call(f32[64,1280]{1,0:T(8,128)S(1)} %get-tuple-element.38.acc_ref, bf16[64,1280]{1,0:T(8,128)(2,1)S(1)} %collective-permute-done.7.recv_ref, f32[8,2048]{1,0:T(8,128)S(1)} %get-tuple-element.25.frame_ref, bf16[2,2048,256]{2,1,0:T(8,128)(2,1)S(1)} %trig_own.1.refs_0_, ...), custom_call_target="tpu_custom_call" | custom-call | flops 251658240 | bytes 983040 | tf_op jit(solution)/shard_map/back/pallas_call | solution.py:262
  29.4 1.5 %collective-permute-done.4.recv_ref = bf16[64,768]{1,0:T(8,128)(2,1)S(1)} collective-permute-done((bf16[64,768]{1,0:T(8,128)(2,1)S(1)}, bf16[64,768]{1,0:T(8,128)(2,1)S(1)}, u32[]{:S(2)}, u32[]{:S(2)}) %collective-permute-start.4) | collective-permute-done | bytes 98336 | tf_op jit(solution)/shard_map/ppermute | solution.py:248
  30.9 0.6 %back.3 = (f32[48,512]{1,0:T(8,128)S(1)}, bf16[48,512]{1,0:T(8,128)(2,1)S(1)}) custom-call(f32[64,768]{1,0:T(8,128)S(1)} %get-tuple-element.40.acc_ref, bf16[64,768]{1,0:T(8,128)(2,1)S(1)} %collective-permute-done.4.recv_ref, f32[8,2048]{1,0:T(8,128)S(1)} %get-tuple-element.25.frame_ref, bf16[2,2048,256]{2,1,0:T(8,128)(2,1)S(1)} %trig_own.1.refs_0_, ...), custom_call_target="tpu_custom_call" | custom-call | flops 150994944 | bytes 589824 | tf_op jit(solution)/shard_map/back/pallas_call | solution.py:265
  31.6 1.2 %collective-permute-done.8 = bf16[48,512]{1,0:T(8,128)(2,1)S(1)} collective-permute-done((bf16[48,512]{1,0:T(8,128)(2,1)S(1)}, bf16[48,512]{1,0:T(8,128)(2,1)S(1)}, u32[]{:S(2)}, u32[]{:S(2)}) %collective-permute-start.8) | collective-permute-done | bytes 49184 | tf_op jit(solution)/shard_map/ppermute | solution.py:207
  32.9 2.4 %collective-permute-start.9 = (bf16[48,256]{1,0:T(8,128)(2,1)S(1)}, bf16[48,256]{1,0:T(8,128)(2,1)S(1)}, u32[]{:S(2)}, u32[]{:S(2)}) collective-permute-start(bf16[48,256]{1,0:T(8,128)(2,1)S(1)} %slice.13), channel_id=1, source_target_pairs={{0,16},{1,17},{2,18},{3,19},{4,20},{5,21},{6,22},{7,23},{8,24},{9,... | collective-permute-start | bytes 73736 | tf_op jit(solution)/shard_map/ppermute | solution.py:207
  35.3 2.4 %collective-permute-done.9 = bf16[48,256]{1,0:T(8,128)(2,1)S(1)} collective-permute-done((bf16[48,256]{1,0:T(8,128)(2,1)S(1)}, bf16[48,256]{1,0:T(8,128)(2,1)S(1)}, u32[]{:S(2)}, u32[]{:S(2)}) %collective-permute-start.9) | collective-permute-done | bytes 24608 | tf_op jit(solution)/shard_map/ppermute | solution.py:207
  37.7 0.6 %slice_add_fusion = f32[48,256]{1,0:T(8,128)} fusion(f32[48,512]{1,0:T(8,128)S(1)} %convert_add_fusion.4, bf16[48,256]{1,0:T(8,128)(2,1)S(1)} %collective-permute-done.9), kind=kLoop, calls=%fused_computation.9 | loop fusion | flops 24576 | bytes 122880 | tf_op jit(solution)/shard_map/add | solution.py:275
  (12 shorter events, 0.5 us)
Async XLA Ops:
  0.9 6.4 %collective-permute-start = (bf16[64,256]{1,0:T(8,128)(2,1)S(1)}, bf16[64,256]{1,0:T(8,128)(2,1)S(1)}, u32[]{:S(2)}, u32[]{:S(2)}) collective-permute-start(bf16[64,256]{1,0:T(8,128)(2,1)S(1)} %get-tuple-element.21.pack_ref.refs_1_.refs_2_), channel_id=1, source_target_pairs={{0,16},{1,17},{2,18},{3,19},{4,20},{5,21},{6,22},{7,23},{8,24},{9,... | collective-permute-start | bytes 98312 | tf_op jit(solution)/shard_map/ppermute | solution.py:207
  7.3 1.3 %collective-permute-start.1 = (bf16[2,64,256]{2,1,0:T(8,128)(2,1)S(1)}, bf16[2,64,256]{2,1,0:T(8,128)(2,1)S(1)}, u32[]{:S(2)}, u32[]{:S(2)}) collective-permute-start(bf16[2,64,256]{2,1,0:T(8,128)(2,1)S(1)} %pad_maximum_fusion), channel_id=1, source_target_pairs={{0,1},{1,0},{2,3},{3,2},{4,5},{5,4},{6,7},{7,6},{8,9},{9,8},{10,11... | collective-permute-start | bytes 196616 | tf_op jit(solution)/shard_map/ppermute | solution.py:207
  11.2 5.5 %collective-permute-start.5 = (bf16[64,1280]{1,0:T(8,128)(2,1)S(1)}, bf16[64,1280]{1,0:T(8,128)(2,1)S(1)}, u32[]{:S(2)}, u32[]{:S(2)}) collective-permute-start(bf16[64,1280]{1,0:T(8,128)(2,1)S(1)} %get-tuple-element.33), channel_id=1, source_target_pairs={{0,2},{1,5},{2,0},{3,7},{4,6},{5,1},{6,4},{7,3},{8,10},{9,13},{10,... | collective-permute-start | bytes 491528 | tf_op jit(solution)/shard_map/ppermute | solution.py:248
  15.2 5.4 %collective-permute-start.2 = (bf16[64,768]{1,0:T(8,128)(2,1)S(1)}, bf16[64,768]{1,0:T(8,128)(2,1)S(1)}, u32[]{:S(2)}, u32[]{:S(2)}) collective-permute-start(bf16[64,768]{1,0:T(8,128)(2,1)S(1)} %get-tuple-element.30), channel_id=1, source_target_pairs={{0,8},{1,3},{2,10},{3,1},{4,12},{5,7},{6,14},{7,5},{8,0},{9,11},{1... | collective-permute-start | bytes 294920 | tf_op jit(solution)/shard_map/ppermute | solution.py:248
  16.7 5.7 %collective-permute-start.6 = (bf16[64,1280]{1,0:T(8,128)(2,1)S(1)}, bf16[64,1280]{1,0:T(8,128)(2,1)S(1)}, u32[]{:S(2)}, u32[]{:S(2)}) collective-permute-start(bf16[64,1280]{1,0:T(8,128)(2,1)S(1)} %fusion), channel_id=1, source_target_pairs={{0,4},{1,9},{2,6},{3,11},{4,0},{5,13},{6,2},{7,15},{8,12},{9,1},{1... | collective-permute-start | bytes 491528 | tf_op jit(solution)/shard_map/ppermute | solution.py:248
  20.6 5.5 %collective-permute-start.3 = (bf16[64,768]{1,0:T(8,128)(2,1)S(1)}, bf16[64,768]{1,0:T(8,128)(2,1)S(1)}, u32[]{:S(2)}, u32[]{:S(2)}) collective-permute-start(bf16[64,768]{1,0:T(8,128)(2,1)S(1)} %fusion.1), channel_id=1, source_target_pairs={{0,2},{1,5},{2,0},{3,7},{4,6},{5,1},{6,4},{7,3},{8,10},{9,13},{10,... | collective-permute-start | bytes 294920 | tf_op jit(solution)/shard_map/ppermute | solution.py:248
  22.4 6.0 %collective-permute-start.7 = (bf16[64,1280]{1,0:T(8,128)(2,1)S(1)}, bf16[64,1280]{1,0:T(8,128)(2,1)S(1)}, u32[]{:S(2)}, u32[]{:S(2)}) collective-permute-start(bf16[64,1280]{1,0:T(8,128)(2,1)S(1)} %get-tuple-element.37), channel_id=1, source_target_pairs={{0,8},{1,3},{2,10},{3,1},{4,12},{5,7},{6,14},{7,5},{8,0},{9,11},{1... | collective-permute-start | bytes 491528 | tf_op jit(solution)/shard_map/ppermute | solution.py:248
  26.2 4.7 %collective-permute-start.4 = (bf16[64,768]{1,0:T(8,128)(2,1)S(1)}, bf16[64,768]{1,0:T(8,128)(2,1)S(1)}, u32[]{:S(2)}, u32[]{:S(2)}) collective-permute-start(bf16[64,768]{1,0:T(8,128)(2,1)S(1)} %get-tuple-element.39), channel_id=1, source_target_pairs={{0,4},{1,9},{2,6},{3,11},{4,0},{5,13},{6,2},{7,15},{8,12},{9,1},{1... | collective-permute-start | bytes 294920 | tf_op jit(solution)/shard_map/ppermute | solution.py:248
  31.6 1.3 %collective-permute-start.8 = (bf16[48,512]{1,0:T(8,128)(2,1)S(1)}, bf16[48,512]{1,0:T(8,128)(2,1)S(1)}, u32[]{:S(2)}, u32[]{:S(2)}) collective-permute-start(bf16[48,512]{1,0:T(8,128)(2,1)S(1)} %get-tuple-element.36), channel_id=1, source_target_pairs={{0,1},{1,0},{2,3},{3,2},{4,5},{5,4},{6,7},{7,6},{8,9},{9,8},{10,11... | collective-permute-start | bytes 147464 | tf_op jit(solution)/shard_map/ppermute | solution.py:207
  32.9 4.8 %collective-permute-start.9 = (bf16[48,256]{1,0:T(8,128)(2,1)S(1)}, bf16[48,256]{1,0:T(8,128)(2,1)S(1)}, u32[]{:S(2)}, u32[]{:S(2)}) collective-permute-start(bf16[48,256]{1,0:T(8,128)(2,1)S(1)} %slice.13), channel_id=1, source_target_pairs={{0,16},{1,17},{2,18},{3,19},{4,20},{5,21},{6,22},{7,23},{8,24},{9,... | collective-permute-start | bytes 73736 | tf_op jit(solution)/shard_map/ppermute | solution.py:207

commit v6 on v5

--- a/solution.py
+++ b/solution.py
@@ -101,12 +101,31 @@
     tab_ref[1, rows, cols] = (s * (rest * lax.rsqrt(rest))).astype(bf16)
 
 
-def trig_kernel(first, wt_ref, pack_ref, tab_ref):
+def product(force, table):
+    return lax.dot_general(force, table, (((1,), (1,)), ((), ())), preferred_element_type=f32)
+
+
+def trig_kernel(first, chunk, wt_ref, pack_ref, *refs):
+    earlier, tab_ref, raw_ref = refs if len(refs) == 3 else (None, *refs)
+    half = pack_ref.shape[0] - HEAD
     strip = 64
-    phase = pack_ref[:HEAD]
-
-    for row in range(0, tab_ref.shape[1], strip):
-        trig(wt_ref[first + row : first + row + strip, :], phase, tab_ref, slice(row, row + strip), slice(None))
+    phase, force = pack_ref[:HEAD], pack_ref[HEAD:]
+    count = tab_ref.shape[1]
+
+    def sum_up(base, part):
+        rows, cols = slice(part * half, (part + 1) * half), slice(base, base + chunk)
+        sums = product(force, tab_ref[part, cols, :])
+        raw_ref[rows, cols] = sums if earlier is None else sums + earlier[rows, cols]
+
+    waiting = []
+    for base in range(0, count, chunk):
+        for row in range(base, base + chunk, strip):
+            trig(wt_ref[first + row : first + row + strip, :], phase, tab_ref, slice(row, row + strip), slice(None))
+            if waiting and (row - base) // strip % 2 == 0:
+                sum_up(*waiting.pop(0))
+        waiting.extend((base, part) for part in range(2))
+    for late in waiting:
+        sum_up(*late)
 
 
 def unpacked(refs):
@@ -116,25 +135,20 @@
     return blocks
 
 
-def sums_kernel(first, offsets, chunk, frame_ref, wt_ref, *refs):
-    count = len(offsets)
-    ready, packs, todo = refs[:count], refs[count : 2 * count], refs[2 * count : -3]
+def sums_kernel(first, start, chunk, frame_ref, wt_ref, raw_ref, *refs):
+    todo = refs[:-3]
     tab_ref, acc_ref, send_ref = refs[-3:]
     kwaves = tab_ref.shape[1]
     probes = acc_ref.shape[0] // 4
+    half = 3 * probes
     blocks = unpacked(todo)
     width = blocks[0].shape[1]
     forces = jnp.concatenate([b[HEAD:] for b in blocks], axis=1)
     strip = 32
 
-    sources = list(zip(ready, offsets, [pack[HEAD:] for pack in packs])) + [(tab_ref, 0, forces)]
-
     def sum_up(base, part):
-        sums = 0.0
-        for table, offset, force in sources:
-            t = table[part, offset + base : offset + base + chunk, :]
-            sums += lax.dot_general(force, t, (((1,), (1,)), ((), ())), preferred_element_type=f32)
         cols = slice(base, base + chunk)
+        sums = product(forces, tab_ref[part, cols, :]) + raw_ref[part * half : (part + 1) * half, start + base : start + base + chunk]
         fr = frame_ref[:, first + base : first + base + chunk]
         for j in range(2):
             value = sum(fr[3 * j + x : 3 * j + x + 1] * sums[x * probes : (x + 1) * probes] for x in range(3))
@@ -222,23 +236,30 @@
     frame, wt = call(
         functools.partial(frame_kernel, amp), (shape((8, mine), f32), shape((mine, HEAD), bf16)), "frame", "v", flops=mine * 1000
     )(owned)
-    tab_own = call(functools.partial(trig_kernel, 0), shape((2, mine, rows), bf16), "trig_own", "vv", flops=mine * fl)(wt, own)
-    both, tab_own, frame, wt = lax.optimization_barrier((jnp.stack([own, far]), tab_own, frame, wt))
+
+    def trig_call(name, first, count, *operands):
+        return call(
+            functools.partial(trig_kernel, first, 256),
+            (shape((2, count, rows), bf16), shape((2 * half, count), f32)),
+            name,
+            "v" * (1 + len(operands)),
+            flops=count * fl,
+        )(wt, *operands)
+
+    tab_own, raw = trig_call("trig_own", 0, mine, own)
+    both, tab_own, raw, frame, wt = lax.optimization_barrier((jnp.stack([own, far]), tab_own, raw, frame, wt))
     near = swap(both, 1)
     split = mine * 5 // 8 // 256 * 256
     parts = (split, mine - split)
 
-    def trig_call(name, first, count, pack):
-        return call(functools.partial(trig_kernel, first), shape((2, count, rows), bf16), name, "vv", flops=count * fl)(wt, pack)
-
-    def sums(first, count, offsets, ready, packs, todo, width):
+    def sums(first, count, start, raw, todo, width):
         return call(
-            functools.partial(sums_kernel, first, offsets, 256),
+            functools.partial(sums_kernel, first, start, 256),
             (shape((2, count, width), bf16), shape((4 * probes, count), f32), shape((4 * probes, count), bf16)),
             "sums",
-            "v" * (2 + 2 * len(ready) + len(todo)),
+            "v" * (3 + len(todo)),
             flops=count * fl * (width // rows),
-        )(frame, wt, *ready, *packs, *todo)
+        )(frame, wt, raw, *todo)
 
     middle = [1 << j for j in range(1, bits - 1)]
     steps = len(middle)
@@ -247,9 +268,9 @@
         turn = [middle[(j + core + 2 * chunk) % steps] for core in range(2)]
         return lax.ppermute(x, AXES, [(d, d ^ turn[d % 2]) for d in range(devices)])
 
-    tab_far = trig_call("trig_far", 0, split, far)
-    tab_a, acc_a, send_a = sums(0, parts[0], (0, 0), (tab_own, tab_far), (own, far), (near,), 2 * rows)
-    tab_b, acc_b, send_b = sums(split, parts[1], (split,), (tab_own,), (own,), (far, near), 3 * rows)
+    tab_far, raw_a = trig_call("trig_far", 0, split, far, raw)
+    tab_a, acc_a, send_a = sums(0, parts[0], 0, raw_a, (near,), 2 * rows)
+    tab_b, acc_b, send_b = sums(split, parts[1], split, raw, (far, near), 3 * rows)
     state = [[acc_a, send_a, None], [acc_b, send_b, None]]
     for j in range(steps):
         for chunk in range(2):

time: 38.5 us -> 37.7 us (0.979)
  waiting for transfers between devices: 11.9 us -> 11.2 us
  starting transfers between devices: 15.6 us -> 15.2 us
    ppermute x4, waiting for transfers between devices: 4.45 us -> 4.06 us  [swap(): return lax.ppermute(x, AXES, [(d, d ^ bit) for d in range(devices)])]
  transfers between devices with their start and end apart: 10 -> 10, of which waited for: 9 -> 9; matrix products, arithmetic and copies ran while one was open for 0% -> 0% of each run, Pallas kernels for 15% -> 17%
where the time goes in v6:
time: 37.7 us; the launch traced here: 37.5 us
  starting transfers between devices  15.2 us (40%)
  waiting for transfers between devices  11.2 us (30%)
  Pallas kernels  10.2 us (27%)
  other arithmetic  0.78 us (2%)
    ppermute x6, starting transfers between devices, exchange(): return lax.ppermute(x, AXES, [(d, d ^ turn[d % 2]) for d in range(devices)])  8.58 us
    ppermute x6, waiting for transfers between devices, exchange(): return lax.ppermute(x, AXES, [(d, d ^ turn[d % 2]) for d in range(devices)])  7.17 us
    ppermute x4, starting transfers between devices, swap(): return lax.ppermute(x, AXES, [(d, d ^ bit) for d in range(devices)])  6.61 us
    pallas_call x2, Pallas kernels, sums(): call(functools.partial(sums_kernel, first, start, 256), (shape((2, count,...  4.3 us
    ppermute x4, waiting for transfers between devices, swap(): return lax.ppermute(x, AXES, [(d, d ^ bit) for d in range(devices)])  4.06 us
    pallas_call x2, Pallas kernels, trig_call(): call(functools.partial(trig_kernel, first, 256), (shape((2, count, rows),...  3.15 us
    pallas_call x1, Pallas kernels, shards(): call(functools.partial(back_kernel, 0, (0, 0, 0), 256, False), shape((hal...  0.99 us
    pallas_call x1, Pallas kernels, shards(): call(pack_kernel, (shape((HEAD + half, rows), bf16), shape((3, mine), jnp...  0.86 us
  transfers between devices with their start and end apart: 10, of which 9 were waited for; matrix products, arithmetic and copies ran while one was open for 0% of the time, Pallas kernels for 17%

profile of v6, /device:TPU:0, one launch (start us, length us, event | category | flops | bytes accessed | tf_op | source)
XLA Modules:
  0.0 37.5 jit_solution(5117653030878711211)
XLA Ops:
  0.0 0.9 %pack.1 = (bf16[64,256]{1,0:T(8,128)(2,1)S(1)}, s32[3,2048]{1,0:T(4,128)S(1)}) custom-call(s32[1]{0:T(128)} %bitcast.idx_ref, f32[3,256]{1,0:T(4,128)} %pos_hbm.1, f32[3,16,256]{2,1,0:T(8,128)} %force_hbm.1, s32[3,8192]{1,0:T(4,128)} %waves_hbm.1), custom_call_target="tpu_custom_call" | custom-call | tf_op jit(solution)/shard_map/pack/pallas_call | solution.py:228
  0.9 4.1 %collective-permute-start = (bf16[64,256]{1,0:T(8,128)(2,1)S(1)}, bf16[64,256]{1,0:T(8,128)(2,1)S(1)}, u32[]{:S(2)}, u32[]{:S(2)}) collective-permute-start(bf16[64,256]{1,0:T(8,128)(2,1)S(1)} %get-tuple-element.26.pack_ref), channel_id=1, source_target_pairs={{0,16},{1,17},{2,18},{3,19},{4,20},{5,21},{6,22},{7,23},{8,24},{9,... | collective-permute-start | bytes 98312 | tf_op jit(solution)/shard_map/ppermute | solution.py:221
  5.0 0.2 frame.1
  5.2 1.9 %trig_own.1 = (bf16[2,2048,256]{2,1,0:T(8,128)(2,1)S(1)}, f32[96,2048]{1,0:T(8,128)S(1)}) custom-call(bf16[2048,16]{1,0:T(8,128)(2,1)S(1)} %get-tuple-element.33.wt_ref, bf16[64,256]{1,0:T(8,128)(2,1)S(1)} %get-tuple-element.26.pack_ref), custom_call_target="tpu_custom_call" | custom-call | flops 100663296 | bytes 393216 | tf_op jit(solution)/shard_map/trig_own/pallas_call | solution.py:241
  7.3 1.3 %trig_far.1 = (bf16[2,1280,256]{2,1,0:T(8,128)(2,1)S(1)}, f32[96,1280]{1,0:T(8,128)S(1)}) custom-call(bf16[2048,16]{1,0:T(8,128)(2,1)S(1)} %get-tuple-element.33.wt_ref, bf16[64,256]{1,0:T(8,128)(2,1)S(1)} %collective-permute-done.refs_0_.pack_ref, f32[96,2048]{1,0:T(8,128)S(1)} %get-tuple-element.34.raw_ref.refs_0_), custom_call_target="tpu_custom_call" | custom-call | flops 62914560 | bytes 245760 | tf_op jit(solution)/shard_map/trig_far/pallas_call | solution.py:241
  8.6 2.3 %sums.3 = (bf16[2,1280,512]{2,1,0:T(8,128)(2,1)S(1)}, f32[64,1280]{1,0:T(8,128)S(1)}, bf16[64,1280]{1,0:T(8,128)(2,1)S(1)}) custom-call(f32[8,2048]{1,0:T(8,128)S(1)} %get-tuple-element.32.frame_ref, bf16[2048,16]{1,0:T(8,128)(2,1)S(1)} %get-tuple-element.33.wt_ref, f32[96,1280]{1,0:T(8,128)S(1)} %get-tuple-element.40.raw_ref, ...), custom_call_target="tpu_custom_call" | custom-call | flops 125829120 | bytes 491520 | tf_op jit(solution)/shard_map/sums/pallas_call | solution.py:256
  10.9 1.8 %collective-permute-start.5 = (bf16[64,1280]{1,0:T(8,128)(2,1)S(1)}, bf16[64,1280]{1,0:T(8,128)(2,1)S(1)}, u32[]{:S(2)}, u32[]{:S(2)}) collective-permute-start(bf16[64,1280]{1,0:T(8,128)(2,1)S(1)} %get-tuple-element.42), channel_id=1, source_target_pairs={{0,2},{1,5},{2,0},{3,7},{4,6},{5,1},{6,4},{7,3},{8,10},{9,13},{10,... | collective-permute-start | bytes 491528 | tf_op jit(solution)/shard_map/ppermute | solution.py:269
  12.6 2.0 %sums.2 = (bf16[2,768,768]{2,1,0:T(8,128)(2,1)S(1)}, f32[64,768]{1,0:T(8,128)S(1)}, bf16[64,768]{1,0:T(8,128)(2,1)S(1)}) custom-call(f32[8,2048]{1,0:T(8,128)S(1)} %get-tuple-element.32.frame_ref, bf16[2048,16]{1,0:T(8,128)(2,1)S(1)} %get-tuple-element.33.wt_ref, f32[96,2048]{1,0:T(8,128)S(1)} %get-tuple-element.34.raw_ref.refs_0_, ...), custom_call_target="tpu_custom_call" | custom-call | flops 113246208 | bytes 442368 | tf_op jit(solution)/shard_map/sums/pallas_call | solution.py:256
  14.7 1.4 %collective-permute-start.2 = (bf16[64,768]{1,0:T(8,128)(2,1)S(1)}, bf16[64,768]{1,0:T(8,128)(2,1)S(1)}, u32[]{:S(2)}, u32[]{:S(2)}) collective-permute-start(bf16[64,768]{1,0:T(8,128)(2,1)S(1)} %get-tuple-element.37), channel_id=1, source_target_pairs={{0,8},{1,3},{2,10},{3,1},{4,12},{5,7},{6,14},{7,5},{8,0},{9,11},{1... | collective-permute-start | bytes 294920 | tf_op jit(solution)/shard_map/ppermute | solution.py:269
  16.1 0.2 collective-permute-done.5
  16.3 1.9 %collective-permute-start.6 = (bf16[64,1280]{1,0:T(8,128)(2,1)S(1)}, bf16[64,1280]{1,0:T(8,128)(2,1)S(1)}, u32[]{:S(2)}, u32[]{:S(2)}) collective-permute-start(bf16[64,1280]{1,0:T(8,128)(2,1)S(1)} %fusion), channel_id=1, source_target_pairs={{0,4},{1,9},{2,6},{3,11},{4,0},{5,13},{6,2},{7,15},{8,12},{9,1},{1... | collective-permute-start | bytes 491528 | tf_op jit(solution)/shard_map/ppermute | solution.py:269
  18.2 1.7 %collective-permute-done.2 = bf16[64,768]{1,0:T(8,128)(2,1)S(1)} collective-permute-done((bf16[64,768]{1,0:T(8,128)(2,1)S(1)}, bf16[64,768]{1,0:T(8,128)(2,1)S(1)}, u32[]{:S(2)}, u32[]{:S(2)}) %collective-permute-start.2) | collective-permute-done | bytes 98336 | tf_op jit(solution)/shard_map/ppermute | solution.py:269
  19.9 2.1 %collective-permute-done.6 = bf16[64,1280]{1,0:T(8,128)(2,1)S(1)} collective-permute-done((bf16[64,1280]{1,0:T(8,128)(2,1)S(1)}, bf16[64,1280]{1,0:T(8,128)(2,1)S(1)}, u32[]{:S(2)}, u32[]{:S(2)}) %collective-permute-start.6) | collective-permute-done | bytes 163872 | tf_op jit(solution)/shard_map/ppermute | solution.py:269
  22.1 1.7 %collective-permute-start.7 = (bf16[64,1280]{1,0:T(8,128)(2,1)S(1)}, bf16[64,1280]{1,0:T(8,128)(2,1)S(1)}, u32[]{:S(2)}, u32[]{:S(2)}) collective-permute-start(bf16[64,1280]{1,0:T(8,128)(2,1)S(1)} %get-tuple-element.47), channel_id=1, source_target_pairs={{0,8},{1,3},{2,10},{3,1},{4,12},{5,7},{6,14},{7,5},{8,0},{9,11},{1... | collective-permute-start | bytes 491528 | tf_op jit(solution)/shard_map/ppermute | solution.py:269
  23.8 1.3 %collective-permute-done.3 = bf16[64,768]{1,0:T(8,128)(2,1)S(1)} collective-permute-done((bf16[64,768]{1,0:T(8,128)(2,1)S(1)}, bf16[64,768]{1,0:T(8,128)(2,1)S(1)}, u32[]{:S(2)}, u32[]{:S(2)}) %collective-permute-start.3) | collective-permute-done | bytes 98336 | tf_op jit(solution)/shard_map/ppermute | solution.py:269
  25.2 1.8 %collective-permute-start.4 = (bf16[64,768]{1,0:T(8,128)(2,1)S(1)}, bf16[64,768]{1,0:T(8,128)(2,1)S(1)}, u32[]{:S(2)}, u32[]{:S(2)}) collective-permute-start(bf16[64,768]{1,0:T(8,128)(2,1)S(1)} %get-tuple-element.49), channel_id=1, source_target_pairs={{0,4},{1,9},{2,6},{3,11},{4,0},{5,13},{6,2},{7,15},{8,12},{9,1},{1... | collective-permute-start | bytes 294920 | tf_op jit(solution)/shard_map/ppermute | solution.py:269
  27.0 1.1 %collective-permute-done.7.recv_ref = bf16[64,1280]{1,0:T(8,128)(2,1)S(1)} collective-permute-done((bf16[64,1280]{1,0:T(8,128)(2,1)S(1)}, bf16[64,1280]{1,0:T(8,128)(2,1)S(1)}, u32[]{:S(2)}, u32[]{:S(2)}) %collective-permute-start.7) | collective-permute-done | bytes 163872 | tf_op jit(solution)/shard_map/ppermute | solution.py:269
  28.1 1.0 %back.2.refs_2_ = f32[48,1024]{1,0:T(8,128)S(1)} custom-call(f32[64,1280]{1,0:T(8,128)S(1)} %get-tuple-element.48.acc_ref, bf16[64,1280]{1,0:T(8,128)(2,1)S(1)} %collective-permute-done.7.recv_ref, f32[8,2048]{1,0:T(8,128)S(1)} %get-tuple-element.32.frame_ref, bf16[2,2048,256]{2,1,0:T(8,128)(2,1)S(1)} %get-tuple-element.38.refs_0_, ...), custom_call_target="tpu_custom_call" | custom-call | flops 251658240 | bytes 983040 | tf_op jit(solution)/shard_map/back/pallas_call | solution.py:283
  29.1 0.8 %collective-permute-done.4.recv_ref = bf16[64,768]{1,0:T(8,128)(2,1)S(1)} collective-permute-done((bf16[64,768]{1,0:T(8,128)(2,1)S(1)}, bf16[64,768]{1,0:T(8,128)(2,1)S(1)}, u32[]{:S(2)}, u32[]{:S(2)}) %collective-permute-start.4) | collective-permute-done | bytes 98336 | tf_op jit(solution)/shard_map/ppermute | solution.py:269
  29.8 0.6 %back.3 = (f32[48,512]{1,0:T(8,128)S(1)}, bf16[48,512]{1,0:T(8,128)(2,1)S(1)}) custom-call(f32[64,768]{1,0:T(8,128)S(1)} %get-tuple-element.50.acc_ref, bf16[64,768]{1,0:T(8,128)(2,1)S(1)} %collective-permute-done.4.recv_ref, f32[8,2048]{1,0:T(8,128)S(1)} %get-tuple-element.32.frame_ref, bf16[2,2048,256]{2,1,0:T(8,128)(2,1)S(1)} %get-tuple-element.38.refs_0_, ...), custom_call_target="tpu_custom_call" | custom-call | flops 150994944 | bytes 589824 | tf_op jit(solution)/shard_map/back/pallas_call | solution.py:286
  30.6 1.2 %collective-permute-done.8 = bf16[48,512]{1,0:T(8,128)(2,1)S(1)} collective-permute-done((bf16[48,512]{1,0:T(8,128)(2,1)S(1)}, bf16[48,512]{1,0:T(8,128)(2,1)S(1)}, u32[]{:S(2)}, u32[]{:S(2)}) %collective-permute-start.8) | collective-permute-done | bytes 49184 | tf_op jit(solution)/shard_map/ppermute | solution.py:221
  31.8 2.3 %collective-permute-start.9 = (bf16[48,256]{1,0:T(8,128)(2,1)S(1)}, bf16[48,256]{1,0:T(8,128)(2,1)S(1)}, u32[]{:S(2)}, u32[]{:S(2)}) collective-permute-start(bf16[48,256]{1,0:T(8,128)(2,1)S(1)} %slice.13), channel_id=1, source_target_pairs={{0,16},{1,17},{2,18},{3,19},{4,20},{5,21},{6,22},{7,23},{8,24},{9,... | collective-permute-start | bytes 73736 | tf_op jit(solution)/shard_map/ppermute | solution.py:221
  34.2 2.7 %collective-permute-done.9 = bf16[48,256]{1,0:T(8,128)(2,1)S(1)} collective-permute-done((bf16[48,256]{1,0:T(8,128)(2,1)S(1)}, bf16[48,256]{1,0:T(8,128)(2,1)S(1)}, u32[]{:S(2)}, u32[]{:S(2)}) %collective-permute-start.9) | collective-permute-done | bytes 24608 | tf_op jit(solution)/shard_map/ppermute | solution.py:221
  36.9 0.6 %slice_add_fusion = f32[48,256]{1,0:T(8,128)} fusion(f32[48,512]{1,0:T(8,128)S(1)} %convert_add_fusion.4, bf16[48,256]{1,0:T(8,128)(2,1)S(1)} %collective-permute-done.9), kind=kLoop, calls=%fused_computation.9 | loop fusion | flops 24576 | bytes 122880 | tf_op jit(solution)/shard_map/add | solution.py:296
  (12 shorter events, 0.5 us)
Async XLA Ops:
  0.9 6.4 %collective-permute-start = (bf16[64,256]{1,0:T(8,128)(2,1)S(1)}, bf16[64,256]{1,0:T(8,128)(2,1)S(1)}, u32[]{:S(2)}, u32[]{:S(2)}) collective-permute-start(bf16[64,256]{1,0:T(8,128)(2,1)S(1)} %get-tuple-element.26.pack_ref), channel_id=1, source_target_pairs={{0,16},{1,17},{2,18},{3,19},{4,20},{5,21},{6,22},{7,23},{8,24},{9,... | collective-permute-start | bytes 98312 | tf_op jit(solution)/shard_map/ppermute | solution.py:221
  7.3 1.4 %collective-permute-start.1 = (bf16[2,64,256]{2,1,0:T(8,128)(2,1)S(1)}, bf16[2,64,256]{2,1,0:T(8,128)(2,1)S(1)}, u32[]{:S(2)}, u32[]{:S(2)}) collective-permute-start(bf16[2,64,256]{2,1,0:T(8,128)(2,1)S(1)} %pad_maximum_fusion), channel_id=1, source_target_pairs={{0,1},{1,0},{2,3},{3,2},{4,5},{5,4},{6,7},{7,6},{8,9},{9,8},{10,11... | collective-permute-start | bytes 196616 | tf_op jit(solution)/shard_map/ppermute | solution.py:221
  10.9 5.4 %collective-permute-start.5 = (bf16[64,1280]{1,0:T(8,128)(2,1)S(1)}, bf16[64,1280]{1,0:T(8,128)(2,1)S(1)}, u32[]{:S(2)}, u32[]{:S(2)}) collective-permute-start(bf16[64,1280]{1,0:T(8,128)(2,1)S(1)} %get-tuple-element.42), channel_id=1, source_target_pairs={{0,2},{1,5},{2,0},{3,7},{4,6},{5,1},{6,4},{7,3},{8,10},{9,13},{10,... | collective-permute-start | bytes 491528 | tf_op jit(solution)/shard_map/ppermute | solution.py:269
  14.7 5.1 %collective-permute-start.2 = (bf16[64,768]{1,0:T(8,128)(2,1)S(1)}, bf16[64,768]{1,0:T(8,128)(2,1)S(1)}, u32[]{:S(2)}, u32[]{:S(2)}) collective-permute-start(bf16[64,768]{1,0:T(8,128)(2,1)S(1)} %get-tuple-element.37), channel_id=1, source_target_pairs={{0,8},{1,3},{2,10},{3,1},{4,12},{5,7},{6,14},{7,5},{8,0},{9,11},{1... | collective-permute-start | bytes 294920 | tf_op jit(solution)/shard_map/ppermute | solution.py:269
  16.3 5.8 %collective-permute-start.6 = (bf16[64,1280]{1,0:T(8,128)(2,1)S(1)}, bf16[64,1280]{1,0:T(8,128)(2,1)S(1)}, u32[]{:S(2)}, u32[]{:S(2)}) collective-permute-start(bf16[64,1280]{1,0:T(8,128)(2,1)S(1)} %fusion), channel_id=1, source_target_pairs={{0,4},{1,9},{2,6},{3,11},{4,0},{5,13},{6,2},{7,15},{8,12},{9,1},{1... | collective-permute-start | bytes 491528 | tf_op jit(solution)/shard_map/ppermute | solution.py:269
  19.9 5.3 %collective-permute-start.3 = (bf16[64,768]{1,0:T(8,128)(2,1)S(1)}, bf16[64,768]{1,0:T(8,128)(2,1)S(1)}, u32[]{:S(2)}, u32[]{:S(2)}) collective-permute-start(bf16[64,768]{1,0:T(8,128)(2,1)S(1)} %fusion.1), channel_id=1, source_target_pairs={{0,2},{1,5},{2,0},{3,7},{4,6},{5,1},{6,4},{7,3},{8,10},{9,13},{10,... | collective-permute-start | bytes 294920 | tf_op jit(solution)/shard_map/ppermute | solution.py:269
  22.1 5.9 %collective-permute-start.7 = (bf16[64,1280]{1,0:T(8,128)(2,1)S(1)}, bf16[64,1280]{1,0:T(8,128)(2,1)S(1)}, u32[]{:S(2)}, u32[]{:S(2)}) collective-permute-start(bf16[64,1280]{1,0:T(8,128)(2,1)S(1)} %get-tuple-element.47), channel_id=1, source_target_pairs={{0,8},{1,3},{2,10},{3,1},{4,12},{5,7},{6,14},{7,5},{8,0},{9,11},{1... | collective-permute-start | bytes 491528 | tf_op jit(solution)/shard_map/ppermute | solution.py:269
  25.2 4.7 %collective-permute-start.4 = (bf16[64,768]{1,0:T(8,128)(2,1)S(1)}, bf16[64,768]{1,0:T(8,128)(2,1)S(1)}, u32[]{:S(2)}, u32[]{:S(2)}) collective-permute-start(bf16[64,768]{1,0:T(8,128)(2,1)S(1)} %get-tuple-element.49), channel_id=1, source_target_pairs={{0,4},{1,9},{2,6},{3,11},{4,0},{5,13},{6,2},{7,15},{8,12},{9,1},{1... | collective-permute-start | bytes 294920 | tf_op jit(solution)/shard_map/ppermute | solution.py:269
  30.5 1.3 %collective-permute-start.8 = (bf16[48,512]{1,0:T(8,128)(2,1)S(1)}, bf16[48,512]{1,0:T(8,128)(2,1)S(1)}, u32[]{:S(2)}, u32[]{:S(2)}) collective-permute-start(bf16[48,512]{1,0:T(8,128)(2,1)S(1)} %get-tuple-element.46), channel_id=1, source_target_pairs={{0,1},{1,0},{2,3},{3,2},{4,5},{5,4},{6,7},{7,6},{8,9},{9,8},{10,11... | collective-permute-start | bytes 147464 | tf_op jit(solution)/shard_map/ppermute | solution.py:221
  31.8 5.1 %collective-permute-start.9 = (bf16[48,256]{1,0:T(8,128)(2,1)S(1)}, bf16[48,256]{1,0:T(8,128)(2,1)S(1)}, u32[]{:S(2)}, u32[]{:S(2)}) collective-permute-start(bf16[48,256]{1,0:T(8,128)(2,1)S(1)} %slice.13), channel_id=1, source_target_pairs={{0,16},{1,17},{2,18},{3,19},{4,20},{5,21},{6,22},{7,23},{8,24},{9,... | collective-permute-start | bytes 73736 | tf_op jit(solution)/shard_map/ppermute | solution.py:221

commit v7 on v6

--- a/solution.py
+++ b/solution.py
@@ -16,8 +16,8 @@
 f32, bf16 = jnp.float32, jnp.bfloat16
 
 SIN = (4.442867901617319, -7.307443368323551, 3.594787581869042, -0.7843727161608242)
-ROUND = 12582912.0
 TINY = 1e-30
+STRIP = 32
 PACE = 2
 HEAD = 16
 
@@ -91,9 +91,8 @@
     wt_ref[...] = jnp.transpose(head).astype(bf16)
 
 
-def trig(w, phase, tab_ref, rows, cols):
-    u = jnp.dot(w, phase, preferred_element_type=f32)
-    r = u - ((u + ROUND) - ROUND)
+def trig(u, tab_ref, rows, cols):
+    r = u - jnp.round(u)
     s = r * horner(SIN, r * r)
     square = s * s
     tab_ref[0, rows, cols] = (1.0 - square).astype(bf16)
@@ -101,31 +100,46 @@
     tab_ref[1, rows, cols] = (s * (rest * lax.rsqrt(rest))).astype(bf16)
 
 
+def tables(first, chunk, wt_ref, phase, tab_ref, u_ref, sum_up):
+    count = tab_ref.shape[1]
+    width = phase.shape[1]
+    lanes = min(width, 256)
+
+    def phases(base):
+        w = wt_ref[first + base : first + base + chunk, :]
+        u_ref[base // chunk % 2] = jnp.dot(w, phase, preferred_element_type=f32)
+
+    phases(0)
+    waiting = []
+    for base in range(0, count, chunk):
+        if base + chunk < count:
+            phases(base + chunk)
+        for row in range(0, chunk, STRIP):
+            for low in range(0, width, lanes):
+                cols = slice(low, low + lanes)
+                trig(u_ref[base // chunk % 2, row : row + STRIP, cols], tab_ref, slice(base + row, base + row + STRIP), cols)
+            if waiting and row // STRIP % PACE == 0:
+                sum_up(*waiting.pop(0))
+        waiting.extend((base, part) for part in range(2))
+    for late in waiting:
+        sum_up(*late)
+
+
 def product(force, table):
     return lax.dot_general(force, table, (((1,), (1,)), ((), ())), preferred_element_type=f32)
 
 
 def trig_kernel(first, chunk, wt_ref, pack_ref, *refs):
-    earlier, tab_ref, raw_ref = refs if len(refs) == 3 else (None, *refs)
+    earlier, tab_ref, raw_ref, u_ref = refs if len(refs) == 4 else (None, *refs)
     half = pack_ref.shape[0] - HEAD
-    strip = 64
     phase, force = pack_ref[:HEAD], pack_ref[HEAD:]
-    count = tab_ref.shape[1]
 
     def sum_up(base, part):
         rows, cols = slice(part * half, (part + 1) * half), slice(base, base + chunk)
         sums = product(force, tab_ref[part, cols, :])
         raw_ref[rows, cols] = sums if earlier is None else sums + earlier[rows, cols]
 
-    waiting = []
-    for base in range(0, count, chunk):
-        for row in range(base, base + chunk, strip):
-            trig(wt_ref[first + row : first + row + strip, :], phase, tab_ref, slice(row, row + strip), slice(None))
-            if waiting and (row - base) // strip % 2 == 0:
-                sum_up(*waiting.pop(0))
-        waiting.extend((base, part) for part in range(2))
-    for late in waiting:
-        sum_up(*late)
+    tables(first, chunk, wt_ref, phase, tab_ref, u_ref, sum_up)
 
 
 def unpacked(refs):
@@ -136,15 +150,14 @@
 
 
 def sums_kernel(first, start, chunk, frame_ref, wt_ref, raw_ref, *refs):
-    todo = refs[:-3]
-    tab_ref, acc_ref, send_ref = refs[-3:]
+    todo = refs[:-4]
+    tab_ref, acc_ref, send_ref, u_ref = refs[-4:]
     kwaves = tab_ref.shape[1]
     probes = acc_ref.shape[0] // 4
     half = 3 * probes
     blocks = unpacked(todo)
-    width = blocks[0].shape[1]
+    phase = jnp.concatenate([b[:HEAD] for b in blocks], axis=1)
     forces = jnp.concatenate([b[HEAD:] for b in blocks], axis=1)
-    strip = 32
 
     def sum_up(base, part):
         cols = slice(base, base + chunk)
@@ -156,17 +169,7 @@
             acc_ref[low : low + probes, cols] = value
             send_ref[low : low + probes, cols] = value.astype(bf16)
 
-    waiting = []
-    for base in range(0, kwaves, chunk):
-        for row in range(base, base + chunk, strip):
-            w = wt_ref[first + row : first + row + strip, :]
-            for j, block in enumerate(blocks):
-                trig(w, block[:HEAD], tab_ref, slice(row, row + strip), slice(j * width, (j + 1) * width))
-            if waiting and (row - base) // strip % PACE == 0:
-                sum_up(*waiting.pop(0))
-        waiting.extend((base, part) for part in range(2))
-    for late in waiting:
-        sum_up(*late)
+    tables(first, chunk, wt_ref, phase, tab_ref, u_ref, sum_up)
 
 
 def back_kernel(first, offsets, chunk, last, acc_ref, recv_ref, frame_ref, *refs):
@@ -243,6 +246,7 @@
             (shape((2, count, rows), bf16), shape((2 * half, count), f32)),
             name,
             "v" * (1 + len(operands)),
+            scratch=[VMEM((2, 256, rows), f32)],
             flops=count * fl,
         )(wt, *operands)
 
@@ -258,6 +262,7 @@
             (shape((2, count, width), bf16), shape((4 * probes, count), f32), shape((4 * probes, count), bf16)),
             "sums",
             "v" * (3 + len(todo)),
+            scratch=[VMEM((2, 256, width), f32)],
             flops=count * fl * (width // rows),
         )(frame, wt, raw, *todo)
 

time: 37.7 us -> 37.2 us (0.987)
  Pallas kernels: 10.2 us -> 9.65 us
  transfers between devices with their start and end apart: 10 -> 10, of which waited for: 9 -> 10; matrix products, arithmetic and copies ran while one was open for 0% -> 0% of each run, Pallas kernels for 17% -> 17%
where the time goes in v7:
time: 37.2 us; the launch traced here: 37 us
  starting transfers between devices  15.4 us (41%)
  waiting for transfers between devices  11.1 us (30%)
  Pallas kernels  9.65 us (26%)
  other arithmetic  0.78 us (2%)
    ppermute x6, starting transfers between devices, exchange(): return lax.ppermute(x, AXES, [(d, d ^ turn[d % 2]) for d in range(devices)])  8.8 us
    ppermute x6, waiting for transfers between devices, exchange(): return lax.ppermute(x, AXES, [(d, d ^ turn[d % 2]) for d in range(devices)])  7.05 us
    ppermute x4, starting transfers between devices, swap(): return lax.ppermute(x, AXES, [(d, d ^ bit) for d in range(devices)])  6.61 us
    pallas_call x2, Pallas kernels, sums(): call(functools.partial(sums_kernel, first, start, 256), (shape((2, count,...  4.04 us
    ppermute x4, waiting for transfers between devices, swap(): return lax.ppermute(x, AXES, [(d, d ^ bit) for d in range(devices)])  4.04 us
    pallas_call x2, Pallas kernels, trig_call(): call(functools.partial(trig_kernel, first, 256), (shape((2, count, rows),...  2.88 us
    pallas_call x1, Pallas kernels, shards(): call(functools.partial(back_kernel, 0, (0, 0, 0), 256, False), shape((hal...  0.99 us
    pallas_call x1, Pallas kernels, shards(): call(pack_kernel, (shape((HEAD + half, rows), bf16), shape((3, mine), jnp...  0.86 us
  transfers between devices with their start and end apart: 10, of which 10 were waited for; matrix products, arithmetic and copies ran while one was open for 0% of the time, Pallas kernels for 17%

profile of v7, /device:TPU:0, one launch (start us, length us, event | category | flops | bytes accessed | tf_op | source)
XLA Modules:
  0.0 37.0 jit_solution(4996761249430013837)
XLA Ops:
  0.0 0.9 %pack.1 = (bf16[64,256]{1,0:T(8,128)(2,1)S(1)}, s32[3,2048]{1,0:T(4,128)S(1)}) custom-call(s32[1]{0:T(128)} %bitcast.idx_ref, f32[3,256]{1,0:T(4,128)} %pos_hbm.1, f32[3,16,256]{2,1,0:T(8,128)} %force_hbm.1, s32[3,8192]{1,0:T(4,128)} %waves_hbm.1), custom_call_target="tpu_custom_call" | custom-call | tf_op jit(solution)/shard_map/pack/pallas_call | solution.py:231
  0.9 4.1 %collective-permute-start = (bf16[64,256]{1,0:T(8,128)(2,1)S(1)}, bf16[64,256]{1,0:T(8,128)(2,1)S(1)}, u32[]{:S(2)}, u32[]{:S(2)}) collective-permute-start(bf16[64,256]{1,0:T(8,128)(2,1)S(1)} %get-tuple-element.26.pack_ref), channel_id=1, source_target_pairs={{0,16},{1,17},{2,18},{3,19},{4,20},{5,21},{6,22},{7,23},{8,24},{9,... | collective-permute-start | bytes 98312 | tf_op jit(solution)/shard_map/ppermute | solution.py:224
  5.0 0.2 frame.1
  5.2 1.7 %trig_own.1 = (bf16[2,2048,256]{2,1,0:T(8,128)(2,1)S(1)}, f32[96,2048]{1,0:T(8,128)S(1)}) custom-call(bf16[2048,16]{1,0:T(8,128)(2,1)S(1)} %get-tuple-element.33.wt_ref, bf16[64,256]{1,0:T(8,128)(2,1)S(1)} %get-tuple-element.26.pack_ref), custom_call_target="tpu_custom_call" | custom-call | flops 100663296 | bytes 393216 | tf_op jit(solution)/shard_map/trig_own/pallas_call | solution.py:244
  6.9 0.3 collective-permute-done.refs_0_.pack_ref
  7.3 1.2 %trig_far.1 = (bf16[2,1280,256]{2,1,0:T(8,128)(2,1)S(1)}, f32[96,1280]{1,0:T(8,128)S(1)}) custom-call(bf16[2048,16]{1,0:T(8,128)(2,1)S(1)} %get-tuple-element.33.wt_ref, bf16[64,256]{1,0:T(8,128)(2,1)S(1)} %collective-permute-done.refs_0_.pack_ref, f32[96,2048]{1,0:T(8,128)S(1)} %get-tuple-element.34.raw_ref.refs_0_), custom_call_target="tpu_custom_call" | custom-call | flops 62914560 | bytes 245760 | tf_op jit(solution)/shard_map/trig_far/pallas_call | solution.py:244
  8.6 2.0 %sums.3 = (bf16[2,1280,512]{2,1,0:T(8,128)(2,1)S(1)}, f32[64,1280]{1,0:T(8,128)S(1)}, bf16[64,1280]{1,0:T(8,128)(2,1)S(1)}) custom-call(f32[8,2048]{1,0:T(8,128)S(1)} %get-tuple-element.32.frame_ref, bf16[2048,16]{1,0:T(8,128)(2,1)S(1)} %get-tuple-element.33.wt_ref, f32[96,1280]{1,0:T(8,128)S(1)} %get-tuple-element.40.raw_ref, ...), custom_call_target="tpu_custom_call" | custom-call | flops 125829120 | bytes 491520 | tf_op jit(solution)/shard_map/sums/pallas_call | solution.py:260
  10.6 1.8 %collective-permute-start.5 = (bf16[64,1280]{1,0:T(8,128)(2,1)S(1)}, bf16[64,1280]{1,0:T(8,128)(2,1)S(1)}, u32[]{:S(2)}, u32[]{:S(2)}) collective-permute-start(bf16[64,1280]{1,0:T(8,128)(2,1)S(1)} %get-tuple-element.42), channel_id=1, source_target_pairs={{0,2},{1,5},{2,0},{3,7},{4,6},{5,1},{6,4},{7,3},{8,10},{9,13},{10,... | collective-permute-start | bytes 491528 | tf_op jit(solution)/shard_map/ppermute | solution.py:274
  12.3 2.0 %sums.2 = (bf16[2,768,768]{2,1,0:T(8,128)(2,1)S(1)}, f32[64,768]{1,0:T(8,128)S(1)}, bf16[64,768]{1,0:T(8,128)(2,1)S(1)}) custom-call(f32[8,2048]{1,0:T(8,128)S(1)} %get-tuple-element.32.frame_ref, bf16[2048,16]{1,0:T(8,128)(2,1)S(1)} %get-tuple-element.33.wt_ref, f32[96,2048]{1,0:T(8,128)S(1)} %get-tuple-element.34.raw_ref.refs_0_, ...), custom_call_target="tpu_custom_call" | custom-call | flops 113246208 | bytes 442368 | tf_op jit(solution)/shard_map/sums/pallas_call | solution.py:260
  14.4 1.4 %collective-permute-start.2 = (bf16[64,768]{1,0:T(8,128)(2,1)S(1)}, bf16[64,768]{1,0:T(8,128)(2,1)S(1)}, u32[]{:S(2)}, u32[]{:S(2)}) collective-permute-start(bf16[64,768]{1,0:T(8,128)(2,1)S(1)} %get-tuple-element.37), channel_id=1, source_target_pairs={{0,8},{1,3},{2,10},{3,1},{4,12},{5,7},{6,14},{7,5},{8,0},{9,11},{1... | collective-permute-start | bytes 294920 | tf_op jit(solution)/shard_map/ppermute | solution.py:274
  16.0 1.9 %collective-permute-start.6 = (bf16[64,1280]{1,0:T(8,128)(2,1)S(1)}, bf16[64,1280]{1,0:T(8,128)(2,1)S(1)}, u32[]{:S(2)}, u32[]{:S(2)}) collective-permute-start(bf16[64,1280]{1,0:T(8,128)(2,1)S(1)} %fusion), channel_id=1, source_target_pairs={{0,4},{1,9},{2,6},{3,11},{4,0},{5,13},{6,2},{7,15},{8,12},{9,1},{1... | collective-permute-start | bytes 491528 | tf_op jit(solution)/shard_map/ppermute | solution.py:274
  17.9 1.6 %collective-permute-done.2 = bf16[64,768]{1,0:T(8,128)(2,1)S(1)} collective-permute-done((bf16[64,768]{1,0:T(8,128)(2,1)S(1)}, bf16[64,768]{1,0:T(8,128)(2,1)S(1)}, u32[]{:S(2)}, u32[]{:S(2)}) %collective-permute-start.2) | collective-permute-done | bytes 98336 | tf_op jit(solution)/shard_map/ppermute | solution.py:274
  19.7 2.0 %collective-permute-done.6 = bf16[64,1280]{1,0:T(8,128)(2,1)S(1)} collective-permute-done((bf16[64,1280]{1,0:T(8,128)(2,1)S(1)}, bf16[64,1280]{1,0:T(8,128)(2,1)S(1)}, u32[]{:S(2)}, u32[]{:S(2)}) %collective-permute-start.6) | collective-permute-done | bytes 163872 | tf_op jit(solution)/shard_map/ppermute | solution.py:274
  21.8 1.8 %collective-permute-start.7 = (bf16[64,1280]{1,0:T(8,128)(2,1)S(1)}, bf16[64,1280]{1,0:T(8,128)(2,1)S(1)}, u32[]{:S(2)}, u32[]{:S(2)}) collective-permute-start(bf16[64,1280]{1,0:T(8,128)(2,1)S(1)} %get-tuple-element.47), channel_id=1, source_target_pairs={{0,8},{1,3},{2,10},{3,1},{4,12},{5,7},{6,14},{7,5},{8,0},{9,11},{1... | collective-permute-start | bytes 491528 | tf_op jit(solution)/shard_map/ppermute | solution.py:274
  23.6 1.3 %collective-permute-done.3 = bf16[64,768]{1,0:T(8,128)(2,1)S(1)} collective-permute-done((bf16[64,768]{1,0:T(8,128)(2,1)S(1)}, bf16[64,768]{1,0:T(8,128)(2,1)S(1)}, u32[]{:S(2)}, u32[]{:S(2)}) %collective-permute-start.3) | collective-permute-done | bytes 98336 | tf_op jit(solution)/shard_map/ppermute | solution.py:274
  24.9 1.8 %collective-permute-start.4 = (bf16[64,768]{1,0:T(8,128)(2,1)S(1)}, bf16[64,768]{1,0:T(8,128)(2,1)S(1)}, u32[]{:S(2)}, u32[]{:S(2)}) collective-permute-start(bf16[64,768]{1,0:T(8,128)(2,1)S(1)} %get-tuple-element.49), channel_id=1, source_target_pairs={{0,4},{1,9},{2,6},{3,11},{4,0},{5,13},{6,2},{7,15},{8,12},{9,1},{1... | collective-permute-start | bytes 294920 | tf_op jit(solution)/shard_map/ppermute | solution.py:274
  26.7 1.0 %collective-permute-done.7.recv_ref = bf16[64,1280]{1,0:T(8,128)(2,1)S(1)} collective-permute-done((bf16[64,1280]{1,0:T(8,128)(2,1)S(1)}, bf16[64,1280]{1,0:T(8,128)(2,1)S(1)}, u32[]{:S(2)}, u32[]{:S(2)}) %collective-permute-start.7) | collective-permute-done | bytes 163872 | tf_op jit(solution)/shard_map/ppermute | solution.py:274
  27.8 1.0 %back.2.refs_2_ = f32[48,1024]{1,0:T(8,128)S(1)} custom-call(f32[64,1280]{1,0:T(8,128)S(1)} %get-tuple-element.48.acc_ref, bf16[64,1280]{1,0:T(8,128)(2,1)S(1)} %collective-permute-done.7.recv_ref, f32[8,2048]{1,0:T(8,128)S(1)} %get-tuple-element.32.frame_ref, bf16[2,2048,256]{2,1,0:T(8,128)(2,1)S(1)} %get-tuple-element.38.refs_0_, ...), custom_call_target="tpu_custom_call" | custom-call | flops 251658240 | bytes 983040 | tf_op jit(solution)/shard_map/back/pallas_call | solution.py:288
  28.8 0.9 %collective-permute-done.4.recv_ref = bf16[64,768]{1,0:T(8,128)(2,1)S(1)} collective-permute-done((bf16[64,768]{1,0:T(8,128)(2,1)S(1)}, bf16[64,768]{1,0:T(8,128)(2,1)S(1)}, u32[]{:S(2)}, u32[]{:S(2)}) %collective-permute-start.4) | collective-permute-done | bytes 98336 | tf_op jit(solution)/shard_map/ppermute | solution.py:274
  29.6 0.6 %back.3 = (f32[48,512]{1,0:T(8,128)S(1)}, bf16[48,512]{1,0:T(8,128)(2,1)S(1)}) custom-call(f32[64,768]{1,0:T(8,128)S(1)} %get-tuple-element.50.acc_ref, bf16[64,768]{1,0:T(8,128)(2,1)S(1)} %collective-permute-done.4.recv_ref, f32[8,2048]{1,0:T(8,128)S(1)} %get-tuple-element.32.frame_ref, bf16[2,2048,256]{2,1,0:T(8,128)(2,1)S(1)} %get-tuple-element.38.refs_0_, ...), custom_call_target="tpu_custom_call" | custom-call | flops 150994944 | bytes 589824 | tf_op jit(solution)/shard_map/back/pallas_call | solution.py:291
  30.4 1.2 %collective-permute-done.8 = bf16[48,512]{1,0:T(8,128)(2,1)S(1)} collective-permute-done((bf16[48,512]{1,0:T(8,128)(2,1)S(1)}, bf16[48,512]{1,0:T(8,128)(2,1)S(1)}, u32[]{:S(2)}, u32[]{:S(2)}) %collective-permute-start.8) | collective-permute-done | bytes 49184 | tf_op jit(solution)/shard_map/ppermute | solution.py:224
  31.6 2.3 %collective-permute-start.9 = (bf16[48,256]{1,0:T(8,128)(2,1)S(1)}, bf16[48,256]{1,0:T(8,128)(2,1)S(1)}, u32[]{:S(2)}, u32[]{:S(2)}) collective-permute-start(bf16[48,256]{1,0:T(8,128)(2,1)S(1)} %slice.13), channel_id=1, source_target_pairs={{0,16},{1,17},{2,18},{3,19},{4,20},{5,21},{6,22},{7,23},{8,24},{9,... | collective-permute-start | bytes 73736 | tf_op jit(solution)/shard_map/ppermute | solution.py:224
  33.9 2.5 %collective-permute-done.9 = bf16[48,256]{1,0:T(8,128)(2,1)S(1)} collective-permute-done((bf16[48,256]{1,0:T(8,128)(2,1)S(1)}, bf16[48,256]{1,0:T(8,128)(2,1)S(1)}, u32[]{:S(2)}, u32[]{:S(2)}) %collective-permute-start.9) | collective-permute-done | bytes 24608 | tf_op jit(solution)/shard_map/ppermute | solution.py:224
  36.4 0.6 %slice_add_fusion = f32[48,256]{1,0:T(8,128)} fusion(f32[48,512]{1,0:T(8,128)S(1)} %convert_add_fusion.4, bf16[48,256]{1,0:T(8,128)(2,1)S(1)} %collective-permute-done.9), kind=kLoop, calls=%fused_computation.9 | loop fusion | flops 24576 | bytes 122880 | tf_op jit(solution)/shard_map/add | solution.py:301
  (12 shorter events, 0.6 us)
Async XLA Ops:
  0.9 6.4 %collective-permute-start = (bf16[64,256]{1,0:T(8,128)(2,1)S(1)}, bf16[64,256]{1,0:T(8,128)(2,1)S(1)}, u32[]{:S(2)}, u32[]{:S(2)}) collective-permute-start(bf16[64,256]{1,0:T(8,128)(2,1)S(1)} %get-tuple-element.26.pack_ref), channel_id=1, source_target_pairs={{0,16},{1,17},{2,18},{3,19},{4,20},{5,21},{6,22},{7,23},{8,24},{9,... | collective-permute-start | bytes 98312 | tf_op jit(solution)/shard_map/ppermute | solution.py:224
  7.3 1.3 %collective-permute-start.1 = (bf16[2,64,256]{2,1,0:T(8,128)(2,1)S(1)}, bf16[2,64,256]{2,1,0:T(8,128)(2,1)S(1)}, u32[]{:S(2)}, u32[]{:S(2)}) collective-permute-start(bf16[2,64,256]{2,1,0:T(8,128)(2,1)S(1)} %pad_maximum_fusion), channel_id=1, source_target_pairs={{0,1},{1,0},{2,3},{3,2},{4,5},{5,4},{6,7},{7,6},{8,9},{9,8},{10,11... | collective-permute-start | bytes 196616 | tf_op jit(solution)/shard_map/ppermute | solution.py:224
  10.6 5.4 %collective-permute-start.5 = (bf16[64,1280]{1,0:T(8,128)(2,1)S(1)}, bf16[64,1280]{1,0:T(8,128)(2,1)S(1)}, u32[]{:S(2)}, u32[]{:S(2)}) collective-permute-start(bf16[64,1280]{1,0:T(8,128)(2,1)S(1)} %get-tuple-element.42), channel_id=1, source_target_pairs={{0,2},{1,5},{2,0},{3,7},{4,6},{5,1},{6,4},{7,3},{8,10},{9,13},{10,... | collective-permute-start | bytes 491528 | tf_op jit(solution)/shard_map/ppermute | solution.py:274
  14.4 5.2 %collective-permute-start.2 = (bf16[64,768]{1,0:T(8,128)(2,1)S(1)}, bf16[64,768]{1,0:T(8,128)(2,1)S(1)}, u32[]{:S(2)}, u32[]{:S(2)}) collective-permute-start(bf16[64,768]{1,0:T(8,128)(2,1)S(1)} %get-tuple-element.37), channel_id=1, source_target_pairs={{0,8},{1,3},{2,10},{3,1},{4,12},{5,7},{6,14},{7,5},{8,0},{9,11},{1... | collective-permute-start | bytes 294920 | tf_op jit(solution)/shard_map/ppermute | solution.py:274
  16.0 5.7 %collective-permute-start.6 = (bf16[64,1280]{1,0:T(8,128)(2,1)S(1)}, bf16[64,1280]{1,0:T(8,128)(2,1)S(1)}, u32[]{:S(2)}, u32[]{:S(2)}) collective-permute-start(bf16[64,1280]{1,0:T(8,128)(2,1)S(1)} %fusion), channel_id=1, source_target_pairs={{0,4},{1,9},{2,6},{3,11},{4,0},{5,13},{6,2},{7,15},{8,12},{9,1},{1... | collective-permute-start | bytes 491528 | tf_op jit(solution)/shard_map/ppermute | solution.py:274
  19.6 5.3 %collective-permute-start.3 = (bf16[64,768]{1,0:T(8,128)(2,1)S(1)}, bf16[64,768]{1,0:T(8,128)(2,1)S(1)}, u32[]{:S(2)}, u32[]{:S(2)}) collective-permute-start(bf16[64,768]{1,0:T(8,128)(2,1)S(1)} %fusion.1), channel_id=1, source_target_pairs={{0,2},{1,5},{2,0},{3,7},{4,6},{5,1},{6,4},{7,3},{8,10},{9,13},{10,... | collective-permute-start | bytes 294920 | tf_op jit(solution)/shard_map/ppermute | solution.py:274
  21.8 6.0 %collective-permute-start.7 = (bf16[64,1280]{1,0:T(8,128)(2,1)S(1)}, bf16[64,1280]{1,0:T(8,128)(2,1)S(1)}, u32[]{:S(2)}, u32[]{:S(2)}) collective-permute-start(bf16[64,1280]{1,0:T(8,128)(2,1)S(1)} %get-tuple-element.47), channel_id=1, source_target_pairs={{0,8},{1,3},{2,10},{3,1},{4,12},{5,7},{6,14},{7,5},{8,0},{9,11},{1... | collective-permute-start | bytes 491528 | tf_op jit(solution)/shard_map/ppermute | solution.py:274
  24.9 4.7 %collective-permute-start.4 = (bf16[64,768]{1,0:T(8,128)(2,1)S(1)}, bf16[64,768]{1,0:T(8,128)(2,1)S(1)}, u32[]{:S(2)}, u32[]{:S(2)}) collective-permute-start(bf16[64,768]{1,0:T(8,128)(2,1)S(1)} %get-tuple-element.49), channel_id=1, source_target_pairs={{0,4},{1,9},{2,6},{3,11},{4,0},{5,13},{6,2},{7,15},{8,12},{9,1},{1... | collective-permute-start | bytes 294920 | tf_op jit(solution)/shard_map/ppermute | solution.py:274
  30.3 1.3 %collective-permute-start.8 = (bf16[48,512]{1,0:T(8,128)(2,1)S(1)}, bf16[48,512]{1,0:T(8,128)(2,1)S(1)}, u32[]{:S(2)}, u32[]{:S(2)}) collective-permute-start(bf16[48,512]{1,0:T(8,128)(2,1)S(1)} %get-tuple-element.46), channel_id=1, source_target_pairs={{0,1},{1,0},{2,3},{3,2},{4,5},{5,4},{6,7},{7,6},{8,9},{9,8},{10,11... | collective-permute-start | bytes 147464 | tf_op jit(solution)/shard_map/ppermute | solution.py:224
  31.6 4.8 %collective-permute-start.9 = (bf16[48,256]{1,0:T(8,128)(2,1)S(1)}, bf16[48,256]{1,0:T(8,128)(2,1)S(1)}, u32[]{:S(2)}, u32[]{:S(2)}) collective-permute-start(bf16[48,256]{1,0:T(8,128)(2,1)S(1)} %slice.13), channel_id=1, source_target_pairs={{0,16},{1,17},{2,18},{3,19},{4,20},{5,21},{6,22},{7,23},{8,24},{9,... | collective-permute-start | bytes 73736 | tf_op jit(solution)/shard_map/ppermute | solution.py:224

commit v8 on v7

--- a/solution.py
+++ b/solution.py
@@ -15,8 +15,7 @@
 SMEM = pltpu.SMEM
 f32, bf16 = jnp.float32, jnp.bfloat16
 
-SIN = (4.442867901617319, -7.307443368323551, 3.594787581869042, -0.7843727161608242)
-TINY = 1e-30
+SIN = (4.4428676475109, -7.307433203747474, 3.5946900772135946, -0.7841130155066478)
 STRIP = 32
 PACE = 2
 HEAD = 16
@@ -96,31 +95,37 @@
     s = r * horner(SIN, r * r)
     square = s * s
     tab_ref[0, rows, cols] = (1.0 - square).astype(bf16)
-    rest = jnp.maximum(2.0 - square, TINY)
+    rest = 2.0 - square
     tab_ref[1, rows, cols] = (s * (rest * lax.rsqrt(rest))).astype(bf16)
 
 
-def tables(first, chunk, wt_ref, phase, tab_ref, u_ref, sum_up):
-    count = tab_ref.shape[1]
+def runs_of(count):
+    cuts = [*range(0, count, 256), count] if count % 256 else [*range(0, count - 256, 256), count - 256, count - 128, count]
+    return [(a, b - a) for a, b in zip(cuts, cuts[1:])]
+
+
+def tables(first, wt_ref, phase, tab_ref, u_ref, sum_up):
     width = phase.shape[1]
     lanes = min(width, 256)
-
-    def phases(base):
-        w = wt_ref[first + base : first + base + chunk, :]
-        u_ref[base // chunk % 2] = jnp.dot(w, phase, preferred_element_type=f32)
+    runs = runs_of(tab_ref.shape[1])
+
+    def phases(n):
+        base, count = runs[n]
+        w = wt_ref[first + base : first + base + count, :]
+        u_ref[n % 2, :count] = jnp.dot(w, phase, preferred_element_type=f32)
 
     phases(0)
     waiting = []
-    for base in range(0, count, chunk):
-        if base + chunk < count:
-            phases(base + chunk)
-        for row in range(0, chunk, STRIP):
+    for n, (base, count) in enumerate(runs):
+        if n + 1 < len(runs):
+            phases(n + 1)
+        for row in range(0, count, STRIP):
             for low in range(0, width, lanes):
                 cols = slice(low, low + lanes)
-                trig(u_ref[base // chunk % 2, row : row + STRIP, cols], tab_ref, slice(base + row, base + row + STRIP), cols)
+                trig(u_ref[n % 2, row : row + STRIP, cols], tab_ref, slice(base + row, base + row + STRIP), cols)
             if waiting and row // STRIP % PACE == 0:
                 sum_up(*waiting.pop(0))
-        waiting.extend((base, part) for part in range(2))
+        waiting.extend((slice(base, base + count), part) for part in range(2))
     for late in waiting:
         sum_up(*late)
 
@@ -129,17 +134,17 @@
     return lax.dot_general(force, table, (((1,), (1,)), ((), ())), preferred_element_type=f32)
 
 
-def trig_kernel(first, chunk, wt_ref, pack_ref, *refs):
+def trig_kernel(first, wt_ref, pack_ref, *refs):
     earlier, tab_ref, raw_ref, u_ref = refs if len(refs) == 4 else (None, *refs)
     half = pack_ref.shape[0] - HEAD
     phase, force = pack_ref[:HEAD], pack_ref[HEAD:]
 
-    def sum_up(base, part):
-        rows, cols = slice(part * half, (part + 1) * half), slice(base, base + chunk)
+    def sum_up(cols, part):
+        rows = slice(part * half, (part + 1) * half)
         sums = product(force, tab_ref[part, cols, :])
         raw_ref[rows, cols] = sums if earlier is None else sums + earlier[rows, cols]
 
-    tables(first, chunk, wt_ref, phase, tab_ref, u_ref, sum_up)
+    tables(first, wt_ref, phase, tab_ref, u_ref, sum_up)
 
 
 def unpacked(refs):
@@ -149,7 +154,7 @@
     return blocks
 
 
-def sums_kernel(first, start, chunk, frame_ref, wt_ref, raw_ref, *refs):
+def sums_kernel(first, start, frame_ref, wt_ref, raw_ref, *refs):
     todo = refs[:-4]
     tab_ref, acc_ref, send_ref, u_ref = refs[-4:]
     kwaves = tab_ref.shape[1]
@@ -159,17 +164,16 @@
     phase = jnp.concatenate([b[:HEAD] for b in blocks], axis=1)
     forces = jnp.concatenate([b[HEAD:] for b in blocks], axis=1)
 
-    def sum_up(base, part):
-        cols = slice(base, base + chunk)
-        sums = product(forces, tab_ref[part, cols, :]) + raw_ref[part * half : (part + 1) * half, start + base : start + base + chunk]
-        fr = frame_ref[:, first + base : first + base + chunk]
+    def sum_up(cols, part):
+        sums = product(forces, tab_ref[part, cols, :]) + raw_ref[part * half : (part + 1) * half, start + cols.start : start + cols.stop]
+        fr = frame_ref[:, first + cols.start : first + cols.stop]
         for j in range(2):
             value = sum(fr[3 * j + x : 3 * j + x + 1] * sums[x * probes : (x + 1) * probes] for x in range(3))
             low = (2 * part + j) * probes
             acc_ref[low : low + probes, cols] = value
             send_ref[low : low + probes, cols] = value.astype(bf16)
 
-    tables(first, chunk, wt_ref, phase, tab_ref, u_ref, sum_up)
+    tables(first, wt_ref, phase, tab_ref, u_ref, sum_up)
 
 
 def back_kernel(first, offsets, chunk, last, acc_ref, recv_ref, frame_ref, *refs):
@@ -242,7 +246,7 @@
 
     def trig_call(name, first, count, *operands):
         return call(
-            functools.partial(trig_kernel, first, 256),
+            functools.partial(trig_kernel, first),
             (shape((2, count, rows), bf16), shape((2 * half, count), f32)),
             name,
             "v" * (1 + len(operands)),
@@ -258,7 +262,7 @@
 
     def sums(first, count, start, raw, todo, width):
         return call(
-            functools.partial(sums_kernel, first, start, 256),
+            functools.partial(sums_kernel, first, start),
             (shape((2, count, width), bf16), shape((4 * probes, count), f32), shape((4 * probes, count), bf16)),
             "sums",
             "v" * (3 + len(todo)),
@@ -269,8 +273,8 @@
     middle = [1 << j for j in range(1, bits - 1)]
     steps = len(middle)
 
-    def exchange(x, j, chunk):
-        turn = [middle[(j + core + 2 * chunk) % steps] for core in range(2)]
+    def exchange(x, j):
+        turn = [middle[(j + core) % steps] for core in range(2)]
         return lax.ppermute(x, AXES, [(d, d ^ turn[d % 2]) for d in range(devices)])
 
     tab_far, raw_a = trig_call("trig_far", 0, split, far, raw)
@@ -280,7 +284,7 @@
     for j in range(steps):
         for chunk in range(2):
             acc, send, _ = state[chunk]
-            got = exchange(send, j, chunk)
+            got = exchange(send, j)
             if j + 1 < steps:
                 acc = acc + got.astype(f32)
                 send = acc.astype(bf16)

time: 37.2 us -> 35.8 us (0.962)
  waiting for transfers between devices: 11.1 us -> 10.2 us
    ppermute x6, waiting for transfers between devices: 7.05 us -> 6.15 us  [exchange(): return lax.ppermute(x, AXES, [(d, d ^ turn[d % 2]) for d in range(devices)])]
  transfers between devices with their start and end apart: 10 -> 10, of which waited for: 10 -> 10; matrix products, arithmetic and copies ran while one was open for 0% -> 0% of each run, Pallas kernels for 17% -> 16%
where the time goes in v8:
time: 35.8 us; the launch traced here: 35.7 us
  starting transfers between devices  15.3 us (43%)
  waiting for transfers between devices  10.2 us (28%)
  Pallas kernels  9.31 us (26%)
  other arithmetic  0.78 us (2%)
    ppermute x6, starting transfers between devices, exchange(): return lax.ppermute(x, AXES, [(d, d ^ turn[d % 2]) for d in range(devices)])  8.58 us
    ppermute x4, starting transfers between devices, swap(): return lax.ppermute(x, AXES, [(d, d ^ bit) for d in range(devices)])  6.72 us
    ppermute x6, waiting for transfers between devices, exchange(): return lax.ppermute(x, AXES, [(d, d ^ turn[d % 2]) for d in range(devices)])  6.15 us
    ppermute x4, waiting for transfers between devices, swap(): return lax.ppermute(x, AXES, [(d, d ^ bit) for d in range(devices)])  4.02 us
    pallas_call x2, Pallas kernels, sums(): call(functools.partial(sums_kernel, first, start), (shape((2, count, widt...  3.79 us
    pallas_call x2, Pallas kernels, trig_call(): call(functools.partial(trig_kernel, first), (shape((2, count, rows), bf16...  2.79 us
    pallas_call x1, Pallas kernels, shards(): call(functools.partial(back_kernel, 0, (0, 0, 0), 256, False), shape((hal...  0.99 us
    pallas_call x1, Pallas kernels, shards(): call(pack_kernel, (shape((HEAD + half, rows), bf16), shape((3, mine), jnp...  0.86 us
  transfers between devices with their start and end apart: 10, of which 10 were waited for; matrix products, arithmetic and copies ran while one was open for 0% of the time, Pallas kernels for 16%

profile of v8, /device:TPU:0, one launch (start us, length us, event | category | flops | bytes accessed | tf_op | source)
XLA Modules:
  0.0 35.7 jit_solution(14113662396541331386)
XLA Ops:
  0.0 0.9 %pack.1 = (bf16[64,256]{1,0:T(8,128)(2,1)S(1)}, s32[3,2048]{1,0:T(4,128)S(1)}) custom-call(s32[1]{0:T(128)} %bitcast.idx_ref, f32[3,256]{1,0:T(4,128)} %pos_hbm.1, f32[3,16,256]{2,1,0:T(8,128)} %force_hbm.1, s32[3,8192]{1,0:T(4,128)} %waves_hbm.1), custom_call_target="tpu_custom_call" | custom-call | tf_op jit(solution)/shard_map/pack/pallas_call | solution.py:235
  0.9 4.1 %collective-permute-start = (bf16[64,256]{1,0:T(8,128)(2,1)S(1)}, bf16[64,256]{1,0:T(8,128)(2,1)S(1)}, u32[]{:S(2)}, u32[]{:S(2)}) collective-permute-start(bf16[64,256]{1,0:T(8,128)(2,1)S(1)} %get-tuple-element.26.pack_ref), channel_id=1, source_target_pairs={{0,16},{1,17},{2,18},{3,19},{4,20},{5,21},{6,22},{7,23},{8,24},{9,... | collective-permute-start | bytes 98312 | tf_op jit(solution)/shard_map/ppermute | solution.py:228
  5.2 1.7 %trig_own.1 = (bf16[2,2048,256]{2,1,0:T(8,128)(2,1)S(1)}, f32[96,2048]{1,0:T(8,128)S(1)}) custom-call(bf16[2048,16]{1,0:T(8,128)(2,1)S(1)} %get-tuple-element.33.wt_ref, bf16[64,256]{1,0:T(8,128)(2,1)S(1)} %get-tuple-element.26.pack_ref), custom_call_target="tpu_custom_call" | custom-call | flops 100663296 | bytes 393216 | tf_op jit(solution)/shard_map/trig_own/pallas_call | solution.py:248
  7.3 1.1 %trig_far.1 = (bf16[2,1280,256]{2,1,0:T(8,128)(2,1)S(1)}, f32[96,1280]{1,0:T(8,128)S(1)}) custom-call(bf16[2048,16]{1,0:T(8,128)(2,1)S(1)} %get-tuple-element.33.wt_ref, bf16[64,256]{1,0:T(8,128)(2,1)S(1)} %collective-permute-done.refs_0_.pack_ref, f32[96,2048]{1,0:T(8,128)S(1)} %get-tuple-element.34.raw_ref.refs_0_), custom_call_target="tpu_custom_call" | custom-call | flops 62914560 | bytes 245760 | tf_op jit(solution)/shard_map/trig_far/pallas_call | solution.py:248
  8.6 2.0 %sums.3 = (bf16[2,1280,512]{2,1,0:T(8,128)(2,1)S(1)}, f32[64,1280]{1,0:T(8,128)S(1)}, bf16[64,1280]{1,0:T(8,128)(2,1)S(1)}) custom-call(f32[8,2048]{1,0:T(8,128)S(1)} %get-tuple-element.32.frame_ref, bf16[2048,16]{1,0:T(8,128)(2,1)S(1)} %get-tuple-element.33.wt_ref, f32[96,1280]{1,0:T(8,128)S(1)} %get-tuple-element.40.raw_ref, ...), custom_call_target="tpu_custom_call" | custom-call | flops 125829120 | bytes 491520 | tf_op jit(solution)/shard_map/sums/pallas_call | solution.py:264
  10.5 1.8 %collective-permute-start.5 = (bf16[64,1280]{1,0:T(8,128)(2,1)S(1)}, bf16[64,1280]{1,0:T(8,128)(2,1)S(1)}, u32[]{:S(2)}, u32[]{:S(2)}) collective-permute-start(bf16[64,1280]{1,0:T(8,128)(2,1)S(1)} %get-tuple-element.42), channel_id=1, source_target_pairs={{0,2},{1,5},{2,0},{3,7},{4,6},{5,1},{6,4},{7,3},{8,10},{9,13},{10,... | collective-permute-start | bytes 491528 | tf_op jit(solution)/shard_map/ppermute | solution.py:278
  12.3 1.8 %sums.2 = (bf16[2,768,768]{2,1,0:T(8,128)(2,1)S(1)}, f32[64,768]{1,0:T(8,128)S(1)}, bf16[64,768]{1,0:T(8,128)(2,1)S(1)}) custom-call(f32[8,2048]{1,0:T(8,128)S(1)} %get-tuple-element.32.frame_ref, bf16[2048,16]{1,0:T(8,128)(2,1)S(1)} %get-tuple-element.33.wt_ref, f32[96,2048]{1,0:T(8,128)S(1)} %get-tuple-element.34.raw_ref.refs_0_, ...), custom_call_target="tpu_custom_call" | custom-call | flops 113246208 | bytes 442368 | tf_op jit(solution)/shard_map/sums/pallas_call | solution.py:264
  14.1 0.4 %collective-permute-start.2 = (bf16[64,768]{1,0:T(8,128)(2,1)S(1)}, bf16[64,768]{1,0:T(8,128)(2,1)S(1)}, u32[]{:S(2)}, u32[]{:S(2)}) collective-permute-start(bf16[64,768]{1,0:T(8,128)(2,1)S(1)} %get-tuple-element.37), channel_id=1, source_target_pairs={{0,2},{1,5},{2,0},{3,7},{4,6},{5,1},{6,4},{7,3},{8,10},{9,13},{10,... | collective-permute-start | bytes 294920 | tf_op jit(solution)/shard_map/ppermute | solution.py:278
  14.5 1.4 %collective-permute-done.5 = bf16[64,1280]{1,0:T(8,128)(2,1)S(1)} collective-permute-done((bf16[64,1280]{1,0:T(8,128)(2,1)S(1)}, bf16[64,1280]{1,0:T(8,128)(2,1)S(1)}, u32[]{:S(2)}, u32[]{:S(2)}) %collective-permute-start.5) | collective-permute-done | bytes 163872 | tf_op jit(solution)/shard_map/ppermute | solution.py:278
  16.0 1.8 %collective-permute-start.6 = (bf16[64,1280]{1,0:T(8,128)(2,1)S(1)}, bf16[64,1280]{1,0:T(8,128)(2,1)S(1)}, u32[]{:S(2)}, u32[]{:S(2)}) collective-permute-start(bf16[64,1280]{1,0:T(8,128)(2,1)S(1)} %fusion), channel_id=1, source_target_pairs={{0,4},{1,9},{2,6},{3,11},{4,0},{5,13},{6,2},{7,15},{8,12},{9,1},{1... | collective-permute-start | bytes 491528 | tf_op jit(solution)/shard_map/ppermute | solution.py:278
  17.8 1.1 %collective-permute-done.2 = bf16[64,768]{1,0:T(8,128)(2,1)S(1)} collective-permute-done((bf16[64,768]{1,0:T(8,128)(2,1)S(1)}, bf16[64,768]{1,0:T(8,128)(2,1)S(1)}, u32[]{:S(2)}, u32[]{:S(2)}) %collective-permute-start.2) | collective-permute-done | bytes 98336 | tf_op jit(solution)/shard_map/ppermute | solution.py:278
  18.8 1.6 %collective-permute-start.3 = (bf16[64,768]{1,0:T(8,128)(2,1)S(1)}, bf16[64,768]{1,0:T(8,128)(2,1)S(1)}, u32[]{:S(2)}, u32[]{:S(2)}) collective-permute-start(bf16[64,768]{1,0:T(8,128)(2,1)S(1)} %fusion.1), channel_id=1, source_target_pairs={{0,4},{1,9},{2,6},{3,11},{4,0},{5,13},{6,2},{7,15},{8,12},{9,1},{1... | collective-permute-start | bytes 294920 | tf_op jit(solution)/shard_map/ppermute | solution.py:278
  20.4 0.9 %collective-permute-done.6 = bf16[64,1280]{1,0:T(8,128)(2,1)S(1)} collective-permute-done((bf16[64,1280]{1,0:T(8,128)(2,1)S(1)}, bf16[64,1280]{1,0:T(8,128)(2,1)S(1)}, u32[]{:S(2)}, u32[]{:S(2)}) %collective-permute-start.6) | collective-permute-done | bytes 163872 | tf_op jit(solution)/shard_map/ppermute | solution.py:278
  21.4 1.6 %collective-permute-start.7 = (bf16[64,1280]{1,0:T(8,128)(2,1)S(1)}, bf16[64,1280]{1,0:T(8,128)(2,1)S(1)}, u32[]{:S(2)}, u32[]{:S(2)}) collective-permute-start(bf16[64,1280]{1,0:T(8,128)(2,1)S(1)} %get-tuple-element.47), channel_id=1, source_target_pairs={{0,8},{1,3},{2,10},{3,1},{4,12},{5,7},{6,14},{7,5},{8,0},{9,11},{1... | collective-permute-start | bytes 491528 | tf_op jit(solution)/shard_map/ppermute | solution.py:278
  23.0 0.5 %collective-permute-done.3 = bf16[64,768]{1,0:T(8,128)(2,1)S(1)} collective-permute-done((bf16[64,768]{1,0:T(8,128)(2,1)S(1)}, bf16[64,768]{1,0:T(8,128)(2,1)S(1)}, u32[]{:S(2)}, u32[]{:S(2)}) %collective-permute-start.3) | collective-permute-done | bytes 98336 | tf_op jit(solution)/shard_map/ppermute | solution.py:278
  23.6 1.4 %collective-permute-start.4 = (bf16[64,768]{1,0:T(8,128)(2,1)S(1)}, bf16[64,768]{1,0:T(8,128)(2,1)S(1)}, u32[]{:S(2)}, u32[]{:S(2)}) collective-permute-start(bf16[64,768]{1,0:T(8,128)(2,1)S(1)} %get-tuple-element.49), channel_id=1, source_target_pairs={{0,8},{1,3},{2,10},{3,1},{4,12},{5,7},{6,14},{7,5},{8,0},{9,11},{1... | collective-permute-start | bytes 294920 | tf_op jit(solution)/shard_map/ppermute | solution.py:278
  25.0 1.8 %collective-permute-done.7.recv_ref = bf16[64,1280]{1,0:T(8,128)(2,1)S(1)} collective-permute-done((bf16[64,1280]{1,0:T(8,128)(2,1)S(1)}, bf16[64,1280]{1,0:T(8,128)(2,1)S(1)}, u32[]{:S(2)}, u32[]{:S(2)}) %collective-permute-start.7) | collective-permute-done | bytes 163872 | tf_op jit(solution)/shard_map/ppermute | solution.py:278
  26.8 1.0 %back.2.refs_2_ = f32[48,1024]{1,0:T(8,128)S(1)} custom-call(f32[64,1280]{1,0:T(8,128)S(1)} %get-tuple-element.48.acc_ref, bf16[64,1280]{1,0:T(8,128)(2,1)S(1)} %collective-permute-done.7.recv_ref, f32[8,2048]{1,0:T(8,128)S(1)} %get-tuple-element.32.frame_ref, bf16[2,2048,256]{2,1,0:T(8,128)(2,1)S(1)} %get-tuple-element.38.refs_0_, ...), custom_call_target="tpu_custom_call" | custom-call | flops 251658240 | bytes 983040 | tf_op jit(solution)/shard_map/back/pallas_call | solution.py:292
  27.8 0.5 %collective-permute-done.4.recv_ref = bf16[64,768]{1,0:T(8,128)(2,1)S(1)} collective-permute-done((bf16[64,768]{1,0:T(8,128)(2,1)S(1)}, bf16[64,768]{1,0:T(8,128)(2,1)S(1)}, u32[]{:S(2)}, u32[]{:S(2)}) %collective-permute-start.4) | collective-permute-done | bytes 98336 | tf_op jit(solution)/shard_map/ppermute | solution.py:278
  28.2 0.6 %back.3 = (f32[48,512]{1,0:T(8,128)S(1)}, bf16[48,512]{1,0:T(8,128)(2,1)S(1)}) custom-call(f32[64,768]{1,0:T(8,128)S(1)} %get-tuple-element.50.acc_ref, bf16[64,768]{1,0:T(8,128)(2,1)S(1)} %collective-permute-done.4.recv_ref, f32[8,2048]{1,0:T(8,128)S(1)} %get-tuple-element.32.frame_ref, bf16[2,2048,256]{2,1,0:T(8,128)(2,1)S(1)} %get-tuple-element.38.refs_0_, ...), custom_call_target="tpu_custom_call" | custom-call | flops 150994944 | bytes 589824 | tf_op jit(solution)/shard_map/back/pallas_call | solution.py:295
  29.0 1.2 %collective-permute-done.8 = bf16[48,512]{1,0:T(8,128)(2,1)S(1)} collective-permute-done((bf16[48,512]{1,0:T(8,128)(2,1)S(1)}, bf16[48,512]{1,0:T(8,128)(2,1)S(1)}, u32[]{:S(2)}, u32[]{:S(2)}) %collective-permute-start.8) | collective-permute-done | bytes 49184 | tf_op jit(solution)/shard_map/ppermute | solution.py:228
  30.2 2.4 %collective-permute-start.9 = (bf16[48,256]{1,0:T(8,128)(2,1)S(1)}, bf16[48,256]{1,0:T(8,128)(2,1)S(1)}, u32[]{:S(2)}, u32[]{:S(2)}) collective-permute-start(bf16[48,256]{1,0:T(8,128)(2,1)S(1)} %slice.13), channel_id=1, source_target_pairs={{0,16},{1,17},{2,18},{3,19},{4,20},{5,21},{6,22},{7,23},{8,24},{9,... | collective-permute-start | bytes 73736 | tf_op jit(solution)/shard_map/ppermute | solution.py:228
  32.7 2.4 %collective-permute-done.9 = bf16[48,256]{1,0:T(8,128)(2,1)S(1)} collective-permute-done((bf16[48,256]{1,0:T(8,128)(2,1)S(1)}, bf16[48,256]{1,0:T(8,128)(2,1)S(1)}, u32[]{:S(2)}, u32[]{:S(2)}) %collective-permute-start.9) | collective-permute-done | bytes 24608 | tf_op jit(solution)/shard_map/ppermute | solution.py:228
  35.0 0.6 %slice_add_fusion = f32[48,256]{1,0:T(8,128)} fusion(f32[48,512]{1,0:T(8,128)S(1)} %convert_add_fusion.4, bf16[48,256]{1,0:T(8,128)(2,1)S(1)} %collective-permute-done.9), kind=kLoop, calls=%fused_computation.9 | loop fusion | flops 24576 | bytes 122880 | tf_op jit(solution)/shard_map/add | solution.py:305
  (12 shorter events, 1.0 us)
Async XLA Ops:
  0.9 6.4 %collective-permute-start = (bf16[64,256]{1,0:T(8,128)(2,1)S(1)}, bf16[64,256]{1,0:T(8,128)(2,1)S(1)}, u32[]{:S(2)}, u32[]{:S(2)}) collective-permute-start(bf16[64,256]{1,0:T(8,128)(2,1)S(1)} %get-tuple-element.26.pack_ref), channel_id=1, source_target_pairs={{0,16},{1,17},{2,18},{3,19},{4,20},{5,21},{6,22},{7,23},{8,24},{9,... | collective-permute-start | bytes 98312 | tf_op jit(solution)/shard_map/ppermute | solution.py:228
  7.3 1.3 %collective-permute-start.1 = (bf16[2,64,256]{2,1,0:T(8,128)(2,1)S(1)}, bf16[2,64,256]{2,1,0:T(8,128)(2,1)S(1)}, u32[]{:S(2)}, u32[]{:S(2)}) collective-permute-start(bf16[2,64,256]{2,1,0:T(8,128)(2,1)S(1)} %pad_maximum_fusion), channel_id=1, source_target_pairs={{0,1},{1,0},{2,3},{3,2},{4,5},{5,4},{6,7},{7,6},{8,9},{9,8},{10,11... | collective-permute-start | bytes 196616 | tf_op jit(solution)/shard_map/ppermute | solution.py:228
  10.5 5.4 %collective-permute-start.5 = (bf16[64,1280]{1,0:T(8,128)(2,1)S(1)}, bf16[64,1280]{1,0:T(8,128)(2,1)S(1)}, u32[]{:S(2)}, u32[]{:S(2)}) collective-permute-start(bf16[64,1280]{1,0:T(8,128)(2,1)S(1)} %get-tuple-element.42), channel_id=1, source_target_pairs={{0,2},{1,5},{2,0},{3,7},{4,6},{5,1},{6,4},{7,3},{8,10},{9,13},{10,... | collective-permute-start | bytes 491528 | tf_op jit(solution)/shard_map/ppermute | solution.py:278
  14.1 4.7 %collective-permute-start.2 = (bf16[64,768]{1,0:T(8,128)(2,1)S(1)}, bf16[64,768]{1,0:T(8,128)(2,1)S(1)}, u32[]{:S(2)}, u32[]{:S(2)}) collective-permute-start(bf16[64,768]{1,0:T(8,128)(2,1)S(1)} %get-tuple-element.37), channel_id=1, source_target_pairs={{0,2},{1,5},{2,0},{3,7},{4,6},{5,1},{6,4},{7,3},{8,10},{9,13},{10,... | collective-permute-start | bytes 294920 | tf_op jit(solution)/shard_map/ppermute | solution.py:278
  16.0 5.4 %collective-permute-start.6 = (bf16[64,1280]{1,0:T(8,128)(2,1)S(1)}, bf16[64,1280]{1,0:T(8,128)(2,1)S(1)}, u32[]{:S(2)}, u32[]{:S(2)}) collective-permute-start(bf16[64,1280]{1,0:T(8,128)(2,1)S(1)} %fusion), channel_id=1, source_target_pairs={{0,4},{1,9},{2,6},{3,11},{4,0},{5,13},{6,2},{7,15},{8,12},{9,1},{1... | collective-permute-start | bytes 491528 | tf_op jit(solution)/shard_map/ppermute | solution.py:278
  18.8 4.7 %collective-permute-start.3 = (bf16[64,768]{1,0:T(8,128)(2,1)S(1)}, bf16[64,768]{1,0:T(8,128)(2,1)S(1)}, u32[]{:S(2)}, u32[]{:S(2)}) collective-permute-start(bf16[64,768]{1,0:T(8,128)(2,1)S(1)} %fusion.1), channel_id=1, source_target_pairs={{0,4},{1,9},{2,6},{3,11},{4,0},{5,13},{6,2},{7,15},{8,12},{9,1},{1... | collective-permute-start | bytes 294920 | tf_op jit(solution)/shard_map/ppermute | solution.py:278
  21.4 5.4 %collective-permute-start.7 = (bf16[64,1280]{1,0:T(8,128)(2,1)S(1)}, bf16[64,1280]{1,0:T(8,128)(2,1)S(1)}, u32[]{:S(2)}, u32[]{:S(2)}) collective-permute-start(bf16[64,1280]{1,0:T(8,128)(2,1)S(1)} %get-tuple-element.47), channel_id=1, source_target_pairs={{0,8},{1,3},{2,10},{3,1},{4,12},{5,7},{6,14},{7,5},{8,0},{9,11},{1... | collective-permute-start | bytes 491528 | tf_op jit(solution)/shard_map/ppermute | solution.py:278
  23.6 4.7 %collective-permute-start.4 = (bf16[64,768]{1,0:T(8,128)(2,1)S(1)}, bf16[64,768]{1,0:T(8,128)(2,1)S(1)}, u32[]{:S(2)}, u32[]{:S(2)}) collective-permute-start(bf16[64,768]{1,0:T(8,128)(2,1)S(1)} %get-tuple-element.49), channel_id=1, source_target_pairs={{0,8},{1,3},{2,10},{3,1},{4,12},{5,7},{6,14},{7,5},{8,0},{9,11},{1... | collective-permute-start | bytes 294920 | tf_op jit(solution)/shard_map/ppermute | solution.py:278
  28.9 1.3 %collective-permute-start.8 = (bf16[48,512]{1,0:T(8,128)(2,1)S(1)}, bf16[48,512]{1,0:T(8,128)(2,1)S(1)}, u32[]{:S(2)}, u32[]{:S(2)}) collective-permute-start(bf16[48,512]{1,0:T(8,128)(2,1)S(1)} %get-tuple-element.46), channel_id=1, source_target_pairs={{0,1},{1,0},{2,3},{3,2},{4,5},{5,4},{6,7},{7,6},{8,9},{9,8},{10,11... | collective-permute-start | bytes 147464 | tf_op jit(solution)/shard_map/ppermute | solution.py:228
  30.2 4.8 %collective-permute-start.9 = (bf16[48,256]{1,0:T(8,128)(2,1)S(1)}, bf16[48,256]{1,0:T(8,128)(2,1)S(1)}, u32[]{:S(2)}, u32[]{:S(2)}) collective-permute-start(bf16[48,256]{1,0:T(8,128)(2,1)S(1)} %slice.13), channel_id=1, source_target_pairs={{0,16},{1,17},{2,18},{3,19},{4,20},{5,21},{6,22},{7,23},{8,24},{9,... | collective-permute-start | bytes 73736 | tf_op jit(solution)/shard_map/ppermute | solution.py:228

commit v9 on v8

--- a/solution.py
+++ b/solution.py
@@ -239,6 +239,7 @@
         "shhh",
         scratch=[VMEM(positions.shape, f32), VMEM(forces.shape, f32), pltpu.SemaphoreType.DMA((3,))],
     )(block.reshape(1), *(pltpu.with_memory_space_constraint(x, pltpu.HBM) for x in (positions, forces, waves)))
+    near = swap(own, 1)
     far = swap(own, top)
     frame, wt = call(
         functools.partial(frame_kernel, amp), (shape((8, mine), f32), shape((mine, HEAD), bf16)), "frame", "v", flops=mine * 1000
@@ -255,10 +256,11 @@
         )(wt, *operands)
 
     tab_own, raw = trig_call("trig_own", 0, mine, own)
-    both, tab_own, raw, frame, wt = lax.optimization_barrier((jnp.stack([own, far]), tab_own, raw, frame, wt))
-    near = swap(both, 1)
     split = mine * 5 // 8 // 256 * 256
     parts = (split, mine - split)
+    tab_near, raw_a = trig_call("trig_near", 0, split, near, raw)
+    away, tab_near, raw_a = lax.optimization_barrier((far, tab_near, raw_a))
+    across = swap(away, 1)
 
     def sums(first, count, start, raw, todo, width):
         return call(
@@ -277,9 +279,9 @@
         turn = [middle[(j + core) % steps] for core in range(2)]
         return lax.ppermute(x, AXES, [(d, d ^ turn[d % 2]) for d in range(devices)])
 
-    tab_far, raw_a = trig_call("trig_far", 0, split, far, raw)
-    tab_a, acc_a, send_a = sums(0, parts[0], 0, raw_a, (near,), 2 * rows)
-    tab_b, acc_b, send_b = sums(split, parts[1], split, raw, (far, near), 3 * rows)
+    tab_far, raw_a = trig_call("trig_far", 0, split, far, raw_a)
+    tab_a, acc_a, send_a = sums(0, parts[0], 0, raw_a, (across,), rows)
+    tab_b, acc_b, send_b = sums(split, parts[1], split, raw, (far, near, across), 3 * rows)
     state = [[acc_a, send_a, None], [acc_b, send_b, None]]
     for j in range(steps):
         for chunk in range(2):
@@ -290,8 +292,8 @@
                 send = acc.astype(bf16)
             state[chunk] = [acc, send, got]
     first = call(
-        functools.partial(back_kernel, 0, (0, 0, 0), 256, False), shape((half, 4 * rows), f32), "back", "vvvvvv", flops=parts[0] * fl * 4
-    )(state[0][0], state[0][2], frame, tab_own, tab_far, tab_a)
+        functools.partial(back_kernel, 0, (0, 0, 0, 0), 256, False), shape((half, 4 * rows), f32), "back", "vvvvvvv", flops=parts[0] * fl * 4
+    )(state[0][0], state[0][2], frame, tab_own, tab_far, tab_near, tab_a)
     keep, send = call(
         functools.partial(back_kernel, split, (split, 0), 256, True),
         (shape((half, 2 * rows), f32), shape((half, 2 * rows), bf16)),

time: 35.8 us -> 35.8 us (level)
  starting transfers between devices: 15.3 us -> 14.9 us
  Pallas kernels: 9.31 us -> 9.67 us
    pallas_call x2 -> x3, Pallas kernels: 2.79 us -> 3.92 us  [trig_call(): call(functools.partial(trig_kernel, first), (shape((2, count, rows), bf16...]
    pallas_call x2, Pallas kernels: 3.79 us -> 3.02 us  [sums(): call(functools.partial(sums_kernel, first, start), (shape((2, count, widt...]
    ppermute x4 -> x5, starting transfers between devices: 6.72 us -> 6.29 us  [swap(): return lax.ppermute(x, AXES, [(d, d ^ bit) for d in range(devices)])]
    ppermute x4 -> x5, waiting for transfers between devices: 4.02 us -> 4.24 us  [swap(): return lax.ppermute(x, AXES, [(d, d ^ bit) for d in range(devices)])]
  transfers between devices with their start and end apart: 10 -> 11, of which waited for: 10 -> 8; matrix products, arithmetic and copies ran while one was open for 0% -> 0% of each run, Pallas kernels for 16% -> 20%
where the time goes in v9:
time: 35.8 us; the launch traced here: 35.6 us
  starting transfers between devices  14.9 us (42%)
  waiting for transfers between devices  10.1 us (28%)
  Pallas kernels  9.67 us (27%)
  other arithmetic  0.77 us (2%)
    ppermute x6, starting transfers between devices, exchange(): return lax.ppermute(x, AXES, [(d, d ^ turn[d % 2]) for d in range(devices)])  8.61 us
    ppermute x5, starting transfers between devices, swap(): return lax.ppermute(x, AXES, [(d, d ^ bit) for d in range(devices)])  6.29 us
    ppermute x6, waiting for transfers between devices, exchange(): return lax.ppermute(x, AXES, [(d, d ^ turn[d % 2]) for d in range(devices)])  5.9 us
    ppermute x5, waiting for transfers between devices, swap(): return lax.ppermute(x, AXES, [(d, d ^ bit) for d in range(devices)])  4.24 us
    pallas_call x3, Pallas kernels, trig_call(): call(functools.partial(trig_kernel, first), (shape((2, count, rows), bf16...  3.92 us
    pallas_call x2, Pallas kernels, sums(): call(functools.partial(sums_kernel, first, start), (shape((2, count, widt...  3.02 us
    pallas_call x1, Pallas kernels, shards(): call(functools.partial(back_kernel, 0, (0, 0, 0, 0), 256, False), shape((...  0.99 us
    pallas_call x1, Pallas kernels, shards(): call(pack_kernel, (shape((HEAD + half, rows), bf16), shape((3, mine), jnp...  0.86 us
  transfers between devices with their start and end apart: 11, of which 8 were waited for; matrix products, arithmetic and copies ran while one was open for 0% of the time, Pallas kernels for 20%

profile of v9, /device:TPU:0, one launch (start us, length us, event | category | flops | bytes accessed | tf_op | source)
XLA Modules:
  0.0 35.6 jit_solution(3631752133964591715)
XLA Ops:
  0.0 0.9 %pack.1 = (bf16[64,256]{1,0:T(8,128)(2,1)S(1)}, s32[3,2048]{1,0:T(4,128)S(1)}) custom-call(s32[1]{0:T(128)} %bitcast.idx_ref, f32[3,256]{1,0:T(4,128)} %pos_hbm.1, f32[3,16,256]{2,1,0:T(8,128)} %force_hbm.1, s32[3,8192]{1,0:T(4,128)} %waves_hbm.1), custom_call_target="tpu_custom_call" | custom-call | tf_op jit(solution)/shard_map/pack/pallas_call | solution.py:235
  0.9 0.6 %collective-permute-start.1 = (bf16[64,256]{1,0:T(8,128)(2,1)S(1)}, bf16[64,256]{1,0:T(8,128)(2,1)S(1)}, u32[]{:S(2)}, u32[]{:S(2)}) collective-permute-start(bf16[64,256]{1,0:T(8,128)(2,1)S(1)} %get-tuple-element.29.pack_ref), channel_id=1, source_target_pairs={{0,1},{1,0},{2,3},{3,2},{4,5},{5,4},{6,7},{7,6},{8,9},{9,8},{10,11... | collective-permute-start | bytes 98312 | tf_op jit(solution)/shard_map/ppermute | solution.py:228
  1.4 3.7 %collective-permute-start = (bf16[64,256]{1,0:T(8,128)(2,1)S(1)}, bf16[64,256]{1,0:T(8,128)(2,1)S(1)}, u32[]{:S(2)}, u32[]{:S(2)}) collective-permute-start(bf16[64,256]{1,0:T(8,128)(2,1)S(1)} %get-tuple-element.29.pack_ref), channel_id=1, source_target_pairs={{0,16},{1,17},{2,18},{3,19},{4,20},{5,21},{6,22},{7,23},{8,24},{9,... | collective-permute-start | bytes 98312 | tf_op jit(solution)/shard_map/ppermute | solution.py:228
  5.3 1.7 %trig_own.1 = (bf16[2,2048,256]{2,1,0:T(8,128)(2,1)S(1)}, f32[96,2048]{1,0:T(8,128)S(1)}) custom-call(bf16[2048,16]{1,0:T(8,128)(2,1)S(1)} %get-tuple-element.28.wt_ref, bf16[64,256]{1,0:T(8,128)(2,1)S(1)} %get-tuple-element.29.pack_ref), custom_call_target="tpu_custom_call" | custom-call | flops 100663296 | bytes 393216 | tf_op jit(solution)/shard_map/trig_own/pallas_call | solution.py:249
  7.0 1.1 %trig_near.1 = (bf16[2,1280,256]{2,1,0:T(8,128)(2,1)S(1)}, f32[96,1280]{1,0:T(8,128)S(1)}) custom-call(bf16[2048,16]{1,0:T(8,128)(2,1)S(1)} %get-tuple-element.28.wt_ref, bf16[64,256]{1,0:T(8,128)(2,1)S(1)} %collective-permute-done.1.pack_ref.refs_1_, f32[96,2048]{1,0:T(8,128)S(1)} %get-tuple-element.30.refs_0_.raw_ref), custom_call_target="tpu_custom_call" | custom-call | flops 62914560 | bytes 245760 | tf_op jit(solution)/shard_map/trig_near/pallas_call | solution.py:249
  8.4 1.1 %trig_far.1 = (bf16[2,1280,256]{2,1,0:T(8,128)(2,1)S(1)}, f32[96,1280]{1,0:T(8,128)S(1)}) custom-call(bf16[2048,16]{1,0:T(8,128)(2,1)S(1)} %get-tuple-element.28.wt_ref, bf16[64,256]{1,0:T(8,128)(2,1)S(1)} %collective-permute-done.refs_0_.pack_ref, f32[96,1280]{1,0:T(8,128)S(1)} %get-tuple-element.38.refs_0_), custom_call_target="tpu_custom_call" | custom-call | flops 62914560 | bytes 245760 | tf_op jit(solution)/shard_map/trig_far/pallas_call | solution.py:249
  9.5 1.2 %sums.3 = (bf16[2,1280,256]{2,1,0:T(8,128)(2,1)S(1)}, f32[64,1280]{1,0:T(8,128)S(1)}, bf16[64,1280]{1,0:T(8,128)(2,1)S(1)}) custom-call(f32[8,2048]{1,0:T(8,128)S(1)} %get-tuple-element.27.frame_ref, bf16[2048,16]{1,0:T(8,128)(2,1)S(1)} %get-tuple-element.28.wt_ref, f32[96,1280]{1,0:T(8,128)S(1)} %get-tuple-element.39.raw_ref, ...), custom_call_target="tpu_custom_call" | custom-call | flops 62914560 | bytes 245760 | tf_op jit(solution)/shard_map/sums/pallas_call | solution.py:266
  10.7 1.6 %collective-permute-start.6 = (bf16[64,1280]{1,0:T(8,128)(2,1)S(1)}, bf16[64,1280]{1,0:T(8,128)(2,1)S(1)}, u32[]{:S(2)}, u32[]{:S(2)}) collective-permute-start(bf16[64,1280]{1,0:T(8,128)(2,1)S(1)} %get-tuple-element.41), channel_id=1, source_target_pairs={{0,2},{1,5},{2,0},{3,7},{4,6},{5,1},{6,4},{7,3},{8,10},{9,13},{10,... | collective-permute-start | bytes 491528 | tf_op jit(solution)/shard_map/ppermute | solution.py:280
  12.2 1.8 %sums.2 = (bf16[2,768,768]{2,1,0:T(8,128)(2,1)S(1)}, f32[64,768]{1,0:T(8,128)S(1)}, bf16[64,768]{1,0:T(8,128)(2,1)S(1)}) custom-call(f32[8,2048]{1,0:T(8,128)S(1)} %get-tuple-element.27.frame_ref, bf16[2048,16]{1,0:T(8,128)(2,1)S(1)} %get-tuple-element.28.wt_ref, f32[96,2048]{1,0:T(8,128)S(1)} %get-tuple-element.30.refs_0_.raw_ref, ...), custom_call_target="tpu_custom_call" | custom-call | flops 113246208 | bytes 442368 | tf_op jit(solution)/shard_map/sums/pallas_call | solution.py:266
  14.1 0.6 %collective-permute-start.3 = (bf16[64,768]{1,0:T(8,128)(2,1)S(1)}, bf16[64,768]{1,0:T(8,128)(2,1)S(1)}, u32[]{:S(2)}, u32[]{:S(2)}) collective-permute-start(bf16[64,768]{1,0:T(8,128)(2,1)S(1)} %get-tuple-element.35), channel_id=1, source_target_pairs={{0,2},{1,5},{2,0},{3,7},{4,6},{5,1},{6,4},{7,3},{8,10},{9,13},{10,... | collective-permute-start | bytes 294920 | tf_op jit(solution)/shard_map/ppermute | solution.py:280
  14.7 1.4 %collective-permute-done.6 = bf16[64,1280]{1,0:T(8,128)(2,1)S(1)} collective-permute-done((bf16[64,1280]{1,0:T(8,128)(2,1)S(1)}, bf16[64,1280]{1,0:T(8,128)(2,1)S(1)}, u32[]{:S(2)}, u32[]{:S(2)}) %collective-permute-start.6) | collective-permute-done | bytes 163872 | tf_op jit(solution)/shard_map/ppermute | solution.py:280
  16.1 1.6 %collective-permute-start.7 = (bf16[64,1280]{1,0:T(8,128)(2,1)S(1)}, bf16[64,1280]{1,0:T(8,128)(2,1)S(1)}, u32[]{:S(2)}, u32[]{:S(2)}) collective-permute-start(bf16[64,1280]{1,0:T(8,128)(2,1)S(1)} %fusion), channel_id=1, source_target_pairs={{0,4},{1,9},{2,6},{3,11},{4,0},{5,13},{6,2},{7,15},{8,12},{9,1},{1... | collective-permute-start | bytes 491528 | tf_op jit(solution)/shard_map/ppermute | solution.py:280
  17.7 1.1 %collective-permute-done.3 = bf16[64,768]{1,0:T(8,128)(2,1)S(1)} collective-permute-done((bf16[64,768]{1,0:T(8,128)(2,1)S(1)}, bf16[64,768]{1,0:T(8,128)(2,1)S(1)}, u32[]{:S(2)}, u32[]{:S(2)}) %collective-permute-start.3) | collective-permute-done | bytes 98336 | tf_op jit(solution)/shard_map/ppermute | solution.py:280
  18.8 1.6 %collective-permute-start.4 = (bf16[64,768]{1,0:T(8,128)(2,1)S(1)}, bf16[64,768]{1,0:T(8,128)(2,1)S(1)}, u32[]{:S(2)}, u32[]{:S(2)}) collective-permute-start(bf16[64,768]{1,0:T(8,128)(2,1)S(1)} %fusion.1), channel_id=1, source_target_pairs={{0,4},{1,9},{2,6},{3,11},{4,0},{5,13},{6,2},{7,15},{8,12},{9,1},{1... | collective-permute-start | bytes 294920 | tf_op jit(solution)/shard_map/ppermute | solution.py:280
  20.4 1.1 %collective-permute-done.7 = bf16[64,1280]{1,0:T(8,128)(2,1)S(1)} collective-permute-done((bf16[64,1280]{1,0:T(8,128)(2,1)S(1)}, bf16[64,1280]{1,0:T(8,128)(2,1)S(1)}, u32[]{:S(2)}, u32[]{:S(2)}) %collective-permute-start.7) | collective-permute-done | bytes 163872 | tf_op jit(solution)/shard_map/ppermute | solution.py:280
  21.5 1.6 %collective-permute-start.8 = (bf16[64,1280]{1,0:T(8,128)(2,1)S(1)}, bf16[64,1280]{1,0:T(8,128)(2,1)S(1)}, u32[]{:S(2)}, u32[]{:S(2)}) collective-permute-start(bf16[64,1280]{1,0:T(8,128)(2,1)S(1)} %get-tuple-element.47), channel_id=1, source_target_pairs={{0,8},{1,3},{2,10},{3,1},{4,12},{5,7},{6,14},{7,5},{8,0},{9,11},{1... | collective-permute-start | bytes 491528 | tf_op jit(solution)/shard_map/ppermute | solution.py:280
  23.5 1.6 %collective-permute-start.5 = (bf16[64,768]{1,0:T(8,128)(2,1)S(1)}, bf16[64,768]{1,0:T(8,128)(2,1)S(1)}, u32[]{:S(2)}, u32[]{:S(2)}) collective-permute-start(bf16[64,768]{1,0:T(8,128)(2,1)S(1)} %get-tuple-element.49), channel_id=1, source_target_pairs={{0,8},{1,3},{2,10},{3,1},{4,12},{5,7},{6,14},{7,5},{8,0},{9,11},{1... | collective-permute-start | bytes 294920 | tf_op jit(solution)/shard_map/ppermute | solution.py:280
  25.1 1.8 %collective-permute-done.8.recv_ref = bf16[64,1280]{1,0:T(8,128)(2,1)S(1)} collective-permute-done((bf16[64,1280]{1,0:T(8,128)(2,1)S(1)}, bf16[64,1280]{1,0:T(8,128)(2,1)S(1)}, u32[]{:S(2)}, u32[]{:S(2)}) %collective-permute-start.8) | collective-permute-done | bytes 163872 | tf_op jit(solution)/shard_map/ppermute | solution.py:280
  26.9 1.0 %back.2.refs_2_ = f32[48,1024]{1,0:T(8,128)S(1)} custom-call(f32[64,1280]{1,0:T(8,128)S(1)} %get-tuple-element.48.acc_ref, bf16[64,1280]{1,0:T(8,128)(2,1)S(1)} %collective-permute-done.8.recv_ref, f32[8,2048]{1,0:T(8,128)S(1)} %get-tuple-element.27.frame_ref, bf16[2,2048,256]{2,1,0:T(8,128)(2,1)S(1)} %get-tuple-element.36.refs_0_, ...), custom_call_target="tpu_custom_call" | custom-call | flops 251658240 | bytes 983040 | tf_op jit(solution)/shard_map/back/pallas_call | solution.py:294
  28.2 0.6 %back.3 = (f32[48,512]{1,0:T(8,128)S(1)}, bf16[48,512]{1,0:T(8,128)(2,1)S(1)}) custom-call(f32[64,768]{1,0:T(8,128)S(1)} %get-tuple-element.50.acc_ref, bf16[64,768]{1,0:T(8,128)(2,1)S(1)} %collective-permute-done.5.recv_ref, f32[8,2048]{1,0:T(8,128)S(1)} %get-tuple-element.27.frame_ref, bf16[2,2048,256]{2,1,0:T(8,128)(2,1)S(1)} %get-tuple-element.36.refs_0_, ...), custom_call_target="tpu_custom_call" | custom-call | flops 150994944 | bytes 589824 | tf_op jit(solution)/shard_map/back/pallas_call | solution.py:297
  28.9 1.2 %collective-permute-done.9 = bf16[48,512]{1,0:T(8,128)(2,1)S(1)} collective-permute-done((bf16[48,512]{1,0:T(8,128)(2,1)S(1)}, bf16[48,512]{1,0:T(8,128)(2,1)S(1)}, u32[]{:S(2)}, u32[]{:S(2)}) %collective-permute-start.9) | collective-permute-done | bytes 49184 | tf_op jit(solution)/shard_map/ppermute | solution.py:228
  30.2 1.8 %collective-permute-start.10 = (bf16[48,256]{1,0:T(8,128)(2,1)S(1)}, bf16[48,256]{1,0:T(8,128)(2,1)S(1)}, u32[]{:S(2)}, u32[]{:S(2)}) collective-permute-start(bf16[48,256]{1,0:T(8,128)(2,1)S(1)} %slice.13), channel_id=1, source_target_pairs={{0,16},{1,17},{2,18},{3,19},{4,20},{5,21},{6,22},{7,23},{8,24},{9,... | collective-permute-start | bytes 73736 | tf_op jit(solution)/shard_map/ppermute | solution.py:228
  32.0 3.0 %collective-permute-done.10 = bf16[48,256]{1,0:T(8,128)(2,1)S(1)} collective-permute-done((bf16[48,256]{1,0:T(8,128)(2,1)S(1)}, bf16[48,256]{1,0:T(8,128)(2,1)S(1)}, u32[]{:S(2)}, u32[]{:S(2)}) %collective-permute-start.10) | collective-permute-done | bytes 24608 | tf_op jit(solution)/shard_map/ppermute | solution.py:228
  35.0 0.6 %slice_add_fusion = f32[48,256]{1,0:T(8,128)} fusion(f32[48,512]{1,0:T(8,128)S(1)} %convert_add_fusion.4, bf16[48,256]{1,0:T(8,128)(2,1)S(1)} %collective-permute-done.10), kind=kLoop, calls=%fused_computation.8 | loop fusion | flops 24576 | bytes 122880 | tf_op jit(solution)/shard_map/add | solution.py:307
  (14 shorter events, 1.2 us)
Async XLA Ops:
  0.9 6.1 %collective-permute-start.1 = (bf16[64,256]{1,0:T(8,128)(2,1)S(1)}, bf16[64,256]{1,0:T(8,128)(2,1)S(1)}, u32[]{:S(2)}, u32[]{:S(2)}) collective-permute-start(bf16[64,256]{1,0:T(8,128)(2,1)S(1)} %get-tuple-element.29.pack_ref), channel_id=1, source_target_pairs={{0,1},{1,0},{2,3},{3,2},{4,5},{5,4},{6,7},{7,6},{8,9},{9,8},{10,11... | collective-permute-start | bytes 98312 | tf_op jit(solution)/shard_map/ppermute | solution.py:228
  1.4 6.7 %collective-permute-start = (bf16[64,256]{1,0:T(8,128)(2,1)S(1)}, bf16[64,256]{1,0:T(8,128)(2,1)S(1)}, u32[]{:S(2)}, u32[]{:S(2)}) collective-permute-start(bf16[64,256]{1,0:T(8,128)(2,1)S(1)} %get-tuple-element.29.pack_ref), channel_id=1, source_target_pairs={{0,16},{1,17},{2,18},{3,19},{4,20},{5,21},{6,22},{7,23},{8,24},{9,... | collective-permute-start | bytes 98312 | tf_op jit(solution)/shard_map/ppermute | solution.py:228
  8.1 1.4 %collective-permute-start.2 = (bf16[64,256]{1,0:T(8,128)(2,1)S(1)}, bf16[64,256]{1,0:T(8,128)(2,1)S(1)}, u32[]{:S(2)}, u32[]{:S(2)}) collective-permute-start(bf16[64,256]{1,0:T(8,128)(2,1)S(1)} %collective-permute-done.refs_0_.pack_ref), channel_id=1, source_target_pairs={{0,1},{1,0},{2,3},{3,2},{4,5},{5,4},{6,7},{7,6},{8,9},{9,8},{10,11... | collective-permute-start | bytes 98312 | tf_op jit(solution)/shard_map/ppermute | solution.py:228
  10.7 5.4 %collective-permute-start.6 = (bf16[64,1280]{1,0:T(8,128)(2,1)S(1)}, bf16[64,1280]{1,0:T(8,128)(2,1)S(1)}, u32[]{:S(2)}, u32[]{:S(2)}) collective-permute-start(bf16[64,1280]{1,0:T(8,128)(2,1)S(1)} %get-tuple-element.41), channel_id=1, source_target_pairs={{0,2},{1,5},{2,0},{3,7},{4,6},{5,1},{6,4},{7,3},{8,10},{9,13},{10,... | collective-permute-start | bytes 491528 | tf_op jit(solution)/shard_map/ppermute | solution.py:280
  14.1 4.7 %collective-permute-start.3 = (bf16[64,768]{1,0:T(8,128)(2,1)S(1)}, bf16[64,768]{1,0:T(8,128)(2,1)S(1)}, u32[]{:S(2)}, u32[]{:S(2)}) collective-permute-start(bf16[64,768]{1,0:T(8,128)(2,1)S(1)} %get-tuple-element.35), channel_id=1, source_target_pairs={{0,2},{1,5},{2,0},{3,7},{4,6},{5,1},{6,4},{7,3},{8,10},{9,13},{10,... | collective-permute-start | bytes 294920 | tf_op jit(solution)/shard_map/ppermute | solution.py:280
  16.1 5.4 %collective-permute-start.7 = (bf16[64,1280]{1,0:T(8,128)(2,1)S(1)}, bf16[64,1280]{1,0:T(8,128)(2,1)S(1)}, u32[]{:S(2)}, u32[]{:S(2)}) collective-permute-start(bf16[64,1280]{1,0:T(8,128)(2,1)S(1)} %fusion), channel_id=1, source_target_pairs={{0,4},{1,9},{2,6},{3,11},{4,0},{5,13},{6,2},{7,15},{8,12},{9,1},{1... | collective-permute-start | bytes 491528 | tf_op jit(solution)/shard_map/ppermute | solution.py:280
  18.8 4.7 %collective-permute-start.4 = (bf16[64,768]{1,0:T(8,128)(2,1)S(1)}, bf16[64,768]{1,0:T(8,128)(2,1)S(1)}, u32[]{:S(2)}, u32[]{:S(2)}) collective-permute-start(bf16[64,768]{1,0:T(8,128)(2,1)S(1)} %fusion.1), channel_id=1, source_target_pairs={{0,4},{1,9},{2,6},{3,11},{4,0},{5,13},{6,2},{7,15},{8,12},{9,1},{1... | collective-permute-start | bytes 294920 | tf_op jit(solution)/shard_map/ppermute | solution.py:280
  21.5 5.4 %collective-permute-start.8 = (bf16[64,1280]{1,0:T(8,128)(2,1)S(1)}, bf16[64,1280]{1,0:T(8,128)(2,1)S(1)}, u32[]{:S(2)}, u32[]{:S(2)}) collective-permute-start(bf16[64,1280]{1,0:T(8,128)(2,1)S(1)} %get-tuple-element.47), channel_id=1, source_target_pairs={{0,8},{1,3},{2,10},{3,1},{4,12},{5,7},{6,14},{7,5},{8,0},{9,11},{1... | collective-permute-start | bytes 491528 | tf_op jit(solution)/shard_map/ppermute | solution.py:280
  23.5 4.7 %collective-permute-start.5 = (bf16[64,768]{1,0:T(8,128)(2,1)S(1)}, bf16[64,768]{1,0:T(8,128)(2,1)S(1)}, u32[]{:S(2)}, u32[]{:S(2)}) collective-permute-start(bf16[64,768]{1,0:T(8,128)(2,1)S(1)} %get-tuple-element.49), channel_id=1, source_target_pairs={{0,8},{1,3},{2,10},{3,1},{4,12},{5,7},{6,14},{7,5},{8,0},{9,11},{1... | collective-permute-start | bytes 294920 | tf_op jit(solution)/shard_map/ppermute | solution.py:280
  28.8 1.3 %collective-permute-start.9 = (bf16[48,512]{1,0:T(8,128)(2,1)S(1)}, bf16[48,512]{1,0:T(8,128)(2,1)S(1)}, u32[]{:S(2)}, u32[]{:S(2)}) collective-permute-start(bf16[48,512]{1,0:T(8,128)(2,1)S(1)} %get-tuple-element.46), channel_id=1, source_target_pairs={{0,1},{1,0},{2,3},{3,2},{4,5},{5,4},{6,7},{7,6},{8,9},{9,8},{10,11... | collective-permute-start | bytes 147464 | tf_op jit(solution)/shard_map/ppermute | solution.py:228
  30.2 4.8 %collective-permute-start.10 = (bf16[48,256]{1,0:T(8,128)(2,1)S(1)}, bf16[48,256]{1,0:T(8,128)(2,1)S(1)}, u32[]{:S(2)}, u32[]{:S(2)}) collective-permute-start(bf16[48,256]{1,0:T(8,128)(2,1)S(1)} %slice.13), channel_id=1, source_target_pairs={{0,16},{1,17},{2,18},{3,19},{4,20},{5,21},{6,22},{7,23},{8,24},{9,... | collective-permute-start | bytes 73736 | tf_op jit(solution)/shard_map/ppermute | solution.py:228

commit v10 on v9

--- a/solution.py
+++ b/solution.py
@@ -28,7 +28,7 @@
     return total
 
 
-def call(kernel, out_shape, name, specs, scratch=(), flops=0):
+def call(kernel, out_shape, name, specs, scratch=(), flops=0, aliases={}):
     many = isinstance(out_shape, (list, tuple))
     spaces = {"v": VMEM, "s": SMEM, "h": pltpu.HBM}
     return pl.pallas_call(
@@ -38,6 +38,7 @@
         out_specs=[pl.BlockSpec(memory_space=VMEM)] * len(out_shape) if many else pl.BlockSpec(memory_space=VMEM),
         scratch_shapes=scratch,
         name=name,
+        input_output_aliases=aliases,
         compiler_params=pltpu.CompilerParams(vmem_limit_bytes=24 << 20),
         cost_estimate=pl.CostEstimate(flops=flops, bytes_accessed=flops // 256, transcendentals=0),
     )
@@ -51,7 +52,7 @@
     return hi, mid, low
 
 
-def pack_kernel(idx_ref, pos_hbm, force_hbm, waves_hbm, out_ref, own_ref, pos_ref, force_ref, sems):
+def pack_kernel(amp, idx_ref, pos_hbm, force_hbm, waves_hbm, out_ref, own_ref, frame_ref, wt_ref, pos_ref, force_ref, sems):
     first = pl.multiple_of(idx_ref[0] * own_ref.shape[1], 128)
     copies = [
         pltpu.make_async_copy(pos_hbm, pos_ref, sems.at[0]),
@@ -70,8 +71,18 @@
         p = force_ref.shape[1]
         out_ref[HEAD + a * p : HEAD + (a + 1) * p, :] = force_ref[a].astype(bf16)
 
-
-def frame_kernel(amp, own_ref, frame_ref, wt_ref):
+    @pl.when(idx_ref[0] < 2)
+    def _():
+        frame_of(amp, own_ref, frame_ref, wt_ref)
+
+
+def frame_kernel(amp, idx_ref, own_ref, frame_in, wt_in, frame_ref, wt_ref):
+    @pl.when(idx_ref[0] >= 2)
+    def _():
+        frame_of(amp, own_ref, frame_ref, wt_ref)
+
+
+def frame_of(amp, own_ref, frame_ref, wt_ref):
     kwaves = own_ref.shape[1]
     m = own_ref[...].astype(f32)
     msq = jnp.sum(m * m, axis=0, keepdims=True)
@@ -176,9 +187,7 @@
     tables(first, wt_ref, phase, tab_ref, u_ref, sum_up)
 
 
-def back_kernel(first, offsets, chunk, last, acc_ref, recv_ref, frame_ref, *refs):
-    tables = refs[: len(offsets)]
-    rest = refs[len(offsets) :]
+def back_kernel(first, pieces, earlier, acc_ref, recv_ref, frame_ref, *refs):
     kwaves = acc_ref.shape[1]
     probes = acc_ref.shape[0] // 4
     halves = []
@@ -191,25 +200,14 @@
         halves.append(
             jnp.concatenate([frame_ref[x : x + 1, cols] * t0 + frame_ref[3 + x : 4 + x, cols] * t1 for x in range(3)], axis=0).astype(bf16)
         )
-    begin = 0
-    for offset, table in zip(offsets, tables):
-        width = table.shape[2]
+    for table, row, low, before, out, begin, width in pieces:
         total = sum(
-            jnp.dot(halves[part], table[part, offset : offset + kwaves, :], preferred_element_type=f32) for part in range(2)
+            jnp.dot(halves[part], refs[table][part, row : row + kwaves, low : low + width], preferred_element_type=f32)
+            for part in range(2)
         )
-        if not last:
-            rest[0][:, begin : begin + width] = total
-            begin += width
-            continue
-        earlier, keep, send = rest
-        total += earlier[:, begin : begin + width]
-        split = keep.shape[1]
-        if begin < split:
-            keep[:, begin : min(begin + width, split)] = total[:, : split - begin]
-        if begin + width > split:
-            low = max(begin, split)
-            send[:, low - split : begin + width - split] = total[:, low - begin :].astype(bf16)
-        begin += width
+        if earlier is not None:
+            total += refs[earlier][:, before : before + width]
+        refs[out][:, begin : begin + width] = total.astype(refs[out].dtype)
 
 
 def shards(positions, forces, waves):
@@ -232,18 +230,20 @@
     mine = kwaves // 4
     fl = 4 * half * rows
     shape = jax.ShapeDtypeStruct
-    own, owned = call(
-        pack_kernel,
-        (shape((HEAD + half, rows), bf16), shape((3, mine), jnp.int32)),
+    index = block.reshape(1)
+    framed = (shape((8, mine), f32), shape((mine, HEAD), bf16))
+    own, owned, frame, wt = call(
+        functools.partial(pack_kernel, amp),
+        (shape((HEAD + half, rows), bf16), shape((3, mine), jnp.int32), *framed),
         "pack",
         "shhh",
         scratch=[VMEM(positions.shape, f32), VMEM(forces.shape, f32), pltpu.SemaphoreType.DMA((3,))],
-    )(block.reshape(1), *(pltpu.with_memory_space_constraint(x, pltpu.HBM) for x in (positions, forces, waves)))
+    )(index, *(pltpu.with_memory_space_constraint(x, pltpu.HBM) for x in (positions, forces, waves)))
     near = swap(own, 1)
     far = swap(own, top)
     frame, wt = call(
-        functools.partial(frame_kernel, amp), (shape((8, mine), f32), shape((mine, HEAD), bf16)), "frame", "v", flops=mine * 1000
-    )(owned)
+        functools.partial(frame_kernel, amp), framed, "frame", "svvv", flops=mine * 1000, aliases={2: 0, 3: 1}
+    )(index, owned, frame, wt)
 
     def trig_call(name, first, count, *operands):
         return call(
@@ -291,20 +291,31 @@
                 acc = acc + got.astype(f32)
                 send = acc.astype(bf16)
             state[chunk] = [acc, send, got]
-    first = call(
-        functools.partial(back_kernel, 0, (0, 0, 0, 0), 256, False), shape((half, 4 * rows), f32), "back", "vvvvvvv", flops=parts[0] * fl * 4
-    )(state[0][0], state[0][2], frame, tab_own, tab_far, tab_near, tab_a)
-    keep, send = call(
-        functools.partial(back_kernel, split, (split, 0), 256, True),
-        (shape((half, 2 * rows), f32), shape((half, 2 * rows), bf16)),
+    (acc_a, _, got_a), (acc_b, _, got_b) = state
+    r = rows
+    early = call(
+        functools.partial(back_kernel, 0, [(j, 0, 0, 0, 4, j * r, r) for j in range(4)], None),
+        shape((half, 4 * r), f32),
         "back",
-        "vvvvvv",
-        flops=parts[1] * fl * 4,
-    )(state[1][0], state[1][2], frame, tab_own, tab_b, first)
-    there = swap(send, 1)
-    keep = keep + there.astype(f32)
-    there = swap(keep[:, rows:].astype(bf16), top)
-    total = keep[:, :rows] + there.astype(f32)
+        "vvvvvvv",
+        flops=parts[0] * fl * 4,
+    )(acc_a, got_a, frame, tab_own, tab_far, tab_near, tab_a)
+
+    def late(keep, give):
+        return call(
+            functools.partial(back_kernel, split, [(*keep, 3, 0, r), (*give, 4, 0, r)], 2),
+            (shape((half, r), f32), shape((half, r), bf16)),
+            "back",
+            "vvvvvv",
+            flops=parts[1] * fl * 2,
+        )(acc_b, got_b, frame, tab_own, tab_b, early)
+
+    total_far, send_across = late((1, 0, 0, r), (1, 0, 2 * r, 3 * r))
+    there = swap(send_across, 1)
+    total, send_near = late((0, split, 0, 0), (1, 0, r, 2 * r))
+    near_too = swap(send_near, 1)
+    back = swap((total_far + there.astype(f32)).astype(bf16), top)
+    total = total + near_too.astype(f32) + back.astype(f32)
     return total.reshape(forces.shape)
 
 

time: 35.8 us -> 35.5 us (level)
  waiting for transfers between devices: 10.1 us -> 9.14 us
  starting transfers between devices: 14.9 us -> 15.5 us
    ppermute x5 -> x6, waiting for transfers between devices: 4.24 us -> 3.26 us  [swap(): return lax.ppermute(x, AXES, [(d, d ^ bit) for d in range(devices)])]
    ppermute x5 -> x6, starting transfers between devices: 6.29 us -> 6.84 us  [swap(): return lax.ppermute(x, AXES, [(d, d ^ bit) for d in range(devices)])]
    pallas_call x4 -> x5, Pallas kernels: 2.73 us -> 2.86 us  [the longest x1 1.1 us: shards(): call(functools.partial(pack_kernel, amp), (shape((HEAD + half, rows), bf1...]
  transfers between devices with their start and end apart: 11 -> 12, of which waited for: 8 -> 8; matrix products, arithmetic and copies ran while one was open for 0% -> 0% of each run, Pallas kernels for 20% -> 20%
where the time goes in v10:
time: 35.5 us; the launch traced here: 35.3 us
  starting transfers between devices  15.5 us (44%)
  Pallas kernels  9.81 us (28%)
  waiting for transfers between devices  9.14 us (26%)
  other arithmetic  0.79 us (2%)
    ppermute x6, starting transfers between devices, exchange(): return lax.ppermute(x, AXES, [(d, d ^ turn[d % 2]) for d in range(devices)])  8.61 us
    ppermute x6, starting transfers between devices, swap(): return lax.ppermute(x, AXES, [(d, d ^ bit) for d in range(devices)])  6.84 us
    ppermute x6, waiting for transfers between devices, exchange(): return lax.ppermute(x, AXES, [(d, d ^ turn[d % 2]) for d in range(devices)])  5.88 us
    pallas_call x3, Pallas kernels, trig_call(): call(functools.partial(trig_kernel, first), (shape((2, count, rows), bf16...  3.92 us
    ppermute x6, waiting for transfers between devices, swap(): return lax.ppermute(x, AXES, [(d, d ^ bit) for d in range(devices)])  3.26 us
    pallas_call x2, Pallas kernels, sums(): call(functools.partial(sums_kernel, first, start), (shape((2, count, widt...  3.03 us
    pallas_call x1, Pallas kernels, shards(): call(functools.partial(pack_kernel, amp), (shape((HEAD + half, rows), bf1...  1.1 us
    pallas_call x1, Pallas kernels, shards(): call(functools.partial(back_kernel, 0, [(j, 0, 0, 0, 4, j * r, r) for j i...  1 us
  transfers between devices with their start and end apart: 12, of which 8 were waited for; matrix products, arithmetic and copies ran while one was open for 0% of the time, Pallas kernels for 20%

profile of v10, /device:TPU:0, one launch (start us, length us, event | category | flops | bytes accessed | tf_op | source)
XLA Modules:
  0.0 35.3 jit_solution(6592512607314948225)
XLA Ops:
  0.0 1.1 %pack.1 = (bf16[64,256]{1,0:T(8,128)(2,1)S(1)}, s32[3,2048]{1,0:T(4,128)S(1)}, f32[8,2048]{1,0:T(8,128)S(1)}, bf16[2048,16]{1,0:T(8,128)(2,1)S(1)}) custom-call(s32[1]{0:T(128)} %bitcast.idx_ref, f32[3,256]{1,0:T(4,128)} %pos_hbm.1, f32[3,16,256]{2,1,0:T(8,128)} %force_hbm.1, s32[3,8192]{1,0:T(4,128)} %waves_hbm.1), custom_call_target="tpu_custom_call" | custom-call | tf_op jit(solution)/shard_map/pack/pallas_call | solution.py:235
  1.1 0.6 %collective-permute-start.1 = (bf16[64,256]{1,0:T(8,128)(2,1)S(1)}, bf16[64,256]{1,0:T(8,128)(2,1)S(1)}, u32[]{:S(2)}, u32[]{:S(2)}) collective-permute-start(bf16[64,256]{1,0:T(8,128)(2,1)S(1)} %get-tuple-element.35.pack_ref), channel_id=1, source_target_pairs={{0,1},{1,0},{2,3},{3,2},{4,5},{5,4},{6,7},{7,6},{8,9},{9,8},{10,11... | collective-permute-start | bytes 98312 | tf_op jit(solution)/shard_map/ppermute | solution.py:226
  1.7 3.4 %collective-permute-start = (bf16[64,256]{1,0:T(8,128)(2,1)S(1)}, bf16[64,256]{1,0:T(8,128)(2,1)S(1)}, u32[]{:S(2)}, u32[]{:S(2)}) collective-permute-start(bf16[64,256]{1,0:T(8,128)(2,1)S(1)} %get-tuple-element.35.pack_ref), channel_id=1, source_target_pairs={{0,16},{1,17},{2,18},{3,19},{4,20},{5,21},{6,22},{7,23},{8,24},{9,... | collective-permute-start | bytes 98312 | tf_op jit(solution)/shard_map/ppermute | solution.py:226
  5.1 1.7 %trig_own.1 = (bf16[2,2048,256]{2,1,0:T(8,128)(2,1)S(1)}, f32[96,2048]{1,0:T(8,128)S(1)}) custom-call(bf16[2048,16]{1,0:T(8,128)(2,1)S(1)} %get-tuple-element.34.wt_ref, bf16[64,256]{1,0:T(8,128)(2,1)S(1)} %get-tuple-element.35.pack_ref), custom_call_target="tpu_custom_call" | custom-call | flops 100663296 | bytes 393216 | tf_op jit(solution)/shard_map/trig_own/pallas_call | solution.py:249
  6.7 1.1 %trig_near.1 = (bf16[2,1280,256]{2,1,0:T(8,128)(2,1)S(1)}, f32[96,1280]{1,0:T(8,128)S(1)}) custom-call(bf16[2048,16]{1,0:T(8,128)(2,1)S(1)} %get-tuple-element.34.wt_ref, bf16[64,256]{1,0:T(8,128)(2,1)S(1)} %collective-permute-done.1.pack_ref.refs_1_, f32[96,2048]{1,0:T(8,128)S(1)} %get-tuple-element.36.refs_0_.raw_ref), custom_call_target="tpu_custom_call" | custom-call | flops 62914560 | bytes 245760 | tf_op jit(solution)/shard_map/trig_near/pallas_call | solution.py:249
  8.1 1.1 %trig_far.1 = (bf16[2,1280,256]{2,1,0:T(8,128)(2,1)S(1)}, f32[96,1280]{1,0:T(8,128)S(1)}) custom-call(bf16[2048,16]{1,0:T(8,128)(2,1)S(1)} %get-tuple-element.34.wt_ref, bf16[64,256]{1,0:T(8,128)(2,1)S(1)} %collective-permute-done.refs_0_.pack_ref, f32[96,1280]{1,0:T(8,128)S(1)} %get-tuple-element.44.refs_0_), custom_call_target="tpu_custom_call" | custom-call | flops 62914560 | bytes 245760 | tf_op jit(solution)/shard_map/trig_far/pallas_call | solution.py:249
  9.3 1.2 %sums.3 = (bf16[2,1280,256]{2,1,0:T(8,128)(2,1)S(1)}, f32[64,1280]{1,0:T(8,128)S(1)}, bf16[64,1280]{1,0:T(8,128)(2,1)S(1)}) custom-call(f32[8,2048]{1,0:T(8,128)S(1)} %get-tuple-element.33.frame_ref, bf16[2048,16]{1,0:T(8,128)(2,1)S(1)} %get-tuple-element.34.wt_ref, f32[96,1280]{1,0:T(8,128)S(1)} %get-tuple-element.45.raw_ref, ...), custom_call_target="tpu_custom_call" | custom-call | flops 62914560 | bytes 245760 | tf_op jit(solution)/shard_map/sums/pallas_call | solution.py:266
  10.5 1.6 %collective-permute-start.6 = (bf16[64,1280]{1,0:T(8,128)(2,1)S(1)}, bf16[64,1280]{1,0:T(8,128)(2,1)S(1)}, u32[]{:S(2)}, u32[]{:S(2)}) collective-permute-start(bf16[64,1280]{1,0:T(8,128)(2,1)S(1)} %get-tuple-element.47), channel_id=1, source_target_pairs={{0,2},{1,5},{2,0},{3,7},{4,6},{5,1},{6,4},{7,3},{8,10},{9,13},{10,... | collective-permute-start | bytes 491528 | tf_op jit(solution)/shard_map/ppermute | solution.py:280
  12.0 1.8 %sums.2 = (bf16[2,768,768]{2,1,0:T(8,128)(2,1)S(1)}, f32[64,768]{1,0:T(8,128)S(1)}, bf16[64,768]{1,0:T(8,128)(2,1)S(1)}) custom-call(f32[8,2048]{1,0:T(8,128)S(1)} %get-tuple-element.33.frame_ref, bf16[2048,16]{1,0:T(8,128)(2,1)S(1)} %get-tuple-element.34.wt_ref, f32[96,2048]{1,0:T(8,128)S(1)} %get-tuple-element.36.refs_0_.raw_ref, ...), custom_call_target="tpu_custom_call" | custom-call | flops 113246208 | bytes 442368 | tf_op jit(solution)/shard_map/sums/pallas_call | solution.py:266
  13.9 0.6 %collective-permute-start.3 = (bf16[64,768]{1,0:T(8,128)(2,1)S(1)}, bf16[64,768]{1,0:T(8,128)(2,1)S(1)}, u32[]{:S(2)}, u32[]{:S(2)}) collective-permute-start(bf16[64,768]{1,0:T(8,128)(2,1)S(1)} %get-tuple-element.41), channel_id=1, source_target_pairs={{0,2},{1,5},{2,0},{3,7},{4,6},{5,1},{6,4},{7,3},{8,10},{9,13},{10,... | collective-permute-start | bytes 294920 | tf_op jit(solution)/shard_map/ppermute | solution.py:280
  14.5 1.4 %collective-permute-done.6 = bf16[64,1280]{1,0:T(8,128)(2,1)S(1)} collective-permute-done((bf16[64,1280]{1,0:T(8,128)(2,1)S(1)}, bf16[64,1280]{1,0:T(8,128)(2,1)S(1)}, u32[]{:S(2)}, u32[]{:S(2)}) %collective-permute-start.6) | collective-permute-done | bytes 163872 | tf_op jit(solution)/shard_map/ppermute | solution.py:280
  15.9 1.6 %collective-permute-start.7 = (bf16[64,1280]{1,0:T(8,128)(2,1)S(1)}, bf16[64,1280]{1,0:T(8,128)(2,1)S(1)}, u32[]{:S(2)}, u32[]{:S(2)}) collective-permute-start(bf16[64,1280]{1,0:T(8,128)(2,1)S(1)} %fusion), channel_id=1, source_target_pairs={{0,4},{1,9},{2,6},{3,11},{4,0},{5,13},{6,2},{7,15},{8,12},{9,1},{1... | collective-permute-start | bytes 491528 | tf_op jit(solution)/shard_map/ppermute | solution.py:280
  17.5 1.1 %collective-permute-done.3 = bf16[64,768]{1,0:T(8,128)(2,1)S(1)} collective-permute-done((bf16[64,768]{1,0:T(8,128)(2,1)S(1)}, bf16[64,768]{1,0:T(8,128)(2,1)S(1)}, u32[]{:S(2)}, u32[]{:S(2)}) %collective-permute-start.3) | collective-permute-done | bytes 98336 | tf_op jit(solution)/shard_map/ppermute | solution.py:280
  18.6 1.6 %collective-permute-start.4 = (bf16[64,768]{1,0:T(8,128)(2,1)S(1)}, bf16[64,768]{1,0:T(8,128)(2,1)S(1)}, u32[]{:S(2)}, u32[]{:S(2)}) collective-permute-start(bf16[64,768]{1,0:T(8,128)(2,1)S(1)} %fusion.1), channel_id=1, source_target_pairs={{0,4},{1,9},{2,6},{3,11},{4,0},{5,13},{6,2},{7,15},{8,12},{9,1},{1... | collective-permute-start | bytes 294920 | tf_op jit(solution)/shard_map/ppermute | solution.py:280
  20.1 1.1 %collective-permute-done.7 = bf16[64,1280]{1,0:T(8,128)(2,1)S(1)} collective-permute-done((bf16[64,1280]{1,0:T(8,128)(2,1)S(1)}, bf16[64,1280]{1,0:T(8,128)(2,1)S(1)}, u32[]{:S(2)}, u32[]{:S(2)}) %collective-permute-start.7) | collective-permute-done | bytes 163872 | tf_op jit(solution)/shard_map/ppermute | solution.py:280
  21.3 1.6 %collective-permute-start.8 = (bf16[64,1280]{1,0:T(8,128)(2,1)S(1)}, bf16[64,1280]{1,0:T(8,128)(2,1)S(1)}, u32[]{:S(2)}, u32[]{:S(2)}) collective-permute-start(bf16[64,1280]{1,0:T(8,128)(2,1)S(1)} %get-tuple-element.55), channel_id=1, source_target_pairs={{0,8},{1,3},{2,10},{3,1},{4,12},{5,7},{6,14},{7,5},{8,0},{9,11},{1... | collective-permute-start | bytes 491528 | tf_op jit(solution)/shard_map/ppermute | solution.py:280
  23.3 1.6 %collective-permute-start.5 = (bf16[64,768]{1,0:T(8,128)(2,1)S(1)}, bf16[64,768]{1,0:T(8,128)(2,1)S(1)}, u32[]{:S(2)}, u32[]{:S(2)}) collective-permute-start(bf16[64,768]{1,0:T(8,128)(2,1)S(1)} %get-tuple-element.57), channel_id=1, source_target_pairs={{0,8},{1,3},{2,10},{3,1},{4,12},{5,7},{6,14},{7,5},{8,0},{9,11},{1... | collective-permute-start | bytes 294920 | tf_op jit(solution)/shard_map/ppermute | solution.py:280
  24.9 1.8 %collective-permute-done.8.recv_ref = bf16[64,1280]{1,0:T(8,128)(2,1)S(1)} collective-permute-done((bf16[64,1280]{1,0:T(8,128)(2,1)S(1)}, bf16[64,1280]{1,0:T(8,128)(2,1)S(1)}, u32[]{:S(2)}, u32[]{:S(2)}) %collective-permute-start.8) | collective-permute-done | bytes 163872 | tf_op jit(solution)/shard_map/ppermute | solution.py:280
  26.7 1.0 %back.3.refs_2_ = f32[48,1024]{1,0:T(8,128)S(1)} custom-call(f32[64,1280]{1,0:T(8,128)S(1)} %get-tuple-element.56.acc_ref, bf16[64,1280]{1,0:T(8,128)(2,1)S(1)} %collective-permute-done.8.recv_ref, f32[8,2048]{1,0:T(8,128)S(1)} %get-tuple-element.33.frame_ref, bf16[2,2048,256]{2,1,0:T(8,128)(2,1)S(1)} %get-tuple-element.42.refs_0_, ...), custom_call_target="tpu_custom_call" | custom-call | flops 251658240 | bytes 983040 | tf_op jit(solution)/shard_map/back/pallas_call | solution.py:296
  28.4 0.4 %back.4 = (f32[48,256]{1,0:T(8,128)S(1)}, bf16[48,256]{1,0:T(8,128)(2,1)S(1)}) custom-call(f32[64,768]{1,0:T(8,128)S(1)} %get-tuple-element.58.acc_ref, bf16[64,768]{1,0:T(8,128)(2,1)S(1)} %collective-permute-done.5.recv_ref, f32[8,2048]{1,0:T(8,128)S(1)} %get-tuple-element.33.frame_ref, bf16[2,2048,256]{2,1,0:T(8,128)(2,1)S(1)} %get-tuple-element.42.refs_0_, ...), custom_call_target="tpu_custom_call" | custom-call | flops 75497472 | bytes 294912 | tf_op jit(solution)/shard_map/back/pallas_call | solution.py:305
  28.8 0.6 %collective-permute-start.9 = (bf16[48,256]{1,0:T(8,128)(2,1)S(1)}, bf16[48,256]{1,0:T(8,128)(2,1)S(1)}, u32[]{:S(2)}, u32[]{:S(2)}) collective-permute-start(bf16[48,256]{1,0:T(8,128)(2,1)S(1)} %get-tuple-element.52), channel_id=1, source_target_pairs={{0,1},{1,0},{2,3},{3,2},{4,5},{5,4},{6,7},{7,6},{8,9},{9,8},{10,11... | collective-permute-start | bytes 73736 | tf_op jit(solution)/shard_map/ppermute | solution.py:226
  29.6 2.0 %collective-permute-start.11 = (bf16[48,256]{1,0:T(8,128)(2,1)S(1)}, bf16[48,256]{1,0:T(8,128)(2,1)S(1)}, u32[]{:S(2)}, u32[]{:S(2)}) collective-permute-start(bf16[48,256]{1,0:T(8,128)(2,1)S(1)} %add_convert_fusion), channel_id=1, source_target_pairs={{0,16},{1,17},{2,18},{3,19},{4,20},{5,21},{6,22},{7,23},{8,24},{9,... | collective-permute-start | bytes 73736 | tf_op jit(solution)/shard_map/ppermute | solution.py:226
  31.7 3.0 %collective-permute-done.11 = bf16[48,256]{1,0:T(8,128)(2,1)S(1)} collective-permute-done((bf16[48,256]{1,0:T(8,128)(2,1)S(1)}, bf16[48,256]{1,0:T(8,128)(2,1)S(1)}, u32[]{:S(2)}, u32[]{:S(2)}) %collective-permute-start.11) | collective-permute-done | bytes 24608 | tf_op jit(solution)/shard_map/ppermute | solution.py:226
  34.7 0.6 %convert_add_fusion.4 = f32[48,256]{1,0:T(8,128)} fusion(bf16[48,256]{1,0:T(8,128)(2,1)S(1)} %collective-permute-done.11, f32[48,256]{1,0:T(8,128)S(1)} %get-tuple-element.51, bf16[48,256]{1,0:T(8,128)(2,1)S(1)} %collective-permute-done.9), kind=kLoop, calls=%fused_computation.6 | loop fusion | flops 49152 | bytes 147456 | tf_op jit(solution)/shard_map/add | solution.py:318
  (16 shorter events, 1.6 us)
Async XLA Ops:
  1.1 5.6 %collective-permute-start.1 = (bf16[64,256]{1,0:T(8,128)(2,1)S(1)}, bf16[64,256]{1,0:T(8,128)(2,1)S(1)}, u32[]{:S(2)}, u32[]{:S(2)}) collective-permute-start(bf16[64,256]{1,0:T(8,128)(2,1)S(1)} %get-tuple-element.35.pack_ref), channel_id=1, source_target_pairs={{0,1},{1,0},{2,3},{3,2},{4,5},{5,4},{6,7},{7,6},{8,9},{9,8},{10,11... | collective-permute-start | bytes 98312 | tf_op jit(solution)/shard_map/ppermute | solution.py:226
  1.7 6.2 %collective-permute-start = (bf16[64,256]{1,0:T(8,128)(2,1)S(1)}, bf16[64,256]{1,0:T(8,128)(2,1)S(1)}, u32[]{:S(2)}, u32[]{:S(2)}) collective-permute-start(bf16[64,256]{1,0:T(8,128)(2,1)S(1)} %get-tuple-element.35.pack_ref), channel_id=1, source_target_pairs={{0,16},{1,17},{2,18},{3,19},{4,20},{5,21},{6,22},{7,23},{8,24},{9,... | collective-permute-start | bytes 98312 | tf_op jit(solution)/shard_map/ppermute | solution.py:226
  7.9 1.4 %collective-permute-start.2 = (bf16[64,256]{1,0:T(8,128)(2,1)S(1)}, bf16[64,256]{1,0:T(8,128)(2,1)S(1)}, u32[]{:S(2)}, u32[]{:S(2)}) collective-permute-start(bf16[64,256]{1,0:T(8,128)(2,1)S(1)} %collective-permute-done.refs_0_.pack_ref), channel_id=1, source_target_pairs={{0,1},{1,0},{2,3},{3,2},{4,5},{5,4},{6,7},{7,6},{8,9},{9,8},{10,11... | collective-permute-start | bytes 98312 | tf_op jit(solution)/shard_map/ppermute | solution.py:226
  10.5 5.4 %collective-permute-start.6 = (bf16[64,1280]{1,0:T(8,128)(2,1)S(1)}, bf16[64,1280]{1,0:T(8,128)(2,1)S(1)}, u32[]{:S(2)}, u32[]{:S(2)}) collective-permute-start(bf16[64,1280]{1,0:T(8,128)(2,1)S(1)} %get-tuple-element.47), channel_id=1, source_target_pairs={{0,2},{1,5},{2,0},{3,7},{4,6},{5,1},{6,4},{7,3},{8,10},{9,13},{10,... | collective-permute-start | bytes 491528 | tf_op jit(solution)/shard_map/ppermute | solution.py:280
  13.9 4.7 %collective-permute-start.3 = (bf16[64,768]{1,0:T(8,128)(2,1)S(1)}, bf16[64,768]{1,0:T(8,128)(2,1)S(1)}, u32[]{:S(2)}, u32[]{:S(2)}) collective-permute-start(bf16[64,768]{1,0:T(8,128)(2,1)S(1)} %get-tuple-element.41), channel_id=1, source_target_pairs={{0,2},{1,5},{2,0},{3,7},{4,6},{5,1},{6,4},{7,3},{8,10},{9,13},{10,... | collective-permute-start | bytes 294920 | tf_op jit(solution)/shard_map/ppermute | solution.py:280
  15.9 5.4 %collective-permute-start.7 = (bf16[64,1280]{1,0:T(8,128)(2,1)S(1)}, bf16[64,1280]{1,0:T(8,128)(2,1)S(1)}, u32[]{:S(2)}, u32[]{:S(2)}) collective-permute-start(bf16[64,1280]{1,0:T(8,128)(2,1)S(1)} %fusion), channel_id=1, source_target_pairs={{0,4},{1,9},{2,6},{3,11},{4,0},{5,13},{6,2},{7,15},{8,12},{9,1},{1... | collective-permute-start | bytes 491528 | tf_op jit(solution)/shard_map/ppermute | solution.py:280
  18.6 4.7 %collective-permute-start.4 = (bf16[64,768]{1,0:T(8,128)(2,1)S(1)}, bf16[64,768]{1,0:T(8,128)(2,1)S(1)}, u32[]{:S(2)}, u32[]{:S(2)}) collective-permute-start(bf16[64,768]{1,0:T(8,128)(2,1)S(1)} %fusion.1), channel_id=1, source_target_pairs={{0,4},{1,9},{2,6},{3,11},{4,0},{5,13},{6,2},{7,15},{8,12},{9,1},{1... | collective-permute-start | bytes 294920 | tf_op jit(solution)/shard_map/ppermute | solution.py:280
  21.3 5.4 %collective-permute-start.8 = (bf16[64,1280]{1,0:T(8,128)(2,1)S(1)}, bf16[64,1280]{1,0:T(8,128)(2,1)S(1)}, u32[]{:S(2)}, u32[]{:S(2)}) collective-permute-start(bf16[64,1280]{1,0:T(8,128)(2,1)S(1)} %get-tuple-element.55), channel_id=1, source_target_pairs={{0,8},{1,3},{2,10},{3,1},{4,12},{5,7},{6,14},{7,5},{8,0},{9,11},{1... | collective-permute-start | bytes 491528 | tf_op jit(solution)/shard_map/ppermute | solution.py:280
  23.3 4.7 %collective-permute-start.5 = (bf16[64,768]{1,0:T(8,128)(2,1)S(1)}, bf16[64,768]{1,0:T(8,128)(2,1)S(1)}, u32[]{:S(2)}, u32[]{:S(2)}) collective-permute-start(bf16[64,768]{1,0:T(8,128)(2,1)S(1)} %get-tuple-element.57), channel_id=1, source_target_pairs={{0,8},{1,3},{2,10},{3,1},{4,12},{5,7},{6,14},{7,5},{8,0},{9,11},{1... | collective-permute-start | bytes 294920 | tf_op jit(solution)/shard_map/ppermute | solution.py:280
  28.4 1.3 %collective-permute-start.10 = (bf16[48,256]{1,0:T(8,128)(2,1)S(1)}, bf16[48,256]{1,0:T(8,128)(2,1)S(1)}, u32[]{:S(2)}, u32[]{:S(2)}) collective-permute-start(bf16[48,256]{1,0:T(8,128)(2,1)S(1)} %get-tuple-element.54), channel_id=1, source_target_pairs={{0,1},{1,0},{2,3},{3,2},{4,5},{5,4},{6,7},{7,6},{8,9},{9,8},{10,11... | collective-permute-start | bytes 73736 | tf_op jit(solution)/shard_map/ppermute | solution.py:226
  28.8 2.8 %collective-permute-start.9 = (bf16[48,256]{1,0:T(8,128)(2,1)S(1)}, bf16[48,256]{1,0:T(8,128)(2,1)S(1)}, u32[]{:S(2)}, u32[]{:S(2)}) collective-permute-start(bf16[48,256]{1,0:T(8,128)(2,1)S(1)} %get-tuple-element.52), channel_id=1, source_target_pairs={{0,1},{1,0},{2,3},{3,2},{4,5},{5,4},{6,7},{7,6},{8,9},{9,8},{10,11... | collective-permute-start | bytes 73736 | tf_op jit(solution)/shard_map/ppermute | solution.py:226
  29.6 5.0 %collective-permute-start.11 = (bf16[48,256]{1,0:T(8,128)(2,1)S(1)}, bf16[48,256]{1,0:T(8,128)(2,1)S(1)}, u32[]{:S(2)}, u32[]{:S(2)}) collective-permute-start(bf16[48,256]{1,0:T(8,128)(2,1)S(1)} %add_convert_fusion), channel_id=1, source_target_pairs={{0,16},{1,17},{2,18},{3,19},{4,20},{5,21},{6,22},{7,23},{8,24},{9,... | collective-permute-start | bytes 73736 | tf_op jit(solution)/shard_map/ppermute | solution.py:226

commit v11 on v10

--- a/solution.py
+++ b/solution.py
@@ -301,18 +301,18 @@
         flops=parts[0] * fl * 4,
     )(acc_a, got_a, frame, tab_own, tab_far, tab_near, tab_a)
 
-    def late(keep, give):
+    def late(pieces, *outs):
         return call(
-            functools.partial(back_kernel, split, [(*keep, 3, 0, r), (*give, 4, 0, r)], 2),
-            (shape((half, r), f32), shape((half, r), bf16)),
+            functools.partial(back_kernel, split, [(*piece, 3 + j, 0, r) for j, piece in enumerate(pieces)], 2),
+            [shape((half, r), kind) for kind in outs],
             "back",
             "vvvvvv",
-            flops=parts[1] * fl * 2,
+            flops=parts[1] * fl * len(outs),
         )(acc_b, got_b, frame, tab_own, tab_b, early)
 
-    total_far, send_across = late((1, 0, 0, r), (1, 0, 2 * r, 3 * r))
+    (send_across,) = late([(1, 0, 2 * r, 3 * r)], bf16)
     there = swap(send_across, 1)
-    total, send_near = late((0, split, 0, 0), (1, 0, r, 2 * r))
+    total_far, total, send_near = late([(1, 0, 0, r), (0, split, 0, 0), (1, 0, r, 2 * r)], f32, f32, bf16)
     near_too = swap(send_near, 1)
     back = swap((total_far + there.astype(f32)).astype(bf16), top)
     total = total + near_too.astype(f32) + back.astype(f32)

time: 35.5 us -> 35.3 us (level)
  transfers between devices with their start and end apart: 12 -> 12, of which waited for: 8 -> 8; matrix products, arithmetic and copies ran while one was open for 0% -> 0% of each run, Pallas kernels for 20% -> 21%
where the time goes in v11:
time: 35.3 us; the launch traced here: 35.2 us
  starting transfers between devices  15.5 us (44%)
  Pallas kernels  9.8 us (28%)
  waiting for transfers between devices  9.01 us (26%)
  other arithmetic  0.79 us (2%)
    ppermute x6, starting transfers between devices, exchange(): return lax.ppermute(x, AXES, [(d, d ^ turn[d % 2]) for d in range(devices)])  8.61 us
    ppermute x6, starting transfers between devices, swap(): return lax.ppermute(x, AXES, [(d, d ^ bit) for d in range(devices)])  6.84 us
    ppermute x6, waiting for transfers between devices, exchange(): return lax.ppermute(x, AXES, [(d, d ^ turn[d % 2]) for d in range(devices)])  5.88 us
    pallas_call x3, Pallas kernels, trig_call(): call(functools.partial(trig_kernel, first), (shape((2, count, rows), bf16...  3.92 us
    ppermute x6, waiting for transfers between devices, swap(): return lax.ppermute(x, AXES, [(d, d ^ bit) for d in range(devices)])  3.13 us
    pallas_call x2, Pallas kernels, sums(): call(functools.partial(sums_kernel, first, start), (shape((2, count, widt...  3.03 us
    pallas_call x1, Pallas kernels, shards(): call(functools.partial(pack_kernel, amp), (shape((HEAD + half, rows), bf1...  1.1 us
    pallas_call x1, Pallas kernels, shards(): call(functools.partial(back_kernel, 0, [(j, 0, 0, 0, 4, j * r, r) for j i...  1 us
  transfers between devices with their start and end apart: 12, of which 8 were waited for; matrix products, arithmetic and copies ran while one was open for 0% of the time, Pallas kernels for 21%

profile of v11, /device:TPU:0, one launch (start us, length us, event | category | flops | bytes accessed | tf_op | source)
XLA Modules:
  0.0 35.2 jit_solution(963317906803053589)
XLA Ops:
  0.0 1.1 %pack.1 = (bf16[64,256]{1,0:T(8,128)(2,1)S(1)}, s32[3,2048]{1,0:T(4,128)S(1)}, f32[8,2048]{1,0:T(8,128)S(1)}, bf16[2048,16]{1,0:T(8,128)(2,1)S(1)}) custom-call(s32[1]{0:T(128)} %bitcast.idx_ref, f32[3,256]{1,0:T(4,128)} %pos_hbm.1, f32[3,16,256]{2,1,0:T(8,128)} %force_hbm.1, s32[3,8192]{1,0:T(4,128)} %waves_hbm.1), custom_call_target="tpu_custom_call" | custom-call | tf_op jit(solution)/shard_map/pack/pallas_call | solution.py:235
  1.1 0.6 %collective-permute-start.1 = (bf16[64,256]{1,0:T(8,128)(2,1)S(1)}, bf16[64,256]{1,0:T(8,128)(2,1)S(1)}, u32[]{:S(2)}, u32[]{:S(2)}) collective-permute-start(bf16[64,256]{1,0:T(8,128)(2,1)S(1)} %get-tuple-element.34.pack_ref), channel_id=1, source_target_pairs={{0,1},{1,0},{2,3},{3,2},{4,5},{5,4},{6,7},{7,6},{8,9},{9,8},{10,11... | collective-permute-start | bytes 98312 | tf_op jit(solution)/shard_map/ppermute | solution.py:226
  1.7 3.4 %collective-permute-start = (bf16[64,256]{1,0:T(8,128)(2,1)S(1)}, bf16[64,256]{1,0:T(8,128)(2,1)S(1)}, u32[]{:S(2)}, u32[]{:S(2)}) collective-permute-start(bf16[64,256]{1,0:T(8,128)(2,1)S(1)} %get-tuple-element.34.pack_ref), channel_id=1, source_target_pairs={{0,16},{1,17},{2,18},{3,19},{4,20},{5,21},{6,22},{7,23},{8,24},{9,... | collective-permute-start | bytes 98312 | tf_op jit(solution)/shard_map/ppermute | solution.py:226
  5.1 1.7 %trig_own.1 = (bf16[2,2048,256]{2,1,0:T(8,128)(2,1)S(1)}, f32[96,2048]{1,0:T(8,128)S(1)}) custom-call(bf16[2048,16]{1,0:T(8,128)(2,1)S(1)} %get-tuple-element.33.wt_ref, bf16[64,256]{1,0:T(8,128)(2,1)S(1)} %get-tuple-element.34.pack_ref), custom_call_target="tpu_custom_call" | custom-call | flops 100663296 | bytes 393216 | tf_op jit(solution)/shard_map/trig_own/pallas_call | solution.py:249
  6.7 1.1 %trig_near.1 = (bf16[2,1280,256]{2,1,0:T(8,128)(2,1)S(1)}, f32[96,1280]{1,0:T(8,128)S(1)}) custom-call(bf16[2048,16]{1,0:T(8,128)(2,1)S(1)} %get-tuple-element.33.wt_ref, bf16[64,256]{1,0:T(8,128)(2,1)S(1)} %collective-permute-done.1.pack_ref.refs_1_, f32[96,2048]{1,0:T(8,128)S(1)} %get-tuple-element.35.refs_0_.raw_ref), custom_call_target="tpu_custom_call" | custom-call | flops 62914560 | bytes 245760 | tf_op jit(solution)/shard_map/trig_near/pallas_call | solution.py:249
  8.1 1.1 %trig_far.1 = (bf16[2,1280,256]{2,1,0:T(8,128)(2,1)S(1)}, f32[96,1280]{1,0:T(8,128)S(1)}) custom-call(bf16[2048,16]{1,0:T(8,128)(2,1)S(1)} %get-tuple-element.33.wt_ref, bf16[64,256]{1,0:T(8,128)(2,1)S(1)} %collective-permute-done.refs_0_.pack_ref, f32[96,1280]{1,0:T(8,128)S(1)} %get-tuple-element.43.refs_0_), custom_call_target="tpu_custom_call" | custom-call | flops 62914560 | bytes 245760 | tf_op jit(solution)/shard_map/trig_far/pallas_call | solution.py:249
  9.3 1.2 %sums.3 = (bf16[2,1280,256]{2,1,0:T(8,128)(2,1)S(1)}, f32[64,1280]{1,0:T(8,128)S(1)}, bf16[64,1280]{1,0:T(8,128)(2,1)S(1)}) custom-call(f32[8,2048]{1,0:T(8,128)S(1)} %get-tuple-element.32.frame_ref, bf16[2048,16]{1,0:T(8,128)(2,1)S(1)} %get-tuple-element.33.wt_ref, f32[96,1280]{1,0:T(8,128)S(1)} %get-tuple-element.44.raw_ref, ...), custom_call_target="tpu_custom_call" | custom-call | flops 62914560 | bytes 245760 | tf_op jit(solution)/shard_map/sums/pallas_call | solution.py:266
  10.5 1.6 %collective-permute-start.6 = (bf16[64,1280]{1,0:T(8,128)(2,1)S(1)}, bf16[64,1280]{1,0:T(8,128)(2,1)S(1)}, u32[]{:S(2)}, u32[]{:S(2)}) collective-permute-start(bf16[64,1280]{1,0:T(8,128)(2,1)S(1)} %get-tuple-element.46), channel_id=1, source_target_pairs={{0,2},{1,5},{2,0},{3,7},{4,6},{5,1},{6,4},{7,3},{8,10},{9,13},{10,... | collective-permute-start | bytes 491528 | tf_op jit(solution)/shard_map/ppermute | solution.py:280
  12.0 1.8 %sums.2 = (bf16[2,768,768]{2,1,0:T(8,128)(2,1)S(1)}, f32[64,768]{1,0:T(8,128)S(1)}, bf16[64,768]{1,0:T(8,128)(2,1)S(1)}) custom-call(f32[8,2048]{1,0:T(8,128)S(1)} %get-tuple-element.32.frame_ref, bf16[2048,16]{1,0:T(8,128)(2,1)S(1)} %get-tuple-element.33.wt_ref, f32[96,2048]{1,0:T(8,128)S(1)} %get-tuple-element.35.refs_0_.raw_ref, ...), custom_call_target="tpu_custom_call" | custom-call | flops 113246208 | bytes 442368 | tf_op jit(solution)/shard_map/sums/pallas_call | solution.py:266
  13.9 0.6 %collective-permute-start.3 = (bf16[64,768]{1,0:T(8,128)(2,1)S(1)}, bf16[64,768]{1,0:T(8,128)(2,1)S(1)}, u32[]{:S(2)}, u32[]{:S(2)}) collective-permute-start(bf16[64,768]{1,0:T(8,128)(2,1)S(1)} %get-tuple-element.40), channel_id=1, source_target_pairs={{0,2},{1,5},{2,0},{3,7},{4,6},{5,1},{6,4},{7,3},{8,10},{9,13},{10,... | collective-permute-start | bytes 294920 | tf_op jit(solution)/shard_map/ppermute | solution.py:280
  14.5 1.4 %collective-permute-done.6 = bf16[64,1280]{1,0:T(8,128)(2,1)S(1)} collective-permute-done((bf16[64,1280]{1,0:T(8,128)(2,1)S(1)}, bf16[64,1280]{1,0:T(8,128)(2,1)S(1)}, u32[]{:S(2)}, u32[]{:S(2)}) %collective-permute-start.6) | collective-permute-done | bytes 163872 | tf_op jit(solution)/shard_map/ppermute | solution.py:280
  15.9 1.6 %collective-permute-start.7 = (bf16[64,1280]{1,0:T(8,128)(2,1)S(1)}, bf16[64,1280]{1,0:T(8,128)(2,1)S(1)}, u32[]{:S(2)}, u32[]{:S(2)}) collective-permute-start(bf16[64,1280]{1,0:T(8,128)(2,1)S(1)} %fusion), channel_id=1, source_target_pairs={{0,4},{1,9},{2,6},{3,11},{4,0},{5,13},{6,2},{7,15},{8,12},{9,1},{1... | collective-permute-start | bytes 491528 | tf_op jit(solution)/shard_map/ppermute | solution.py:280
  17.5 1.1 %collective-permute-done.3 = bf16[64,768]{1,0:T(8,128)(2,1)S(1)} collective-permute-done((bf16[64,768]{1,0:T(8,128)(2,1)S(1)}, bf16[64,768]{1,0:T(8,128)(2,1)S(1)}, u32[]{:S(2)}, u32[]{:S(2)}) %collective-permute-start.3) | collective-permute-done | bytes 98336 | tf_op jit(solution)/shard_map/ppermute | solution.py:280
  18.6 1.6 %collective-permute-start.4 = (bf16[64,768]{1,0:T(8,128)(2,1)S(1)}, bf16[64,768]{1,0:T(8,128)(2,1)S(1)}, u32[]{:S(2)}, u32[]{:S(2)}) collective-permute-start(bf16[64,768]{1,0:T(8,128)(2,1)S(1)} %fusion.1), channel_id=1, source_target_pairs={{0,4},{1,9},{2,6},{3,11},{4,0},{5,13},{6,2},{7,15},{8,12},{9,1},{1... | collective-permute-start | bytes 294920 | tf_op jit(solution)/shard_map/ppermute | solution.py:280
  20.1 1.1 %collective-permute-done.7 = bf16[64,1280]{1,0:T(8,128)(2,1)S(1)} collective-permute-done((bf16[64,1280]{1,0:T(8,128)(2,1)S(1)}, bf16[64,1280]{1,0:T(8,128)(2,1)S(1)}, u32[]{:S(2)}, u32[]{:S(2)}) %collective-permute-start.7) | collective-permute-done | bytes 163872 | tf_op jit(solution)/shard_map/ppermute | solution.py:280
  21.3 1.6 %collective-permute-start.8 = (bf16[64,1280]{1,0:T(8,128)(2,1)S(1)}, bf16[64,1280]{1,0:T(8,128)(2,1)S(1)}, u32[]{:S(2)}, u32[]{:S(2)}) collective-permute-start(bf16[64,1280]{1,0:T(8,128)(2,1)S(1)} %get-tuple-element.53), channel_id=1, source_target_pairs={{0,8},{1,3},{2,10},{3,1},{4,12},{5,7},{6,14},{7,5},{8,0},{9,11},{1... | collective-permute-start | bytes 491528 | tf_op jit(solution)/shard_map/ppermute | solution.py:280
  23.3 1.6 %collective-permute-start.5 = (bf16[64,768]{1,0:T(8,128)(2,1)S(1)}, bf16[64,768]{1,0:T(8,128)(2,1)S(1)}, u32[]{:S(2)}, u32[]{:S(2)}) collective-permute-start(bf16[64,768]{1,0:T(8,128)(2,1)S(1)} %get-tuple-element.55), channel_id=1, source_target_pairs={{0,8},{1,3},{2,10},{3,1},{4,12},{5,7},{6,14},{7,5},{8,0},{9,11},{1... | collective-permute-start | bytes 294920 | tf_op jit(solution)/shard_map/ppermute | solution.py:280
  24.9 1.8 %collective-permute-done.8.recv_ref = bf16[64,1280]{1,0:T(8,128)(2,1)S(1)} collective-permute-done((bf16[64,1280]{1,0:T(8,128)(2,1)S(1)}, bf16[64,1280]{1,0:T(8,128)(2,1)S(1)}, u32[]{:S(2)}, u32[]{:S(2)}) %collective-permute-start.8) | collective-permute-done | bytes 163872 | tf_op jit(solution)/shard_map/ppermute | solution.py:280
  26.7 1.0 %back.3.refs_2_ = f32[48,1024]{1,0:T(8,128)S(1)} custom-call(f32[64,1280]{1,0:T(8,128)S(1)} %get-tuple-element.54.acc_ref, bf16[64,1280]{1,0:T(8,128)(2,1)S(1)} %collective-permute-done.8.recv_ref, f32[8,2048]{1,0:T(8,128)S(1)} %get-tuple-element.32.frame_ref, bf16[2,2048,256]{2,1,0:T(8,128)(2,1)S(1)} %get-tuple-element.41.refs_0_, ...), custom_call_target="tpu_custom_call" | custom-call | flops 251658240 | bytes 983040 | tf_op jit(solution)/shard_map/back/pallas_call | solution.py:296
  28.3 0.5 %back.4 = (f32[48,256]{1,0:T(8,128)S(1)}, f32[48,256]{1,0:T(8,128)S(1)}, bf16[48,256]{1,0:T(8,128)(2,1)S(1)}) custom-call(f32[64,768]{1,0:T(8,128)S(1)} %get-tuple-element.56.acc_ref, bf16[64,768]{1,0:T(8,128)(2,1)S(1)} %collective-permute-done.5.recv_ref, f32[8,2048]{1,0:T(8,128)S(1)} %get-tuple-element.32.frame_ref, ...), custom_call_target="tpu_custom_call" | custom-call | flops 113246208 | bytes 442368 | tf_op jit(solution)/shard_map/back/pallas_call | solution.py:305
  28.8 0.6 %collective-permute-start.9 = (bf16[48,256]{1,0:T(8,128)(2,1)S(1)}, bf16[48,256]{1,0:T(8,128)(2,1)S(1)}, u32[]{:S(2)}, u32[]{:S(2)}) collective-permute-start(bf16[48,256]{1,0:T(8,128)(2,1)S(1)} %get-tuple-element.51), channel_id=1, source_target_pairs={{0,1},{1,0},{2,3},{3,2},{4,5},{5,4},{6,7},{7,6},{8,9},{9,8},{10,11... | collective-permute-start | bytes 73736 | tf_op jit(solution)/shard_map/ppermute | solution.py:226
  29.5 2.0 %collective-permute-start.11 = (bf16[48,256]{1,0:T(8,128)(2,1)S(1)}, bf16[48,256]{1,0:T(8,128)(2,1)S(1)}, u32[]{:S(2)}, u32[]{:S(2)}) collective-permute-start(bf16[48,256]{1,0:T(8,128)(2,1)S(1)} %add_convert_fusion), channel_id=1, source_target_pairs={{0,16},{1,17},{2,18},{3,19},{4,20},{5,21},{6,22},{7,23},{8,24},{9,... | collective-permute-start | bytes 73736 | tf_op jit(solution)/shard_map/ppermute | solution.py:226
  31.5 3.0 %collective-permute-done.11 = bf16[48,256]{1,0:T(8,128)(2,1)S(1)} collective-permute-done((bf16[48,256]{1,0:T(8,128)(2,1)S(1)}, bf16[48,256]{1,0:T(8,128)(2,1)S(1)}, u32[]{:S(2)}, u32[]{:S(2)}) %collective-permute-start.11) | collective-permute-done | bytes 24608 | tf_op jit(solution)/shard_map/ppermute | solution.py:226
  34.5 0.6 %convert_add_fusion.4 = f32[48,256]{1,0:T(8,128)} fusion(bf16[48,256]{1,0:T(8,128)(2,1)S(1)} %collective-permute-done.11, f32[48,256]{1,0:T(8,128)S(1)} %get-tuple-element.50, bf16[48,256]{1,0:T(8,128)(2,1)S(1)} %collective-permute-done.9), kind=kLoop, calls=%fused_computation.6 | loop fusion | flops 49152 | bytes 147456 | tf_op jit(solution)/shard_map/add | solution.py:318
  (16 shorter events, 1.3 us)
Async XLA Ops:
  1.1 5.6 %collective-permute-start.1 = (bf16[64,256]{1,0:T(8,128)(2,1)S(1)}, bf16[64,256]{1,0:T(8,128)(2,1)S(1)}, u32[]{:S(2)}, u32[]{:S(2)}) collective-permute-start(bf16[64,256]{1,0:T(8,128)(2,1)S(1)} %get-tuple-element.34.pack_ref), channel_id=1, source_target_pairs={{0,1},{1,0},{2,3},{3,2},{4,5},{5,4},{6,7},{7,6},{8,9},{9,8},{10,11... | collective-permute-start | bytes 98312 | tf_op jit(solution)/shard_map/ppermute | solution.py:226
  1.7 6.2 %collective-permute-start = (bf16[64,256]{1,0:T(8,128)(2,1)S(1)}, bf16[64,256]{1,0:T(8,128)(2,1)S(1)}, u32[]{:S(2)}, u32[]{:S(2)}) collective-permute-start(bf16[64,256]{1,0:T(8,128)(2,1)S(1)} %get-tuple-element.34.pack_ref), channel_id=1, source_target_pairs={{0,16},{1,17},{2,18},{3,19},{4,20},{5,21},{6,22},{7,23},{8,24},{9,... | collective-permute-start | bytes 98312 | tf_op jit(solution)/shard_map/ppermute | solution.py:226
  7.9 1.4 %collective-permute-start.2 = (bf16[64,256]{1,0:T(8,128)(2,1)S(1)}, bf16[64,256]{1,0:T(8,128)(2,1)S(1)}, u32[]{:S(2)}, u32[]{:S(2)}) collective-permute-start(bf16[64,256]{1,0:T(8,128)(2,1)S(1)} %collective-permute-done.refs_0_.pack_ref), channel_id=1, source_target_pairs={{0,1},{1,0},{2,3},{3,2},{4,5},{5,4},{6,7},{7,6},{8,9},{9,8},{10,11... | collective-permute-start | bytes 98312 | tf_op jit(solution)/shard_map/ppermute | solution.py:226
  10.5 5.4 %collective-permute-start.6 = (bf16[64,1280]{1,0:T(8,128)(2,1)S(1)}, bf16[64,1280]{1,0:T(8,128)(2,1)S(1)}, u32[]{:S(2)}, u32[]{:S(2)}) collective-permute-start(bf16[64,1280]{1,0:T(8,128)(2,1)S(1)} %get-tuple-element.46), channel_id=1, source_target_pairs={{0,2},{1,5},{2,0},{3,7},{4,6},{5,1},{6,4},{7,3},{8,10},{9,13},{10,... | collective-permute-start | bytes 491528 | tf_op jit(solution)/shard_map/ppermute | solution.py:280
  13.9 4.7 %collective-permute-start.3 = (bf16[64,768]{1,0:T(8,128)(2,1)S(1)}, bf16[64,768]{1,0:T(8,128)(2,1)S(1)}, u32[]{:S(2)}, u32[]{:S(2)}) collective-permute-start(bf16[64,768]{1,0:T(8,128)(2,1)S(1)} %get-tuple-element.40), channel_id=1, source_target_pairs={{0,2},{1,5},{2,0},{3,7},{4,6},{5,1},{6,4},{7,3},{8,10},{9,13},{10,... | collective-permute-start | bytes 294920 | tf_op jit(solution)/shard_map/ppermute | solution.py:280
  15.9 5.4 %collective-permute-start.7 = (bf16[64,1280]{1,0:T(8,128)(2,1)S(1)}, bf16[64,1280]{1,0:T(8,128)(2,1)S(1)}, u32[]{:S(2)}, u32[]{:S(2)}) collective-permute-start(bf16[64,1280]{1,0:T(8,128)(2,1)S(1)} %fusion), channel_id=1, source_target_pairs={{0,4},{1,9},{2,6},{3,11},{4,0},{5,13},{6,2},{7,15},{8,12},{9,1},{1... | collective-permute-start | bytes 491528 | tf_op jit(solution)/shard_map/ppermute | solution.py:280
  18.6 4.7 %collective-permute-start.4 = (bf16[64,768]{1,0:T(8,128)(2,1)S(1)}, bf16[64,768]{1,0:T(8,128)(2,1)S(1)}, u32[]{:S(2)}, u32[]{:S(2)}) collective-permute-start(bf16[64,768]{1,0:T(8,128)(2,1)S(1)} %fusion.1), channel_id=1, source_target_pairs={{0,4},{1,9},{2,6},{3,11},{4,0},{5,13},{6,2},{7,15},{8,12},{9,1},{1... | collective-permute-start | bytes 294920 | tf_op jit(solution)/shard_map/ppermute | solution.py:280
  21.3 5.4 %collective-permute-start.8 = (bf16[64,1280]{1,0:T(8,128)(2,1)S(1)}, bf16[64,1280]{1,0:T(8,128)(2,1)S(1)}, u32[]{:S(2)}, u32[]{:S(2)}) collective-permute-start(bf16[64,1280]{1,0:T(8,128)(2,1)S(1)} %get-tuple-element.53), channel_id=1, source_target_pairs={{0,8},{1,3},{2,10},{3,1},{4,12},{5,7},{6,14},{7,5},{8,0},{9,11},{1... | collective-permute-start | bytes 491528 | tf_op jit(solution)/shard_map/ppermute | solution.py:280
  23.3 4.7 %collective-permute-start.5 = (bf16[64,768]{1,0:T(8,128)(2,1)S(1)}, bf16[64,768]{1,0:T(8,128)(2,1)S(1)}, u32[]{:S(2)}, u32[]{:S(2)}) collective-permute-start(bf16[64,768]{1,0:T(8,128)(2,1)S(1)} %get-tuple-element.55), channel_id=1, source_target_pairs={{0,8},{1,3},{2,10},{3,1},{4,12},{5,7},{6,14},{7,5},{8,0},{9,11},{1... | collective-permute-start | bytes 294920 | tf_op jit(solution)/shard_map/ppermute | solution.py:280
  28.2 1.3 %collective-permute-start.10 = (bf16[48,256]{1,0:T(8,128)(2,1)S(1)}, bf16[48,256]{1,0:T(8,128)(2,1)S(1)}, u32[]{:S(2)}, u32[]{:S(2)}) collective-permute-start(bf16[48,256]{1,0:T(8,128)(2,1)S(1)} %back.5), channel_id=1, source_target_pairs={{0,1},{1,0},{2,3},{3,2},{4,5},{5,4},{6,7},{7,6},{8,9},{9,8},{10,11... | collective-permute-start | bytes 73736 | tf_op jit(solution)/shard_map/ppermute | solution.py:226
  28.8 2.7 %collective-permute-start.9 = (bf16[48,256]{1,0:T(8,128)(2,1)S(1)}, bf16[48,256]{1,0:T(8,128)(2,1)S(1)}, u32[]{:S(2)}, u32[]{:S(2)}) collective-permute-start(bf16[48,256]{1,0:T(8,128)(2,1)S(1)} %get-tuple-element.51), channel_id=1, source_target_pairs={{0,1},{1,0},{2,3},{3,2},{4,5},{5,4},{6,7},{7,6},{8,9},{9,8},{10,11... | collective-permute-start | bytes 73736 | tf_op jit(solution)/shard_map/ppermute | solution.py:226
  29.5 5.0 %collective-permute-start.11 = (bf16[48,256]{1,0:T(8,128)(2,1)S(1)}, bf16[48,256]{1,0:T(8,128)(2,1)S(1)}, u32[]{:S(2)}, u32[]{:S(2)}) collective-permute-start(bf16[48,256]{1,0:T(8,128)(2,1)S(1)} %add_convert_fusion), channel_id=1, source_target_pairs={{0,16},{1,17},{2,18},{3,19},{4,20},{5,21},{6,22},{7,23},{8,24},{9,... | collective-permute-start | bytes 73736 | tf_op jit(solution)/shard_map/ppermute | solution.py:226
